TPU v7x, 256 devices: a whole 4x4x8 slice. The times are simulated.
256 devices in a mesh: nodes: 128 (over y, z, x), rep: 2 (over core).
Axes of the slice: x: 4, y: 4, z: 8, core: 2. Of those that a mesh axis runs over, the one named last changes fastest.
Arguments:
- node_latent: bfloat16 [40960, 512], P(('nodes', 'rep')), may hold values from -6 to 6
- edge_saved: bfloat16 [327680, 512], P(('nodes', 'rep')), may hold values from -6 to 6
- node_cot: bfloat16 [40960, 512], P(('nodes', 'rep')), may hold values from -6 to 6
- edge_cot: bfloat16 [327680, 512], P(('nodes', 'rep')), may hold values from -6 to 6
- senders: int32 [327680], P(('nodes', 'rep')), may hold values from 0 to 1343, as said below
- receivers: int32 [327680], P(('nodes', 'rep')), may hold values from 0 to 319
- ghost_rows: int32 [128, 128, 8], P('nodes'), may hold values from 0 to 319, as said below
- w_edge_in: bfloat16 [1536, 512], replicated, may hold values from -0.15625 to 0.15625
- w_edge_out: bfloat16 [512, 512], replicated, may hold values from -0.25 to 0.25
- edge_gain: float32 [512], replicated, may hold values from 0.5 to 2
- edge_offset: float32 [512], replicated, may hold values from -3 to 3
- w_node_in: bfloat16 [1024, 512], replicated, may hold values from -0.1875 to 0.1875
- w_node_out: bfloat16 [512, 512], replicated, may hold values from -0.25 to 0.25
- node_gain: float32 [512], replicated, may hold values from 0.5 to 2
Outputs:
- grad_nodes: bfloat16 [40960, 512], P(('nodes', 'rep'))
- grad_edges: bfloat16 [327680, 512], P(('nodes', 'rep'))
- grad_edge_in: bfloat16 [1536, 512], replicated
- grad_edge_out: bfloat16 [512, 512], replicated
- grad_node_in: bfloat16 [1024, 512], replicated
- grad_node_out: bfloat16 [512, 512], replicated
Inputs may be any that keep to these rules, and one draw needn't show every extreme that they name: `senders`: A sender below 320 is a node of the edge's own partition; otherwise it is 320 + q * 8 + s, the ghost slot s of the list of a partition q other than the edge's own. Each list ghost_rows[q, p] holds 8 distinct rows.
All inputs are finite; a program needn't handle non-finite values.
Results may differ from a plain program's by a relative error of at most 0.008.
Values may be sent and summed in bfloat16 or wider, within the bound.
No kernel may reach another device: no remote copies, remote signals or barrier semaphores. Data moves between devices by JAX's collectives and lax.ppermute only.
A program may use at most 128 MiB of HBM per device.

v0:
```python
import math

import jax
import jax.numpy as jnp
from jax import lax
from jax.sharding import PartitionSpec as P

EPS = 1e-05


def swapped(array, axis, bit):
    return lax.ppermute(array, axis, [(i, i ^ 1 << bit) for i in range(lax.axis_size(axis))])


def sent_to_all(array, axis):
    devices = lax.axis_size(axis)
    return lax.all_to_all(
        jnp.broadcast_to(array[None], (devices, *array.shape)), axis, 0, 0, tiled=True
    )


def in_order(blocks, dim):
    blocks = jnp.moveaxis(blocks, 0, dim)
    dims = blocks.shape
    return blocks.reshape(*dims[:dim], dims[dim] * dims[dim + 1], *dims[dim + 2 :])


def gather_directly(array, axis, dim):
    blocks = sent_to_all(array, axis)
    return in_order(blocks, dim)


def split_up(array, dim, devices):
    before, after = (array.shape[:dim], array.shape[dim + 1 :])
    return jnp.moveaxis(array.reshape(*before, devices, -1, *after), dim, 0)


def summed_on_arrival(array, axis, dim):
    devices = lax.axis_size(axis)
    blocks = lax.all_to_all(split_up(array, dim, devices), axis, 0, 0, tiled=True)
    return jnp.sum(blocks, axis=0)


def summed_on_arrival_2(array, axis, dim):
    devices = lax.axis_size(axis)
    blocks = lax.all_to_all(split_up(array, dim, devices), axis, 0, 0, tiled=True)
    return jnp.sum(blocks.astype(jnp.float32), axis=0)


def mat_mul(left, right):
    return jnp.dot(left, right, preferred_element_type=jnp.float32)


def mat_tn(left, right):
    return lax.dot_general(
        left, right, (((0,), (0,)), ((), ())), preferred_element_type=jnp.float32
    )


def mat_nt(left, right):
    return lax.dot_general(
        left, right, (((1,), (1,)), ((), ())), preferred_element_type=jnp.float32
    )


def silu_slope(value):
    sigmoid_v = jax.nn.sigmoid(value)
    return sigmoid_v * (1.0 + value * (1.0 - sigmoid_v))


def norm_forward(value):
    centred = value - jnp.mean(value, axis=-1, keepdims=True)
    inverse = lax.rsqrt(jnp.mean(centred * centred, axis=-1, keepdims=True) + EPS)
    return (centred * inverse, inverse)


def norm_backward(grad_hat, normed, inverse):
    return inverse * (
        grad_hat
        - jnp.mean(grad_hat, axis=-1, keepdims=True)
        - normed * jnp.mean(grad_hat * normed, axis=-1, keepdims=True)
    )


def edge_forward(edge_block, send_rows, recv_rows, w_edge_in, w_edge_out, edge_gain, edge_offset):
    latent_width = edge_block.shape[1]
    pre_act = (
        mat_mul(edge_block, w_edge_in[:latent_width])
        + mat_mul(send_rows, w_edge_in[latent_width : 2 * latent_width])
        + mat_mul(recv_rows, w_edge_in[2 * latent_width :])
    )
    edge_hidden = jax.nn.silu(pre_act).astype(jnp.bfloat16)
    edge_normed, edge_inverse = norm_forward(mat_mul(edge_hidden, w_edge_out))
    message = edge_normed * edge_gain + edge_offset
    return (pre_act, edge_hidden, edge_normed, edge_inverse, message)


def edge_backward(
    edge_block,
    send_rows,
    recv_rows,
    edge_cot,
    message_grad,
    saved,
    w_edge_in,
    w_edge_out,
    edge_gain,
):
    pre_act, edge_hidden, edge_normed, edge_inverse = saved
    latent_width = edge_block.shape[1]
    grad_out = norm_backward(message_grad * edge_gain, edge_normed, edge_inverse).astype(
        jnp.bfloat16
    )
    grad_act = (mat_nt(grad_out, w_edge_out) * silu_slope(pre_act)).astype(jnp.bfloat16)
    in_grad = jnp.concatenate(
        [mat_tn(edge_block, grad_act), mat_tn(send_rows, grad_act), mat_tn(recv_rows, grad_act)], 0
    )
    out_grad = mat_tn(edge_hidden, grad_out)
    edge_grad = (edge_cot.astype(jnp.float32) + mat_nt(grad_act, w_edge_in[:latent_width])).astype(
        jnp.bfloat16
    )
    send_grad = mat_nt(grad_act, w_edge_in[latent_width : 2 * latent_width])
    recv_grad = mat_nt(grad_act, w_edge_in[2 * latent_width :])
    return (edge_grad, send_grad, recv_grad, in_grad, out_grad)


def node_pass(node_rows, totals_b, node_cot, w_node_in, w_node_out, node_gain):
    latent_width = node_rows.shape[1]
    node_pre = mat_mul(node_rows, w_node_in[:latent_width]) + mat_mul(
        totals_b, w_node_in[latent_width:]
    )
    node_hidden = jax.nn.silu(node_pre).astype(jnp.bfloat16)
    node_normed, node_inverse = norm_forward(mat_mul(node_hidden, w_node_out))
    grad_out = norm_backward(
        node_cot.astype(jnp.float32) * node_gain, node_normed, node_inverse
    ).astype(jnp.bfloat16)
    grad_act = (mat_nt(grad_out, w_node_out) * silu_slope(node_pre)).astype(jnp.bfloat16)
    in_grad = jnp.concatenate([mat_tn(node_rows, grad_act), mat_tn(totals_b, grad_act)], 0)
    direct_grad = mat_nt(grad_act, w_node_in[:latent_width])
    totals_grad = mat_nt(grad_act, w_node_in[latent_width:]).astype(jnp.bfloat16)
    return (direct_grad, totals_grad, in_grad, mat_tn(node_hidden, grad_out))


def shards(
    node_latent,
    edge_saved,
    node_cot,
    edge_cot,
    senders,
    receivers,
    ghost_rows,
    w_edge_in,
    w_edge_out,
    edge_gain,
    edge_offset,
    w_node_in,
    w_node_out,
    node_gain,
):
    latent_width = node_latent.shape[1]
    edge_latent = swapped(edge_saved, "rep", 0)
    partition = gather_directly(node_latent, "rep", 0)
    part_rows = partition.shape[0]
    ghost_lists = ghost_rows[0]
    part_count = ghost_lists.shape[0]
    slot_count = ghost_lists.shape[1]
    half_slots = slot_count // lax.axis_size("rep")
    own_lists = lax.dynamic_slice_in_dim(
        ghost_lists, lax.axis_index("rep") * half_slots, half_slots, 1
    )
    outgoing = partition[own_lists.reshape(-1)].reshape(part_count, half_slots, latent_width)
    arrived = lax.all_to_all(outgoing, "nodes", split_axis=0, concat_axis=0, tiled=True)
    ghosts = gather_directly(arrived, "rep", 1)
    node_table = jnp.concatenate(
        [partition, ghosts.reshape(part_count * slot_count, latent_width)], 0
    )
    send_rows = node_table[senders]
    recv_rows = partition[receivers]
    pre_act, edge_hidden, edge_normed, edge_inverse, message = edge_forward(
        edge_latent, send_rows, recv_rows, w_edge_in, w_edge_out, edge_gain, edge_offset
    )
    partial_totals = jax.ops.segment_sum(message, receivers, num_segments=part_rows)
    totals = summed_on_arrival(partial_totals, "rep", 0)
    direct_grad, totals_grad, node_in_grad, node_out_grad = node_pass(
        node_latent, totals.astype(jnp.bfloat16), node_cot, w_node_in, w_node_out, node_gain
    )
    partition_totals_grad = gather_directly(totals_grad, "rep", 0)
    message_grad = edge_cot.astype(jnp.float32) + partition_totals_grad[receivers].astype(
        jnp.float32
    )
    edge_grad, send_grad, recv_grad, edge_in_grad, edge_out_grad = edge_backward(
        edge_latent,
        send_rows,
        recv_rows,
        edge_cot,
        message_grad,
        (pre_act, edge_hidden, edge_normed, edge_inverse),
        w_edge_in,
        w_edge_out,
        edge_gain,
    )
    table_grad = jax.ops.segment_sum(send_grad, senders, num_segments=node_table.shape[0])
    row_grad = table_grad[:part_rows] + jax.ops.segment_sum(
        recv_grad, receivers, num_segments=part_rows
    )
    ghost_grad = table_grad[part_rows:].reshape(part_count, slot_count, latent_width)
    paired = summed_on_arrival_2(ghost_grad.astype(jnp.bfloat16), "rep", 1)
    returned = lax.all_to_all(
        paired.astype(jnp.bfloat16), "nodes", split_axis=0, concat_axis=0, tiled=True
    ).astype(paired.dtype)
    row_grad = row_grad + jax.ops.segment_sum(
        returned.reshape(-1, latent_width), own_lists.reshape(-1), num_segments=part_rows
    )
    own_grad = summed_on_arrival(row_grad, "rep", 0)
    grad_nodes = (own_grad + direct_grad + node_cot.astype(jnp.float32)).astype(jnp.bfloat16)
    weight_grads = (edge_in_grad, edge_out_grad, node_in_grad, node_out_grad)
    device_count = lax.axis_size("nodes") * lax.axis_size("rep")
    edge_scale = 1.0 / math.sqrt(senders.shape[0] * device_count)
    node_scale = 1.0 / math.sqrt(node_latent.shape[0] * device_count)
    weight_total = lax.psum(
        (weight_grads[0], weight_grads[1], weight_grads[2], weight_grads[3]), ("nodes", "rep")
    )
    return (
        grad_nodes,
        edge_grad,
        (weight_total[0] * edge_scale).astype(jnp.bfloat16),
        (weight_total[1] * edge_scale).astype(jnp.bfloat16),
        (weight_total[2] * node_scale).astype(jnp.bfloat16),
        (weight_total[3] * node_scale).astype(jnp.bfloat16),
    )


def solution(mesh):
    return jax.shard_map(
        shards,
        mesh=mesh,
        in_specs=(
            P(("nodes", "rep"), None),
            P(("nodes", "rep"), None),
            P(("nodes", "rep"), None),
            P(("nodes", "rep"), None),
            P(("nodes", "rep")),
            P(("nodes", "rep")),
            P("nodes", None, None),
            P(),
            P(),
            P(),
            P(),
            P(),
            P(),
            P(),
        ),
        out_specs=(P(("nodes", "rep"), None), P(("nodes", "rep"), None), P(), P(), P(), P()),
        check_vma=False,
    )
```

profile of v0, /device:TPU:1, one launch (start us, length us, event | category | flops | bytes accessed | tf_op | source)
XLA Modules:
  0.0 422.8 jit_solution(2287839622179952610)
XLA Ops:
  8.9 6.7 %all-to-all-start = ((bf16[2,160,512]{2,1,0:T(8,128)(2,1)}), bf16[2,160,512]{2,1,0:T(8,128)(2,1)S(1)}, u32[]{:S(2)}, u32[]{:S(2)}) async-start(bf16[2,160,512]{2,1,0:T(8,128)(2,1)} %broadcast_in_dim.18), calls=%async_computation | async-start | bytes 655360 | tf_op jit(solution)/shard_map/all_to_all | solution.py:17
  19.9 14.3 %all-to-all-start.1 = ((bf16[128,4,512]{2,1,0:T(4,128)(2,1)}), bf16[128,4,512]{2,1,0:T(4,128)(2,1)}, u32[]{:S(2)}, u32[]{:S(2)}) async-start(bf16[128,4,512]{2,1,0:T(4,128)(2,1)} %reshape.119), calls=%async_computation.1 | async-start | bytes 1048576 | tf_op jit(solution)/shard_map/all_to_all | solution.py:172
  34.8 4.1 gather_fusion.2
  39.0 2.9 copy.33
  43.5 3.4 fusion.17
  46.9 4.5 %all-to-all-done.1 = bf16[128,4,512]{2,1,0:T(4,128)(2,1)} async-done(((bf16[128,4,512]{2,1,0:T(4,128)(2,1)}), bf16[128,4,512]{2,1,0:T(4,128)(2,1)}, u32[]{:S(2)}, u32[]{:S(2)}) %all-to-all-start.1) | async-done | bytes 524320 | tf_op jit(solution)/shard_map/all_to_all | solution.py:172
  52.7 6.9 %all_to_all.40 = bf16[2,128,4,512]{3,2,1,0:T(4,128)(2,1)S(1)} all-to-all(bf16[2,128,4,512]{3,2,1,0:T(4,128)(2,1)S(1)} %broadcast_in_dim.19), channel_id=1, replica_groups=mesh['nodes'=128,'rep'=2] {'rep'}, dimensions={0} | all-to-all | bytes 2097152 | tf_op jit(solution)/shard_map/all_to_all | solution.py:17
  60.3 4.2 %gather_fusion.1 = bf16[1280,512]{1,0:T(8,128)(2,1)S(1)} fusion(bf16[1344,512]{1,0:T(8,128)(2,1)S(1)} %pad_maximum_fusion.2, s32[2048]{0:T(1024)} %pad_clamp_fusion.1), kind=kCustom, calls=%fused_computation.1 | custom fusion | bytes 2626560 | tf_op jit(solution)/shard_map/gather | solution.py:177
  67.0 4.2 %multiply_convert_fusion.2 = (bf16[1280,512]{1,0:T(8,128)(2,1)S(1)}, f32[1280,512]{1,0:T(8,128)}) fusion(f32[1280,512]{1,0:T(8,128)S(1)} %copy-done.10, f32[1280,512]{1,0:T(8,128)S(1)} %fusion.21, bf16[1280,512]{1,0:T(8,128)(2,1)} %collective-permute-done, bf16[1536,512]{1,0:T(8,128)(2,1)} %param.21), kind=kOutput, calls=%fused_computation.22 | convolution fusion | flops 675676160 | bytes 11010048 | tf_op jit(solution)/shard_map/dot_general | solution.py:51
  74.5 3.2 copy.34
  77.7 11.1 %scatter_custom_fusion = f32[320,512]{1,0:T(8,128)} fusion(s32[1280]{0:T(1024)S(1)} %copy-done.35, f32[1280,512]{1,0:T(8,128)} %copy.34, f32[]{:T(128)} %constant.13.clone.1), kind=kCustom, calls=%fused_computation.72 | custom fusion | flops 655360 | bytes 655872 | tf_op jit(solution)/shard_map/scatter-add | solution.py:182
  88.8 6.4 %all_to_all.41 = f32[2,160,512]{2,1,0:T(8,128)} all-to-all(f32[2,160,512]{2,1,0:T(8,128)} %bitcast.47), channel_id=1, replica_groups=mesh['nodes'=128,'rep'=2] {'rep'}, dimensions={0} | all-to-all | bytes 1310720 | tf_op jit(solution)/shard_map/all_to_all | solution.py:40
  101.0 4.2 all_to_all.42
  105.1 4.7 %gather_fusion.3 = bf16[1280,512]{1,0:T(8,128)(2,1)} fusion(bf16[320,512]{1,0:T(8,128)(2,1)S(1)} %bitcast.44, s32[2048]{0:T(1024)S(1)} %pad_clamp_fusion), kind=kCustom, calls=%fused_computation.3 | custom fusion | bytes 2626560 | tf_op jit(solution)/shard_map/gather | solution.py:188
  131.6 3.5 fusion.19
  135.0 11.1 %scatter_custom_fusion.1 = f32[1344,512]{1,0:T(8,128)S(1)} fusion(s32[1280]{0:T(1024)} %param.18, f32[1280,512]{1,0:T(8,128)} %fusion.19, f32[]{:T(128)} %constant.13.clone.1), kind=kCustom, calls=%fused_computation.30 | custom fusion | flops 655360 | bytes 2753024 | tf_op jit(solution)/shard_map/scatter-add | solution.py:202
  151.2 5.5 %all_to_all.43 = bf16[2,128,4,512]{3,2,1,0:T(4,128)(2,1)} all-to-all(bf16[2,128,4,512]{3,2,1,0:T(4,128)(2,1)S(1)} %bitcast.46), channel_id=1, replica_groups=mesh['nodes'=128,'rep'=2] {'rep'}, dimensions={0} | all-to-all | bytes 2097152 | tf_op jit(solution)/shard_map/all_to_all | solution.py:46
  156.8 2.9 reduce_sum.111
  159.7 7.8 %all-to-all-start.6 = ((bf16[128,4,512]{2,1,0:T(4,128)(2,1)}), bf16[128,4,512]{2,1,0:T(4,128)(2,1)}, u32[]{:S(2)}, u32[]{:S(2)}) async-start(bf16[128,4,512]{2,1,0:T(4,128)(2,1)} %reduce_sum.111), calls=%async_computation.6 | async-start | bytes 1048576 | tf_op jit(solution)/shard_map/all_to_all | solution.py:208
  174.3 9.9 %scatter_fusion = f32[320,512]{1,0:T(8,128)S(1)} fusion(f32[320,512]{1,0:T(8,128)S(1)} %slice-done, s32[1280]{0:T(1024)S(1)} %copy-done.35, f32[1280,512]{1,0:T(8,128)S(1)} %fusion.15), kind=kCustom, calls=%fused_computation.6 | custom fusion | flops 655360 | bytes 7869440 | tf_op jit(solution)/shard_map/scatter-add | solution.py:203
  188.7 4.8 %scatter_custom_fusion.3 = f32[320,512]{1,0:T(8,128)S(1)} fusion(s32[512]{0:T(512)S(1)} %reshape.185, f32[512,512]{1,0:T(8,128)} %reshape.187, f32[]{:T(128)} %constant.13.clone.1), kind=kCustom, calls=%fused_computation.70 | custom fusion | flops 262144 | bytes 655872 | tf_op jit(solution)/shard_map/scatter-add | solution.py:211
  193.6 6.8 %all_to_all.44 = f32[2,160,512]{2,1,0:T(8,128)S(1)} all-to-all(f32[2,160,512]{2,1,0:T(8,128)S(1)} %bitcast.48), channel_id=1, replica_groups=mesh['nodes'=128,'rep'=2] {'rep'}, dimensions={0} | all-to-all | bytes 1310720 | tf_op jit(solution)/shard_map/all_to_all | solution.py:40
  201.5 207.5 %all-reduce.3.cloned.1.call-done = (f32[1536,512]{1,0:T(8,128)}, f32[512,512]{1,0:T(8,128)}, f32[1024,512]{1,0:T(8,128)}, f32[512,512]{1,0:T(8,128)}) async-done(((f32[1536,512]{1,0:T(8,128)}, f32[512,512]{1,0:T(8,128)}, f32[1024,512]{1,0:T(8,128)}, f32[512,512]{1,0:T(8,128)}), (f32[1536,512]{1,0:T(8,128)}, f32[512,512]{1,0:T(8,128)}, f32[1024,512]{1,0:T(8,128)}, ...) | async-done | bytes 7340048 | tf_op jit(solution)/shard_map/psum | solution.py:220
  408.9 3.6 multiply_convert_fusion
  (163 shorter events, 63.8 us)
Async XLA Ops:
  7.2 64.1 %copy-start = (bf16[512,512]{1,0:T(8,128)(2,1)S(1)}, bf16[512,512]{1,0:T(8,128)(2,1)}, u32[]{:S(2)}) copy-start(bf16[512,512]{1,0:T(8,128)(2,1)} %param.22) | copy-start | bytes 1572868
  8.9 7.9 %all-to-all-start = ((bf16[2,160,512]{2,1,0:T(8,128)(2,1)}), bf16[2,160,512]{2,1,0:T(8,128)(2,1)S(1)}, u32[]{:S(2)}, u32[]{:S(2)}) async-start(bf16[2,160,512]{2,1,0:T(8,128)(2,1)} %broadcast_in_dim.18), calls=%async_computation | async-start | bytes 655360 | tf_op jit(solution)/shard_map/all_to_all | solution.py:17
  17.0 17.8 %copy-start.35 = (s32[1280]{0:T(1024)S(1)}, s32[1280]{0:T(1024)}, u32[]{:S(2)}) copy-start(s32[1280]{0:T(1024)} %param.19) | copy-start | bytes 15364
  19.9 31.5 %all-to-all-start.1 = ((bf16[128,4,512]{2,1,0:T(4,128)(2,1)}), bf16[128,4,512]{2,1,0:T(4,128)(2,1)}, u32[]{:S(2)}, u32[]{:S(2)}) async-start(bf16[128,4,512]{2,1,0:T(4,128)(2,1)} %reshape.119), calls=%async_computation.1 | async-start | bytes 1048576 | tf_op jit(solution)/shard_map/all_to_all | solution.py:172
  34.2 374.7 %all-reduce.3.cloned.1.call-start = ((), (), s32[]{:S(2)}) async-start(), calls=%async_computation.8 | async-start | bytes 14680064 | tf_op jit(solution)/shard_map/psum | solution.py:220
  34.3 32.7 %collective-permute-start = (bf16[1280,512]{1,0:T(8,128)(2,1)}, bf16[1280,512]{1,0:T(8,128)(2,1)}, u32[]{:S(2)}, u32[]{:S(2)}) collective-permute-start(bf16[1280,512]{1,0:T(8,128)(2,1)} %param.15), channel_id=1, source_target_pairs={{0,1},{1,0},{2,3},{3,2},{4,5},{5,4},{6,7},{7,6},{8,9},{9,8},{10,11... | collective-permute-start | bytes 3932168 | tf_op jit(solution)/shard_map/ppermute | solution.py:12
  38.9 7.9 %copy-start.5 = (bf16[1280,512]{1,0:T(8,128)(2,1)}, bf16[1280,512]{1,0:T(8,128)(2,1)S(1)}, u32[]{:S(2)}) copy-start(bf16[1280,512]{1,0:T(8,128)(2,1)S(1)} %gather_fusion.2) | copy-start | bytes 3932164
  64.6 6.7 %copy-start.7 = (bf16[1280,512]{1,0:T(8,128)(2,1)}, bf16[1280,512]{1,0:T(8,128)(2,1)S(1)}, u32[]{:S(2)}) copy-start(bf16[1280,512]{1,0:T(8,128)(2,1)S(1)} %gather_fusion.1) | copy-start | bytes 3932164
  88.8 10.9 %copy-start.27 = (bf16[160,512]{1,0:T(8,128)(2,1)S(1)}, bf16[160,512]{1,0:T(8,128)(2,1)}, u32[]{:S(2)}) copy-start(bf16[160,512]{1,0:T(8,128)(2,1)} %param.16) | copy-start | bytes 491524
  88.8 10.9 %copy-start.39 = (f32[512]{0:T(512)S(1)}, f32[512]{0:T(512)}, u32[]{:S(2)}) copy-start(f32[512]{0:T(512)} %param.27) | copy-start | bytes 6148
  96.3 4.0 copy-start.17
  96.3 3.6 copy-start.28
  96.3 3.6 copy-start.44
  99.4 5.8 %copy-start.21 = (f32[160,512]{1,0:T(8,128)}, f32[160,512]{1,0:T(8,128)S(1)}, u32[]{:S(2)}) copy-start(f32[160,512]{1,0:T(8,128)S(1)} %get-tuple-element.37) | copy-start | bytes 983044
  99.9 10.0 %copy-start.40 = (f32[160]{0:T(256)}, f32[160]{0:T(256)S(1)}, u32[]{:S(2)}) copy-start(f32[160]{0:T(256)S(1)} %get-tuple-element.38) | copy-start | bytes 1924
  99.9 10.0 %copy-start.42 = (f32[160]{0:T(256)}, f32[160]{0:T(256)S(1)}, u32[]{:S(2)}) copy-start(f32[160]{0:T(256)S(1)} %get-tuple-element.39) | copy-start | bytes 1924
  118.3 13.3 %copy-start.9 = (bf16[1280,512]{1,0:T(8,128)(2,1)}, bf16[1280,512]{1,0:T(8,128)(2,1)S(1)}, u32[]{:S(2)}) copy-start(bf16[1280,512]{1,0:T(8,128)(2,1)S(1)} %fusion.2) | copy-start | bytes 3932164
  146.2 21.4 %copy-start.2 = (f32[1344,512]{1,0:T(8,128)}, f32[1344,512]{1,0:T(8,128)S(1)}, u32[]{:S(2)}) copy-start(f32[1344,512]{1,0:T(8,128)S(1)} %scatter_custom_fusion.1) | copy-start | bytes 8257540
  151.2 16.2 %copy-start.32 = (s32[1,128,4]{2,1,0:T(8,128)S(1)}, s32[1,128,4]{2,1,0:T(8,128)}, u32[]{:S(2)}) copy-start(s32[1,128,4]{2,1,0:T(8,128)} %copy-done.31) | copy-start | bytes 6148
  159.7 27.0 %all-to-all-start.6 = ((bf16[128,4,512]{2,1,0:T(4,128)(2,1)}), bf16[128,4,512]{2,1,0:T(4,128)(2,1)}, u32[]{:S(2)}, u32[]{:S(2)}) async-start(bf16[128,4,512]{2,1,0:T(4,128)(2,1)} %reduce_sum.111), calls=%async_computation.6 | async-start | bytes 1048576 | tf_op jit(solution)/shard_map/all_to_all | solution.py:208
  188.7 11.7 %copy-start.13 = (bf16[1024,512]{1,0:T(8,128)(2,1)S(1)}, bf16[1024,512]{1,0:T(8,128)(2,1)}, u32[]{:S(2)}) copy-start(bf16[1024,512]{1,0:T(8,128)(2,1)} %param.25) | copy-start | bytes 3145732
  188.7 11.7 %copy-start.30 = (bf16[160,512]{1,0:T(8,128)(2,1)S(1)}, bf16[160,512]{1,0:T(8,128)(2,1)}, u32[]{:S(2)}) copy-start(bf16[160,512]{1,0:T(8,128)(2,1)} %param.16) | copy-start | bytes 491524
  408.9 3.6 copy-start.26
  408.9 4.6 %copy-start.14 = (f32[1024,512]{1,0:T(8,128)S(1)}, f32[1024,512]{1,0:T(8,128)}, u32[]{:S(2)}) copy-start(f32[1024,512]{1,0:T(8,128)} %get-tuple-element.30) | copy-start | bytes 6291460
  (28 other events, 53.4 us)
Sparse Core Ops, SparseCore 0:
  131.7 277.2 all-reduce.2
where the time goes:
time: 430 us; the launch traced here: 423 us
  waiting for transfers between devices  215 us (50%)
  other arithmetic  58.3 us (14%)
  local copies, waits for them, and re-layouts  41.1 us (10%)
  matrix products  34.7 us (8%)
  blocking collectives  29.7 us (7%)
  starting transfers between devices  29.3 us (7%)
  between operations  15 us (3%)
    psum x1, waiting for transfers between devices, shards(): lax.psum((weight_grads[0], weight_grads[1], weight_grads[2], weight_grads...  207 us
    dot_general x7, matrix products, mat_mul(): return jnp.dot(left, right, preferred_element_type=jnp.float32)  14.9 us
    all_to_all x1, starting transfers between devices, shards(): lax.all_to_all(outgoing, 'nodes', split_axis=0, concat_axis=0, tiled=True)  14.3 us
    all_to_all x2, blocking collectives, summed_on_arrival(): lax.all_to_all(split_up(array, dim, devices), axis, 0, 0, tiled=True)  13.2 us
    dot_general x7, matrix products, mat_nt(): lax.dot_general(left, right, (((1,), (1,)), ((), ())), preferred_element_...  11.9 us
    scatter-add x1, other arithmetic, shards(): jax.ops.segment_sum(send_grad, senders, num_segments=node_table.shape[0])  11.1 us
    scatter-add x1, other arithmetic, shards(): jax.ops.segment_sum(message, receivers, num_segments=part_rows)  11.1 us
    all_to_all x2, blocking collectives, sent_to_all(): lax.all_to_all(jnp.broadcast_to(array[None], (devices, *array.shape)), ax...  11 us
  transfers between devices with their start and end apart: 5, of which 4 were waited for; matrix products, arithmetic and copies ran while one was open for 16% of the time, Pallas kernels for 0%

commit v1 on v0

v1 whole, which is shorter than its diff:
```python
import math

import jax
import jax.numpy as jnp
from jax import lax
from jax.sharding import PartitionSpec as P

EPS = 1e-05
bf16 = jnp.bfloat16
f32 = jnp.float32


def swapped(array):
    pairs = [(i, 1 - i) for i in range(2)]
    return lax.ppermute(array, "rep", pairs)


def mat_mul(left, right):
    return jnp.dot(left, right, preferred_element_type=f32)


def mat_tn(left, right):
    return lax.dot_general(left, right, (((0,), (0,)), ((), ())), preferred_element_type=f32)


def mat_nt(left, right):
    return lax.dot_general(left, right, (((1,), (1,)), ((), ())), preferred_element_type=f32)


def split_two(value):
    high = lax.reduce_precision(value, 8, 7)
    return high.astype(bf16), (value - high).astype(bf16)


def silu_slope(value):
    sigmoid_v = jax.nn.sigmoid(value)
    return sigmoid_v * (1.0 + value * (1.0 - sigmoid_v))


def norm_forward(value):
    centred = value - jnp.mean(value, axis=-1, keepdims=True)
    inverse = lax.rsqrt(jnp.mean(centred * centred, axis=-1, keepdims=True) + EPS)
    return (centred * inverse, inverse)


def norm_backward(grad_hat, normed, inverse):
    return inverse * (
        grad_hat
        - jnp.mean(grad_hat, axis=-1, keepdims=True)
        - normed * jnp.mean(grad_hat * normed, axis=-1, keepdims=True)
    )


def one_hot(index, width):
    return (index[:, None] == lax.broadcasted_iota(jnp.int32, (1, width), 1)).astype(bf16)


def reduce_groups(sizes):
    ny, nz, nx = sizes

    def device(y, z, x, r):
        return ((y * nz + z) * nx + x) * 2 + r

    near = [[device(y, z, x, 0) for x in range(nx)] for y in range(ny) for z in range(nz)]
    near += [[device(y, z, x, 1) for y in range(ny)] for x in range(nx) for z in range(nz)]
    far = [[device(y, z, x, 0) for y in range(ny) for z in range(nz)] for x in range(nx)]
    far += [[device(y, z, x, 1) for x in range(nx) for z in range(nz)] for y in range(ny)]
    return near, far


def exchange(array, groups):
    return lax.all_to_all(
        array, ("nodes", "rep"), 0, 0, tiled=True, axis_index_groups=groups
    )


def total_over_devices(weight_grads, core):
    near, far = reduce_groups((4, 8, 4))
    rows, width = weight_grads.shape
    half = rows // 2
    kept = lax.dynamic_slice_in_dim(weight_grads, core * half, half, 0)
    sent = lax.dynamic_slice_in_dim(weight_grads, (1 - core) * half, half, 0).astype(bf16)
    pair = (kept + swapped(sent).astype(f32)).astype(bf16)
    n_near, n_far = len(near[0]), len(far[0])
    blocks = exchange(pair.reshape(n_near, half // n_near, width), near)
    part = jnp.sum(blocks.astype(f32), axis=0).astype(bf16)
    rows_far = half // n_near // n_far
    blocks = exchange(part.reshape(n_far, rows_far, width), far)
    part = jnp.sum(blocks.astype(f32), axis=0).astype(bf16)
    part = exchange(jnp.broadcast_to(part[None], (n_far, rows_far, width)), far)
    part = part.reshape(half // n_near, width)
    part = exchange(jnp.broadcast_to(part[None], (n_near, half // n_near, width)), near)
    return lax.all_gather(part.reshape(half, width), "rep", axis=0, tiled=True)


def shards(
    node_latent,
    edge_saved,
    node_cot,
    edge_cot,
    senders,
    receivers,
    ghost_rows,
    w_edge_in,
    w_edge_out,
    edge_gain,
    edge_offset,
    w_node_in,
    w_node_out,
    node_gain,
):
    width = node_latent.shape[1]
    own = node_latent.shape[0]
    rows = 2 * own
    core = lax.axis_index("rep")
    slots = ghost_rows.shape[2] // 2
    parts = ghost_rows.shape[1]
    ghosts = parts * slots

    def local_row(index):
        moved = index - core * own
        return jnp.where(moved < 0, moved + rows, moved)

    partition = jnp.concatenate([node_latent, swapped(node_latent)], 0)
    lists = lax.dynamic_slice_in_dim(ghost_rows[0], core * slots, slots, 1).reshape(-1)
    pick_ghost = one_hot(local_row(lists), rows)
    outgoing = mat_mul(pick_ghost, partition).astype(bf16)
    arrived = lax.all_to_all(outgoing, "nodes", 0, 0, tiled=True)

    edge_latent = swapped(edge_saved)
    node_cots = jnp.concatenate([node_cot, swapped(node_cot)], 0)
    pick_recv = one_hot(local_row(receivers), rows)
    pick_local = one_hot(jnp.where(senders < rows, local_row(senders), -1), rows)
    slot = senders - rows
    side = ((slot >> 2) & 1) ^ core
    ghost_index = jnp.where(
        slot >= 0, side * ghosts + (slot >> 3) * slots + (slot & (slots - 1)), -1
    )
    pick_sent = one_hot(ghost_index, 2 * ghosts)
    recv_rows = mat_mul(pick_recv, partition).astype(bf16)
    local_rows = mat_mul(pick_local, partition)
    a1, a2, a3 = w_edge_in[:width], w_edge_in[width : 2 * width], w_edge_in[2 * width :]
    known = mat_mul(edge_latent, a1) + mat_mul(recv_rows, a3)

    ghost_table = jnp.concatenate([arrived, swapped(arrived)], 0)
    send_rows = (local_rows + mat_mul(pick_sent, ghost_table)).astype(bf16)
    pre_act = known + mat_mul(send_rows, a2)
    edge_hidden = jax.nn.silu(pre_act).astype(bf16)
    edge_normed, edge_inverse = norm_forward(mat_mul(edge_hidden, w_edge_out))
    message = edge_normed * edge_gain + edge_offset
    high, low = split_two(message)
    partial = mat_tn(pick_recv, high) + mat_tn(pick_recv, low)
    totals = (partial + jnp.roll(swapped(partial), own, 0)).astype(bf16)

    b1, b2 = w_node_in[:width], w_node_in[width:]
    node_pre = mat_mul(partition, b1) + mat_mul(totals, b2)
    node_hidden = jax.nn.silu(node_pre).astype(bf16)
    node_normed, node_inverse = norm_forward(mat_mul(node_hidden, w_node_out))
    node_grad_out = norm_backward(
        node_cots.astype(f32) * node_gain, node_normed, node_inverse
    ).astype(bf16)
    node_grad_act = (mat_nt(node_grad_out, w_node_out) * silu_slope(node_pre)).astype(bf16)
    totals_grad = mat_nt(node_grad_act, b2).astype(bf16)
    direct_grad = mat_nt(node_grad_act[:own], b1)

    message_grad = edge_cot.astype(f32) + mat_mul(pick_recv, totals_grad)
    edge_grad_out = norm_backward(
        message_grad * edge_gain, edge_normed, edge_inverse
    ).astype(bf16)
    edge_grad_act = (mat_nt(edge_grad_out, w_edge_out) * silu_slope(pre_act)).astype(bf16)
    grad_edges = (edge_cot.astype(f32) + mat_nt(edge_grad_act, a1)).astype(bf16)

    sent_sum = mat_tn(pick_sent, edge_grad_act)
    paired = (sent_sum[:ghosts] + swapped(sent_sum[ghosts:].astype(bf16)).astype(f32)).astype(bf16)
    returned = lax.all_to_all(paired, "nodes", 0, 0, tiled=True)

    device_count = lax.axis_size("nodes") * lax.axis_size("rep")
    edge_scale = 1.0 / math.sqrt(senders.shape[0] * device_count)
    node_scale = 1.0 / math.sqrt(own * device_count)
    weight_grads = jnp.concatenate(
        [
            mat_tn(edge_latent, edge_grad_act) * edge_scale,
            mat_tn(send_rows, edge_grad_act) * edge_scale,
            mat_tn(recv_rows, edge_grad_act) * edge_scale,
            mat_tn(edge_hidden, edge_grad_out) * edge_scale,
            mat_tn(node_latent, node_grad_act[:own]) * node_scale,
            mat_tn(totals[:own], node_grad_act[:own]) * node_scale,
            mat_tn(node_hidden[:own], node_grad_out[:own]) * node_scale,
        ],
        0,
    )

    send_high, send_low = split_two(mat_tn(pick_local, edge_grad_act) + mat_tn(pick_ghost, returned))
    recv_high, recv_low = split_two(mat_tn(pick_recv, edge_grad_act))
    row_grad = (
        mat_nt(recv_high, a3) + mat_nt(recv_low, a3) + mat_nt(send_high, a2) + mat_nt(send_low, a2)
    )
    own_grad = row_grad[:own] + swapped(row_grad[own:])
    grad_nodes = (own_grad + direct_grad + node_cot.astype(f32)).astype(bf16)

    total = total_over_devices(weight_grads, core)
    return (
        grad_nodes,
        grad_edges,
        total[: 3 * width],
        total[3 * width : 4 * width],
        total[4 * width : 6 * width],
        total[6 * width :],
    )


def solution(mesh):
    rows = P(("nodes", "rep"), None)
    flat = P(("nodes", "rep"))
    return jax.shard_map(
        shards,
        mesh=mesh,
        in_specs=(rows, rows, rows, rows, flat, flat, P("nodes", None, None)) + (P(),) * 7,
        out_specs=(rows, rows, P(), P(), P(), P()),
        check_vma=False,
    )
```

time: 430 us -> 249 us (0.58)
  waiting for transfers between devices: 215 us -> 36.3 us
  other arithmetic: 58.3 us -> 11.5 us
  blocking collectives: 29.7 us -> 76.2 us
  local copies, waits for them, and re-layouts: 41.1 us -> 24.2 us
  matrix products: 34.7 us -> 46 us
  starting transfers between devices: 29.3 us -> 34.9 us
    psum x1 -> x0, waiting for transfers between devices: 207 us -> none  [shards(): lax.psum((weight_grads[0], weight_grads[1], weight_grads[2], weight_grads...]
    all_to_all x5 -> x4, blocking collectives: 29.7 us -> 76.2 us  [exchange(): lax.all_to_all(array, ('nodes', 'rep'), 0, 0, tiled=True, axis_index_grou...]
    scatter-add x4 -> x0, other arithmetic: 36.8 us -> none  [the longest x1 11.1 us: shards(): jax.ops.segment_sum(send_grad, senders, num_segments=node_table.shape[0])]
    all_to_all x3 -> x2, waiting for transfers between devices: 7.24 us -> 30.8 us  [the longest x1 17.3 us: shards(): arrived = lax.all_to_all(outgoing, 'nodes', 0, 0, tiled=True)]
    gather x5 -> x0, local copies, waits for them, and re-layouts: 17.4 us -> none  [the longest x2 7.13 us: shards(): partition_totals_grad[receivers].astype(jnp.float32)]
    dot_general x7 -> x13, matrix products: 7.9 us -> 22.9 us  [mat_tn(): lax.dot_general(left, right, (((0,), (0,)), ((), ())), preferred_element_...]
    ppermute x1 -> x8, starting transfers between devices: 0.55 us -> 13 us  [swapped(): return lax.ppermute(array, 'rep', pairs)]
    slice x3 -> x6, local copies, waits for them, and re-layouts: 1.28 us -> 8.5 us  [the longest x1 2.71 us: shards(): total[:3 * width]]
  transfers between devices with their start and end apart: 5 -> 11, of which waited for: 4 -> 4; matrix products, arithmetic and copies ran while one was open for 16% -> 12% of each run, Pallas kernels for 0% -> 0%
where the time goes in v1:
time: 249 us; the launch traced here: 244 us
  blocking collectives  76.2 us (31%)
  matrix products  46 us (18%)
  waiting for transfers between devices  36.3 us (15%)
  starting transfers between devices  34.9 us (14%)
  local copies, waits for them, and re-layouts  24.2 us (10%)
  between operations  15 us (6%)
  other arithmetic  11.5 us (5%)
    all_to_all x4, blocking collectives, exchange(): lax.all_to_all(array, ('nodes', 'rep'), 0, 0, tiled=True, axis_index_grou...  76.2 us
    dot_general x13, matrix products, mat_tn(): lax.dot_general(left, right, (((0,), (0,)), ((), ())), preferred_element_...  22.9 us
    all_to_all x1, waiting for transfers between devices, shards(): arrived = lax.all_to_all(outgoing, 'nodes', 0, 0, tiled=True)  17.3 us
    dot_general x12, matrix products, mat_mul(): return jnp.dot(left, right, preferred_element_type=f32)  15.6 us
    all_to_all x1, starting transfers between devices, shards(): arrived = lax.all_to_all(outgoing, 'nodes', 0, 0, tiled=True)  13.8 us
    all_to_all x1, waiting for transfers between devices, shards(): returned = lax.all_to_all(paired, 'nodes', 0, 0, tiled=True)  13.5 us
    ppermute x8, starting transfers between devices, swapped(): return lax.ppermute(array, 'rep', pairs)  13 us
    unnamed x66, local copies, waits for them, and re-layouts  10.3 us
  transfers between devices with their start and end apart: 11, of which 4 were waited for; matrix products, arithmetic and copies ran while one was open for 12% of the time, Pallas kernels for 0%

profile of v1, /device:TPU:1, one launch (start us, length us, event | category | flops | bytes accessed | tf_op | source)
XLA Modules:
  0.0 244.2 jit_solution(6875892590373461369)
XLA Ops:
  7.2 3.3 %collective-permute-start.1 = (bf16[160,512]{1,0:T(8,128)(2,1)}, bf16[160,512]{1,0:T(8,128)(2,1)S(1)}, u32[]{:S(2)}, u32[]{:S(2)}) collective-permute-start(bf16[160,512]{1,0:T(8,128)(2,1)} %param.14), channel_id=1, source_target_pairs={{0,1},{1,0},{2,3},{3,2},{4,5},{5,4},{6,7},{7,6},{8,9},{9,8},{10,11... | collective-permute-start | bytes 491528 | tf_op jit(solution)/shard_map/ppermute | solution.py:15
  13.9 13.8 %all-to-all-start = ((bf16[128,4,512]{2,1,0:T(4,128)(2,1)}), bf16[128,4,512]{2,1,0:T(4,128)(2,1)S(1)}, u32[]{:S(2)}, u32[]{:S(2)}) async-start(bf16[128,4,512]{2,1,0:T(4,128)(2,1)} %all_to_all.28), calls=%async_computation | async-start | bytes 1048576 | tf_op jit(solution)/shard_map/all_to_all | solution.py:128
  28.1 17.3 %all-to-all-done = bf16[128,4,512]{2,1,0:T(4,128)(2,1)S(1)} async-done(((bf16[128,4,512]{2,1,0:T(4,128)(2,1)}), bf16[128,4,512]{2,1,0:T(4,128)(2,1)S(1)}, u32[]{:S(2)}, u32[]{:S(2)}) %all-to-all-start) | async-done | bytes 524320 | tf_op jit(solution)/shard_map/all_to_all | solution.py:128
  45.6 2.1 collective-permute-start.2
  53.1 2.2 fusion.3
  61.5 2.4 copy.27
  75.3 4.7 %fusion.87 = (f32[1280]{0:T(1024)S(1)}, f32[1280]{0:T(1024)S(1)}, f32[1280,512]{0,1:T(8,128)}) fusion(f32[1280]{0:T(1024)S(1)} %add_rsqrt_fusion, f32[1280,512]{0,1:T(8,128)S(1)} %get-tuple-element.29, f32[1280]{0:T(1024)S(1)} %broadcast_multiply_fusion.2, f32[512]{0:T(512)S(1)} %copy-done.27, bf16[320,512]{1,0:T(8,128)(2,1)} %copy-done.16, ...), kind=kOutput, calls=%fused_computation.142 | convolution fusion | flops 593016320 | bytes 7433216 | tf_op jit(solution)/shard_map/dot_general | solution.py:19
  80.0 2.5 %multiply_convert_fusion = bf16[1280,512]{0,1:T(8,128)(2,1)S(1)} fusion(f32[1280,512]{0,1:T(8,128)} %get-tuple-element.34, f32[1280,512]{0,1:T(8,128)S(1)} %get-tuple-element.29, f32[1280]{0:T(1024)S(1)} %broadcast_multiply_fusion, f32[1280]{0:T(1024)S(1)} %broadcast_multiply_fusion.1, f32[1280]{0:T(1024)S(1)} %add_rsqrt_fusion, ...), kind=kLoop, calls=%fused_computation.19 | loop fusion | flops 4587520 | bytes 6574080 | tf_op jit(solution)/shard_map/convert_element_type | solution.py:169
  84.1 3.7 %fusion.20 = f32[3584,512]{1,0:T(8,128)} fusion(bf16[1280,512]{1,0:T(8,128)(2,1)S(1)} %fusion.6, bf16[1280,512]{1,0:T(8,128)(2,1)} %collective-permute-done), kind=kOutput, calls=%fused_computation.47 | convolution fusion | flops 671350784 | bytes 3670016 | tf_op jit(solution)/shard_map/dot_general | solution.py:23
  97.5 2.3 dynamic-slice_convert_fusion
  99.9 3.9 %collective-permute-done.7 = bf16[1792,512]{1,0:T(8,128)(2,1)} collective-permute-done((bf16[1792,512]{1,0:T(8,128)(2,1)S(1)}, bf16[1792,512]{1,0:T(8,128)(2,1)}, u32[]{:S(2)}, u32[]{:S(2)}) %collective-permute-start.7) | collective-permute-done | bytes 1835040 | tf_op jit(solution)/shard_map/ppermute | solution.py:15
  103.8 3.2 %add_convert_fusion = bf16[1792,512]{1,0:T(8,128)(2,1)S(1)} fusion(bf16[1792,512]{1,0:T(8,128)(2,1)} %collective-permute-done.7, f32[3584,512]{1,0:T(8,128)} %fusion.13, s32[]{:T(128)S(6)} %select_n.37), kind=kLoop, calls=%fused_computation.5 | loop fusion | flops 2752512 | bytes 7340036 | tf_op jit(solution)/shard_map/convert_element_type | solution.py:83
  107.0 17.0 %all_to_all.44 = bf16[4,448,512]{2,1,0:T(8,128)(2,1)S(1)} all-to-all(bf16[4,448,512]{2,1,0:T(8,128)(2,1)S(1)} %bitcast.38), channel_id=1, replica_groups={{0,2,4,6},{8,10,12,14},{16,18,20,22},{24,26,28,30},{32,34,36,38},{40,42..., dimensions={0} | all-to-all | bytes 3670016 | tf_op jit(solution)/shard_map/all_to_all | solution.py:72
  124.6 21.1 %all_to_all.45 = bf16[32,14,512]{2,1,0:T(8,128)(2,1)S(1)} all-to-all(bf16[32,14,512]{2,1,0:T(8,128)(2,1)S(1)} %reshape.87), channel_id=1, replica_groups={{0,8,16,24,32,40,48,56,64,72,80,88,96,104,112,120,128,136,144,152,160,1..., dimensions={0} | all-to-all | bytes 917504 | tf_op jit(solution)/shard_map/all_to_all | solution.py:72
  145.9 20.9 %all_to_all.46 = bf16[32,14,512]{2,1,0:T(8,128)(2,1)S(1)} all-to-all(bf16[32,14,512]{2,1,0:T(8,128)(2,1)S(1)} %broadcast_in_dim.12), channel_id=1, replica_groups={{0,8,16,24,32,40,48,56,64,72,80,88,96,104,112,120,128,136,144,152,160,1..., dimensions={0} | all-to-all | bytes 917504 | tf_op jit(solution)/shard_map/all_to_all | solution.py:72
  167.1 17.3 %all_to_all.47 = bf16[4,448,512]{2,1,0:T(8,128)(2,1)} all-to-all(bf16[4,448,512]{2,1,0:T(8,128)(2,1)S(1)} %broadcast_in_dim.14), channel_id=1, replica_groups={{0,2,4,6},{8,10,12,14},{16,18,20,22},{24,26,28,30},{32,34,36,38},{40,42..., dimensions={0} | all-to-all | bytes 3670016 | tf_op jit(solution)/shard_map/all_to_all | solution.py:72
  186.4 3.3 %collective-permute-start.5 = (bf16[512,512]{1,0:T(8,128)(2,1)S(1)}, bf16[512,512]{1,0:T(8,128)(2,1)S(1)}, u32[]{:S(2)}, u32[]{:S(2)}) collective-permute-start(bf16[512,512]{1,0:T(8,128)(2,1)S(1)} %slice.147), channel_id=1, source_target_pairs={{0,1},{1,0},{2,3},{3,2},{4,5},{5,4},{6,7},{7,6},{8,9},{9,8},{10,11... | collective-permute-start | bytes 1572872 | tf_op jit(solution)/shard_map/ppermute | solution.py:15
  192.3 8.1 %all-to-all-start.1 = ((bf16[128,4,512]{2,1,0:T(4,128)(2,1)}), bf16[128,4,512]{2,1,0:T(4,128)(2,1)S(1)}, u32[]{:S(2)}, u32[]{:S(2)}) async-start(bf16[128,4,512]{2,1,0:T(4,128)(2,1)} %all_to_all.31), calls=%async_computation.1 | async-start | bytes 1048576 | tf_op jit(solution)/shard_map/all_to_all | solution.py:175
  204.1 13.5 %all-to-all-done.1 = bf16[128,4,512]{2,1,0:T(4,128)(2,1)S(1)} async-done(((bf16[128,4,512]{2,1,0:T(4,128)(2,1)}), bf16[128,4,512]{2,1,0:T(4,128)(2,1)S(1)}, u32[]{:S(2)}, u32[]{:S(2)}) %all-to-all-start.1) | async-done | bytes 524320 | tf_op jit(solution)/shard_map/all_to_all | solution.py:175
  220.2 3.1 %collective-permute-start.6 = (f32[160,512]{1,0:T(8,128)S(1)}, f32[160,512]{1,0:T(8,128)S(1)}, u32[]{:S(2)}, u32[]{:S(2)}) collective-permute-start(f32[160,512]{1,0:T(8,128)S(1)} %slice.86), channel_id=1, source_target_pairs={{0,1},{1,0},{2,3},{3,2},{4,5},{5,4},{6,7},{7,6},{8,9},{9,8},{10,11... | collective-permute-start | bytes 983048 | tf_op jit(solution)/shard_map/ppermute | solution.py:15
  225.2 2.4 copy.32
  229.7 2.7 %slice.91 = bf16[1536,512]{1,0:T(8,128)(2,1)} slice(bf16[3584,512]{1,0:T(8,128)(2,1)} %all-gather.2.cloned.1.call-done), slice={[0:1536], [0:512]} | slice | bytes 3145728 | tf_op jit(solution)/shard_map/slice | solution.py:205
  232.4 2.2 fusion.88
  234.7 2.3 slice.93
  (142 shorter events, 54.0 us)
Async XLA Ops:
  7.2 48.1 %copy-start = (bf16[512,512]{1,0:T(8,128)(2,1)S(1)}, bf16[512,512]{1,0:T(8,128)(2,1)}, u32[]{:S(2)}) copy-start(bf16[512,512]{1,0:T(8,128)(2,1)} %param.22) | copy-start | bytes 1572868
  7.2 20.9 %copy-start.25 = (s32[1280]{0:T(1024)S(1)}, s32[1280]{0:T(1024)}, u32[]{:S(2)}) copy-start(s32[1280]{0:T(1024)} %param.19) | copy-start | bytes 15364
  7.2 20.9 %copy-start.24 = (s32[1280]{0:T(1024)S(1)}, s32[1280]{0:T(1024)}, u32[]{:S(2)}) copy-start(s32[1280]{0:T(1024)} %param.18) | copy-start | bytes 15364
  7.2 5.2 %collective-permute-start.1 = (bf16[160,512]{1,0:T(8,128)(2,1)}, bf16[160,512]{1,0:T(8,128)(2,1)S(1)}, u32[]{:S(2)}, u32[]{:S(2)}) collective-permute-start(bf16[160,512]{1,0:T(8,128)(2,1)} %param.14), channel_id=1, source_target_pairs={{0,1},{1,0},{2,3},{3,2},{4,5},{5,4},{6,7},{7,6},{8,9},{9,8},{10,11... | collective-permute-start | bytes 491528 | tf_op jit(solution)/shard_map/ppermute | solution.py:15
  12.4 38.9 %copy-start.13 = (bf16[320,512]{1,0:T(8,128)(2,1)}, bf16[320,512]{1,0:T(8,128)(2,1)S(1)}, u32[]{:S(2)}) copy-start(bf16[320,512]{1,0:T(8,128)(2,1)S(1)} %constant_dynamic-update-slice_fusion) | copy-start | bytes 983044
  12.9 35.6 %copy-start.2 = (bf16[1536,512]{1,0:T(8,128)(2,1)S(1)}, bf16[1536,512]{1,0:T(8,128)(2,1)}, u32[]{:S(2)}) copy-start(bf16[1536,512]{1,0:T(8,128)(2,1)} %param.21) | copy-start | bytes 4718596
  13.9 31.6 %all-to-all-start = ((bf16[128,4,512]{2,1,0:T(4,128)(2,1)}), bf16[128,4,512]{2,1,0:T(4,128)(2,1)S(1)}, u32[]{:S(2)}, u32[]{:S(2)}) async-start(bf16[128,4,512]{2,1,0:T(4,128)(2,1)} %all_to_all.28), calls=%async_computation | async-start | bytes 1048576 | tf_op jit(solution)/shard_map/all_to_all | solution.py:128
  27.6 202.1 %all-gather.2.cloned.1.call-start = ((), (), s32[]{:S(2)}) async-start(), calls=%async_computation.6 | async-start | bytes 5505024 | tf_op jit(solution)/shard_map/all_gather | solution.py:93
  27.7 25.4 %collective-permute-start = (bf16[1280,512]{1,0:T(8,128)(2,1)}, bf16[1280,512]{1,0:T(8,128)(2,1)}, u32[]{:S(2)}, u32[]{:S(2)}) collective-permute-start(bf16[1280,512]{1,0:T(8,128)(2,1)} %param.15), channel_id=1, source_target_pairs={{0,1},{1,0},{2,3},{3,2},{4,5},{5,4},{6,7},{7,6},{8,9},{9,8},{10,11... | collective-permute-start | bytes 3932168 | tf_op jit(solution)/shard_map/ppermute | solution.py:15
  45.6 3.8 %collective-permute-start.2 = (bf16[512,512]{1,0:T(8,128)(2,1)S(1)}, bf16[512,512]{1,0:T(8,128)(2,1)S(1)}, u32[]{:S(2)}, u32[]{:S(2)}) collective-permute-start(bf16[512,512]{1,0:T(8,128)(2,1)S(1)} %all_to_all.30), channel_id=1, source_target_pairs={{0,1},{1,0},{2,3},{3,2},{4,5},{5,4},{6,7},{7,6},{8,9},{9,8},{10,11... | collective-permute-start | bytes 1572872 | tf_op jit(solution)/shard_map/ppermute | solution.py:15
  60.8 3.1 %collective-permute-start.3 = (f32[320,512]{1,0:T(8,128)}, f32[320,512]{1,0:T(8,128)}, u32[]{:S(2)}, u32[]{:S(2)}) collective-permute-start(f32[320,512]{1,0:T(8,128)} %fusion.30), channel_id=1, source_target_pairs={{0,1},{1,0},{2,3},{3,2},{4,5},{5,4},{6,7},{7,6},{8,9},{9,8},{10,11... | collective-permute-start | bytes 1966088 | tf_op jit(solution)/shard_map/ppermute | solution.py:15
  60.8 8.7 %collective-permute-start.4 = (bf16[160,512]{1,0:T(8,128)(2,1)}, bf16[160,512]{1,0:T(8,128)(2,1)}, u32[]{:S(2)}, u32[]{:S(2)}) collective-permute-start(bf16[160,512]{1,0:T(8,128)(2,1)} %param.16), channel_id=1, source_target_pairs={{0,1},{1,0},{2,3},{3,2},{4,5},{5,4},{6,7},{7,6},{8,9},{9,8},{10,11... | collective-permute-start | bytes 491528 | tf_op jit(solution)/shard_map/ppermute | solution.py:15
  84.1 5.6 %copy-start.28 = (bf16[1280,512]{1,0:T(8,128)(2,1)}, bf16[1280,512]{1,0:T(8,128)(2,1)S(1)}, u32[]{:S(2)}) copy-start(bf16[1280,512]{1,0:T(8,128)(2,1)S(1)} %fusion.6) | copy-start | bytes 3932164
  84.1 3.7 %copy-start.5 = (bf16[1280,512]{1,0:T(8,128)(2,1)S(1)}, bf16[1280,512]{1,0:T(8,128)(2,1)}, u32[]{:S(2)}) copy-start(bf16[1280,512]{1,0:T(8,128)(2,1)} %copy-done.4) | copy-start | bytes 3932164
  99.8 4.0 %collective-permute-start.7 = (bf16[1792,512]{1,0:T(8,128)(2,1)S(1)}, bf16[1792,512]{1,0:T(8,128)(2,1)}, u32[]{:S(2)}, u32[]{:S(2)}) collective-permute-start(bf16[1792,512]{1,0:T(8,128)(2,1)S(1)} %dynamic-slice_convert_fusion), channel_id=1, source_target_pairs={{0,1},{1,0},{2,3},{3,2},{4,5},{5,4},{6,7},{7,6},{8,9},{9,8},{10,11... | collective-permute-start | bytes 5505032 | tf_op jit(solution)/shard_map/ppermute | solution.py:15
  167.1 17.3 %copy-start.29 = (bf16[1280,512]{1,0:T(8,128)(2,1)S(1)}, bf16[1280,512]{1,0:T(8,128)(2,1)}, u32[]{:S(2)}) copy-start(bf16[1280,512]{1,0:T(8,128)(2,1)} %copy-done.28) | copy-start | bytes 3932164
  186.4 4.8 %collective-permute-start.5 = (bf16[512,512]{1,0:T(8,128)(2,1)S(1)}, bf16[512,512]{1,0:T(8,128)(2,1)S(1)}, u32[]{:S(2)}, u32[]{:S(2)}) collective-permute-start(bf16[512,512]{1,0:T(8,128)(2,1)S(1)} %slice.147), channel_id=1, source_target_pairs={{0,1},{1,0},{2,3},{3,2},{4,5},{5,4},{6,7},{7,6},{8,9},{9,8},{10,11... | collective-permute-start | bytes 1572872 | tf_op jit(solution)/shard_map/ppermute | solution.py:15
  191.4 10.1 %copy-start.3 = (bf16[1536,512]{1,0:T(8,128)(2,1)S(1)}, bf16[1536,512]{1,0:T(8,128)(2,1)}, u32[]{:S(2)}) copy-start(bf16[1536,512]{1,0:T(8,128)(2,1)} %param.21) | copy-start | bytes 4718596
  192.3 25.3 %all-to-all-start.1 = ((bf16[128,4,512]{2,1,0:T(4,128)(2,1)}), bf16[128,4,512]{2,1,0:T(4,128)(2,1)S(1)}, u32[]{:S(2)}, u32[]{:S(2)}) async-start(bf16[128,4,512]{2,1,0:T(4,128)(2,1)} %all_to_all.31), calls=%async_computation.1 | async-start | bytes 1048576 | tf_op jit(solution)/shard_map/all_to_all | solution.py:175
  219.3 3.9 %copy-start.9 = (bf16[1280,512]{0,1:T(8,128)(2,1)S(1)}, bf16[1280,512]{0,1:T(8,128)(2,1)}, u32[]{:S(2)}) copy-start(bf16[1280,512]{0,1:T(8,128)(2,1)} %copy.27) | copy-start | bytes 3932164
  219.3 3.9 %copy-start.30 = (bf16[1280,512]{1,0:T(8,128)(2,1)S(1)}, bf16[1280,512]{1,0:T(8,128)(2,1)}, u32[]{:S(2)}) copy-start(bf16[1280,512]{1,0:T(8,128)(2,1)} %copy-done.28) | copy-start | bytes 3932164
  220.1 7.5 %copy-start.18 = (bf16[320,512]{1,0:T(8,128)(2,1)S(1)}, bf16[320,512]{1,0:T(8,128)(2,1)}, u32[]{:S(2)}) copy-start(bf16[320,512]{1,0:T(8,128)(2,1)} %copy-done.16) | copy-start | bytes 983044
  220.2 7.5 %collective-permute-start.6 = (f32[160,512]{1,0:T(8,128)S(1)}, f32[160,512]{1,0:T(8,128)S(1)}, u32[]{:S(2)}, u32[]{:S(2)}) collective-permute-start(f32[160,512]{1,0:T(8,128)S(1)} %slice.86), channel_id=1, source_target_pairs={{0,1},{1,0},{2,3},{3,2},{4,5},{5,4},{6,7},{7,6},{8,9},{9,8},{10,11... | collective-permute-start | bytes 983048 | tf_op jit(solution)/shard_map/ppermute | solution.py:15
  229.7 7.2 %copy-start.1 = (bf16[512,512]{1,0:T(8,128)(2,1)S(1)}, bf16[512,512]{1,0:T(8,128)(2,1)}, u32[]{:S(2)}) copy-start(bf16[512,512]{1,0:T(8,128)(2,1)} %param.22) | copy-start | bytes 1572868
  (18 other events, 33.1 us)
Sparse Core Ops, SparseCore 0:
  184.5 17.0 all-gather.1

commit v2 on v1

v2 whole, which is shorter than its diff:
```python
import functools
import math

import jax
import jax.numpy as jnp
from jax import lax
from jax.experimental import pallas as pl
from jax.experimental.pallas import tpu as pltpu
from jax.sharding import PartitionSpec as P

EPS = 1e-05
bf16 = jnp.bfloat16
f32 = jnp.float32


def swapped(array):
    pairs = [(i, 1 - i) for i in range(2)]
    return lax.ppermute(array, "rep", pairs)


def mat_mul(left, right):
    return jnp.dot(left, right, preferred_element_type=f32)


def mat_tn(left, right):
    return lax.dot_general(left, right, (((0,), (0,)), ((), ())), preferred_element_type=f32)


def mat_nt(left, right):
    return lax.dot_general(left, right, (((1,), (1,)), ((), ())), preferred_element_type=f32)


def split_two(value):
    high = lax.reduce_precision(value, 8, 7)
    return high.astype(bf16), (value - high).astype(bf16)


def silu_slope(value):
    sigmoid_v = jax.nn.sigmoid(value)
    return sigmoid_v * (1.0 + value * (1.0 - sigmoid_v))


def norm_forward(value):
    centred = value - jnp.mean(value, axis=-1, keepdims=True)
    inverse = lax.rsqrt(jnp.mean(centred * centred, axis=-1, keepdims=True) + EPS)
    return (centred * inverse, inverse)


def norm_backward(grad_hat, normed, inverse):
    return inverse * (
        grad_hat
        - jnp.mean(grad_hat, axis=-1, keepdims=True)
        - normed * jnp.mean(grad_hat * normed, axis=-1, keepdims=True)
    )


def one_hot(index, width):
    return (index[:, None] == lax.broadcasted_iota(jnp.int32, (1, width), 1)).astype(bf16)


def groups(sizes):
    ny, nz, nx = sizes

    def device(y, z, x, r):
        return ((y * nz + z) * nx + x) * 2 + r

    near = [[device(y, z, x, 0) for x in range(nx)] for y in range(ny) for z in range(nz)]
    near += [[device(y, z, x, 1) for y in range(ny)] for x in range(nx) for z in range(nz)]
    far = [[device(y, z, x, 0) for y in range(ny) for z in range(nz)] for x in range(nx)]
    far += [[device(y, z, x, 1) for x in range(nx) for z in range(nz)] for y in range(ny)]
    return near, far


NEAR, FAR = groups((4, 8, 4))


def exchange(array, stage):
    return lax.all_to_all(array, ("nodes", "rep"), 0, 0, tiled=True, axis_index_groups=stage)


def summed(value, stage):
    count = len(stage[0])
    blocks = exchange(value.reshape(count, value.shape[0] // count, value.shape[1]), stage)
    return jnp.sum(blocks.astype(f32), axis=0).astype(bf16)


def gathered(value, stage):
    count = len(stage[0])
    blocks = exchange(jnp.broadcast_to(value[None], (count, *value.shape)), stage)
    return blocks.reshape(count * value.shape[0], value.shape[1])


def reduced(kept, sent, core):
    value = (kept + swapped(sent).astype(f32)).astype(bf16)
    return summed(summed(value, NEAR), FAR)


def spread(value, core):
    value = gathered(gathered(value, FAR), NEAR)
    width = value.shape[1]
    return assemble(value, swapped(value), core, [3 * width, width, 2 * width, width])


def assemble_kernel(sizes, core_ref, mine_ref, got_ref, *refs):
    outs, sems = refs[:-1], refs[-1]
    core = core_ref[0]
    copies = []
    start = 0
    half = mine_ref.shape[1] // 2
    for k, rows in enumerate(sizes):
        for block in range(rows // (2 * half)):
            for source, place in ((mine_ref, core), (got_ref, 1 - core)):
                row = pl.multiple_of(block * 2 * half + place * half, half)
                copies.append(
                    pltpu.make_async_copy(
                        source.at[pl.ds(start, half), :],
                        outs[k].at[pl.ds(row, half), :],
                        sems.at[len(copies)],
                    )
                )
            start += half
    for copy in copies:
        copy.start()
    for copy in copies:
        copy.wait()


def assemble(mine, got, core, sizes):
    return pl.pallas_call(
        functools.partial(assemble_kernel, sizes),
        out_shape=[jax.ShapeDtypeStruct((rows, mine.shape[1]), mine.dtype) for rows in sizes],
        in_specs=[pl.BlockSpec(memory_space=pltpu.SMEM)]
        + [pl.BlockSpec(memory_space=pltpu.VMEM)] * 2,
        out_specs=[pl.BlockSpec(memory_space=pl.ANY)] * len(sizes),
        scratch_shapes=[pltpu.SemaphoreType.DMA((14,))],
        name="assemble",
    )(core.astype(jnp.int32).reshape(1), mine, got)


CHUNK = 1280


def by_lane(index, count):
    return (index == lax.broadcasted_iota(jnp.int32, (index.shape[0], count), 1)).astype(bf16)


def by_row(index, count):
    return (index == lax.broadcasted_iota(jnp.int32, (count, index.shape[1]), 0)).astype(bf16)


def in_two(value):
    high = value.astype(bf16)
    return high, (value - high.astype(f32)).astype(bf16)


def silu_parts(value):
    sigmoid_v = 1.0 / (1.0 + jnp.exp(-value))
    return value * sigmoid_v, sigmoid_v * (1.0 + value * (1.0 - sigmoid_v))


def each_chunk(count, body):
    def step(i, carry):
        body(pl.ds(pl.multiple_of(i * CHUNK, CHUNK), CHUNK))
        return carry

    lax.fori_loop(0, count // CHUNK, step, 0)


def forward_kernel(
    known_ref, local_ref, send_col_ref, recv_row_ref, mine_ref, theirs_ref, w_in_ref, w_out_ref, gain_ref,
    offset_ref, send_ref, slope_ref, hidden_ref, normed_ref, inverse_ref, totals_ref, high_ref, low_ref,
    table_ref,
):
    width = known_ref.shape[1]
    ghosts = mine_ref.shape[0]
    table_ref[:ghosts] = mine_ref[...]
    table_ref[ghosts:] = theirs_ref[...]
    count = totals_ref.shape[0]

    def body(at):
        index = send_col_ref[at] - count
        rows = mat_mul(by_lane(index, 2 * ghosts), table_ref[...])
        send_rows = (local_ref[at].astype(f32) + rows).astype(bf16)
        send_ref[at] = send_rows
        pre_act = known_ref[at] + mat_mul(send_rows, w_in_ref[width : 2 * width])
        hidden, slope = silu_parts(pre_act)
        slope_ref[at] = slope
        hidden = hidden.astype(bf16)
        hidden_ref[at] = hidden
        normed, inverse = norm_forward(mat_mul(hidden, w_out_ref[...]))
        normed_ref[at] = normed
        inverse_ref[at] = jnp.broadcast_to(inverse, (CHUNK, inverse_ref.shape[1]))
        high, low = in_two(normed * gain_ref[...] + offset_ref[...])
        high_ref[at] = high
        low_ref[at] = low

    each_chunk(known_ref.shape[0], body)
    pick = by_row(recv_row_ref[...], count)
    totals_ref[...] = mat_mul(pick, high_ref[...]) + mat_mul(pick, low_ref[...])


def backward_kernel(
    partial_ref, other_ref, part_ref, node_cot_ref, w_node_in_ref, w_node_out_ref, node_gain_ref,
    cot_ref, slope_ref, normed_ref, inverse_ref,
    recv_col_ref, send_row_ref, w_out_ref, gain_ref,
    theirs_ref, mine_ref, grad_act_ref, grad_out_ref,
    totals_ref, node_hidden_ref, node_act_ref, node_out_ref,
    totals_grad_ref,
):
    width = cot_ref.shape[1]
    rows = part_ref.shape[0]
    own = rows // 2
    ghosts = mine_ref.shape[0]
    totals = jnp.concatenate(
        [partial_ref[:own] + other_ref[own:], partial_ref[own:] + other_ref[:own]], 0
    ).astype(bf16)
    node_pre = mat_mul(part_ref[...], w_node_in_ref[:width]) + mat_mul(
        totals, w_node_in_ref[width:]
    )
    hidden, slope = silu_parts(node_pre)
    hidden = hidden.astype(bf16)
    normed, inverse = norm_forward(mat_mul(hidden, w_node_out_ref[...]))
    grad_out = norm_backward(
        node_cot_ref[...].astype(f32) * node_gain_ref[...], normed, inverse
    ).astype(bf16)
    grad_act = (mat_nt(grad_out, w_node_out_ref[...]) * slope).astype(bf16)
    totals_grad_ref[...] = mat_nt(grad_act, w_node_in_ref[width:]).astype(bf16)
    totals_ref[...] = totals[:own]
    node_hidden_ref[...] = hidden[:own]
    node_act_ref[...] = grad_act[:own]
    node_out_ref[...] = grad_out[:own]

    def body(at):
        message_grad = cot_ref[at].astype(f32) + mat_mul(
            by_lane(recv_col_ref[at], rows), totals_grad_ref[...]
        )
        grad_out = norm_backward(
            message_grad * gain_ref[...], normed_ref[at], inverse_ref[at][:, :1]
        ).astype(bf16)
        grad_out_ref[at] = grad_out
        grad_act_ref[at] = (mat_nt(grad_out, w_out_ref[...]) * slope_ref[at]).astype(bf16)

    each_chunk(cot_ref.shape[0], body)
    index = send_row_ref[...]
    theirs_ref[...] = mat_mul(by_row(index - rows - ghosts, ghosts), grad_act_ref[...]).astype(bf16)
    mine_ref[...] = mat_mul(by_row(index - rows, ghosts), grad_act_ref[...])


def weights_kernel(
    core_ref, edge_ref, send_ref, recv_ref, hidden_ref, part_ref, totals_ref, node_hidden_ref,
    grad_act_ref, grad_out_ref, node_act_ref, node_out_ref, cot_ref, w_in_ref,
    recv_row_ref, send_row_ref, node_cot_ref, w_node_in_ref,
    kept_ref, sent_ref, grad_edge_ref, local_ref, recv_sum_ref, direct_ref, block_ref,
    *, edge_scale, node_scale,
):
    width = edge_ref.shape[1]
    half = width // 2
    core = core_ref[0]
    own = totals_ref.shape[0]
    products = [
        (edge_ref[...], grad_act_ref[...], edge_scale),
        (send_ref[...], grad_act_ref[...], edge_scale),
        (recv_ref[...], grad_act_ref[...], edge_scale),
        (hidden_ref[...], grad_out_ref[...], edge_scale),
        (part_ref[:own], node_act_ref[...], node_scale),
        (totals_ref[...], node_act_ref[...], node_scale),
        (node_hidden_ref[...], node_out_ref[...], node_scale),
    ]
    for k, (left, right, scale) in enumerate(products):
        block_ref[...] = mat_tn(left, right) * scale
        mine = block_ref[pl.ds(pl.multiple_of(core * half, half), half), :]
        other = block_ref[pl.ds(pl.multiple_of((1 - core) * half, half), half), :]
        kept_ref[k * half : (k + 1) * half] = mine
        sent_ref[k * half : (k + 1) * half] = other.astype(bf16)

    def body(at):
        grad_edge_ref[at] = (
            cot_ref[at].astype(f32) + mat_nt(grad_act_ref[at], w_in_ref[:width])
        ).astype(bf16)

    each_chunk(cot_ref.shape[0], body)
    rows = part_ref.shape[0]
    local_ref[...] = mat_mul(by_row(send_row_ref[...], rows), grad_act_ref[...])
    recv_sum_ref[...] = mat_mul(by_row(recv_row_ref[...], rows), grad_act_ref[...])
    direct_ref[...] = mat_nt(node_act_ref[...], w_node_in_ref[:width]) + node_cot_ref[...].astype(f32)


def run(kernel, name, arguments, results, scratch=(), scalars=0, flops=0):
    vmem = pl.BlockSpec(memory_space=pltpu.VMEM)
    return pl.pallas_call(
        kernel,
        in_specs=[pl.BlockSpec(memory_space=pltpu.SMEM)] * scalars
        + [vmem] * (len(arguments) - scalars),
        out_specs=[vmem] * len(results),
        out_shape=[jax.ShapeDtypeStruct(*result) for result in results],
        scratch_shapes=list(scratch),
        compiler_params=pltpu.CompilerParams(vmem_limit_bytes=60 * 1024 * 1024),
        cost_estimate=pl.CostEstimate(
            flops=flops, transcendentals=0, bytes_accessed=8 * 1024 * 1024
        ),
        name=name,
    )(*arguments)


def shards(
    node_latent,
    edge_saved,
    node_cot,
    edge_cot,
    senders,
    receivers,
    ghost_rows,
    w_edge_in,
    w_edge_out,
    edge_gain,
    edge_offset,
    w_node_in,
    w_node_out,
    node_gain,
):
    width = node_latent.shape[1]
    own = node_latent.shape[0]
    rows = 2 * own
    core = lax.axis_index("rep")
    slots = ghost_rows.shape[2] // 2
    parts = ghost_rows.shape[1]
    ghosts = parts * slots

    def local_row(index):
        moved = index - core * own
        return jnp.where(moved < 0, moved + rows, moved)

    partition = jnp.concatenate([node_latent, swapped(node_latent)], 0)
    lists = lax.dynamic_slice_in_dim(ghost_rows[0], core * slots, slots, 1).reshape(-1)
    pick_ghost = one_hot(local_row(lists), rows)
    outgoing = mat_mul(pick_ghost, partition).astype(bf16)
    arrived = lax.all_to_all(outgoing.reshape(parts, slots, width), "nodes", 0, 0, tiled=True)

    edge_latent = swapped(edge_saved)
    node_cots = jnp.concatenate([node_cot, swapped(node_cot)], 0)
    edges = senders.shape[0]
    receiver = local_row(receivers)
    slot = senders - rows
    side = ((slot >> 2) & 1) ^ core
    sender = jnp.where(
        slot >= 0,
        rows + side * ghosts + (slot >> 3) * slots + (slot & (slots - 1)),
        local_row(senders),
    )
    recv_col, send_col = receiver[:, None], sender[:, None]
    recv_row, send_row = receiver[None], sender[None]
    square = 2 * edges * width * width
    pick_recv = one_hot(receiver, rows)
    pick_local = one_hot(jnp.where(slot >= 0, -1, sender), rows)
    recv_rows = mat_mul(pick_recv, partition).astype(bf16)
    local_rows = mat_mul(pick_local, partition).astype(bf16)
    known = mat_mul(edge_latent, w_edge_in[:width]) + mat_mul(recv_rows, w_edge_in[2 * width :])
    arrived, known, local_rows, recv_rows, recv_col, send_col = lax.optimization_barrier(
        (arrived, known, local_rows, recv_rows, recv_col, send_col)
    )
    arrived = arrived.reshape(ghosts, width)
    send_rows, edge_slope, edge_hidden, edge_normed, edge_inverse, partial = run(
        forward_kernel,
        "forward",
        [
            known,
            local_rows,
            send_col,
            recv_row,
            arrived,
            swapped(arrived),
            w_edge_in,
            w_edge_out,
            edge_gain[None],
            edge_offset[None],
        ],
        [
            ((edges, width), bf16),
            ((edges, width), f32),
            ((edges, width), bf16),
            ((edges, width), f32),
            ((edges, 128), f32),
            ((rows, width), f32),
        ],
        [pltpu.VMEM((edges, width), bf16)] * 2 + [pltpu.VMEM((2 * ghosts, width), bf16)],
        flops=6 * square,
    )
    device_count = lax.axis_size("nodes") * lax.axis_size("rep")
    edge_scale = 1.0 / math.sqrt(edges * device_count)
    node_scale = 1.0 / math.sqrt(own * device_count)
    (
        theirs, mine, grad_act, grad_out,
        totals, node_hidden, node_act, node_out,
    ) = run(
        backward_kernel,
        "backward",
        [
            partial,
            swapped(partial),
            partition,
            node_cots,
            w_node_in,
            w_node_out,
            node_gain[None],
            edge_cot,
            edge_slope,
            edge_normed,
            edge_inverse,
            recv_col,
            send_row,
            w_edge_out,
            edge_gain[None],
        ],
        [
            ((ghosts, width), bf16),
            ((ghosts, width), f32),
            ((edges, width), bf16),
            ((edges, width), bf16),
        ]
        + [((own, width), bf16)] * 4,
        [pltpu.VMEM((rows, width), bf16)],
        flops=8 * square,
    )
    paired = (mine + swapped(theirs).astype(f32)).astype(bf16)
    paired, grad_act = lax.optimization_barrier((paired, grad_act))
    returned = lax.all_to_all(paired.reshape(parts, slots, width), "nodes", 0, 0, tiled=True)

    kept, sent, grad_edges, local_sum, recv_sum, direct_grad = run(
        functools.partial(weights_kernel, edge_scale=edge_scale, node_scale=node_scale),
        "weights",
        [
            core.astype(jnp.int32).reshape(1),
            edge_latent,
            send_rows,
            recv_rows,
            edge_hidden,
            partition,
            totals,
            node_hidden,
            grad_act,
            grad_out,
            node_act,
            node_out,
            edge_cot,
            w_edge_in,
            recv_row,
            send_row,
            node_cot,
            w_node_in,
        ],
        [((7 * width // 2, width), f32), ((7 * width // 2, width), bf16), ((edges, width), bf16)]
        + [((rows, width), f32)] * 2
        + [((own, width), f32)],
        [pltpu.VMEM((width, width), f32)],
        scalars=1,
        flops=6 * square,
    )

    kept, sent, returned = lax.optimization_barrier((kept, sent, returned))
    value = reduced(kept, sent, core)
    send_high, send_low = split_two(local_sum + mat_tn(pick_ghost, returned.reshape(ghosts, width)))
    recv_high, recv_low = split_two(recv_sum)
    a2, a3 = w_edge_in[width : 2 * width], w_edge_in[2 * width :]
    row_grad = (
        mat_nt(recv_high, a3) + mat_nt(recv_low, a3) + mat_nt(send_high, a2) + mat_nt(send_low, a2)
    )
    own_grad = row_grad[:own] + swapped(row_grad[own:])
    grad_nodes = (own_grad + direct_grad).astype(bf16)

    value, grad_nodes = lax.optimization_barrier((value, grad_nodes))
    total = spread(value, core)
    return (grad_nodes, grad_edges, *total)


def solution(mesh):
    rows = P(("nodes", "rep"), None)
    flat = P(("nodes", "rep"))
    return jax.shard_map(
        shards,
        mesh=mesh,
        in_specs=(rows, rows, rows, rows, flat, flat, P("nodes", None, None)) + (P(),) * 7,
        out_specs=(rows, rows, P(), P(), P(), P()),
        check_vma=False,
    )
```

time: 249 us -> 204 us (0.82); the launches traced: 244 us -> 203 us
  blocking collectives: 76.2 us -> 37.6 us
  Pallas kernels: 0 us -> 36.5 us
  matrix products: 46 us -> 12.4 us
  between operations: 15 us -> 1.11 us
  local copies, waits for them, and re-layouts: 24.2 us -> 12.6 us
  waiting for transfers between devices: 36.3 us -> 47.7 us
  starting transfers between devices: 34.9 us -> 43.5 us
    all_to_all x4 -> x2, blocking collectives: 76.2 us -> 37.6 us  [exchange(): lax.all_to_all(array, ('nodes', 'rep'), 0, 0, tiled=True, axis_index_grou...]
    pallas_call x0 -> x4, Pallas kernels: none -> 36.5 us  [the longest x3 32.5 us: run(): pl.pallas_call(kernel, in_specs=[pl.BlockSpec(memory_space=pltpu.SMEM)] *...]
    dot_general x13 -> x1, matrix products: 22.9 us -> 2.4 us  [mat_tn(): lax.dot_general(left, right, (((0,), (0,)), ((), ())), preferred_element_...]
    dot_general x12 -> x5, matrix products: 15.6 us -> 6.55 us  [mat_mul(): return jnp.dot(left, right, preferred_element_type=f32)]
    slice x5 -> x0, local copies, waits for them, and re-layouts: 8.47 us -> none  [the longest x1 2.71 us: shards(): total[:3 * width]]
    unnamed x66 -> x33, local copies, waits for them, and re-layouts: 10.3 us -> 2.62 us
    all_to_all x2 -> x4, starting transfers between devices: 21.9 us -> 29.2 us  [the longest x1 13.8 us: shards(): lax.all_to_all(outgoing.reshape(parts, slots, width), 'nodes', 0, 0, tile...]
    ppermute x8 -> x9, waiting for transfers between devices: 5.43 us -> 11.6 us  [swapped(): return lax.ppermute(array, 'rep', pairs)]
  transfers between devices with their start and end apart: 11 -> 13, of which waited for: 4 -> 9; matrix products, arithmetic and copies ran while one was open for 12% -> 12% of each run, Pallas kernels for 0% -> 6%
where the time goes in v2:
time: 204 us; the launch traced here: 203 us
  waiting for transfers between devices  47.7 us (23%)
  starting transfers between devices  43.5 us (21%)
  blocking collectives  37.6 us (18%)
  Pallas kernels  36.5 us (18%)
  local copies, waits for them, and re-layouts  12.6 us (6%)
  matrix products  12.4 us (6%)
  other arithmetic  11.2 us (5%)
    all_to_all x2, blocking collectives, exchange(): lax.all_to_all(array, ('nodes', 'rep'), 0, 0, tiled=True, axis_index_grou...  37.6 us
    pallas_call x3, Pallas kernels, run(): pl.pallas_call(kernel, in_specs=[pl.BlockSpec(memory_space=pltpu.SMEM)] *...  32.5 us
    all_to_all x2, waiting for transfers between devices, exchange(): lax.all_to_all(array, ('nodes', 'rep'), 0, 0, tiled=True, axis_index_grou...  19.5 us
    ppermute x9, starting transfers between devices, swapped(): return lax.ppermute(array, 'rep', pairs)  14.3 us
    all_to_all x1, starting transfers between devices, shards(): lax.all_to_all(outgoing.reshape(parts, slots, width), 'nodes', 0, 0, tile...  13.8 us
    ppermute x9, waiting for transfers between devices, swapped(): return lax.ppermute(array, 'rep', pairs)  11.6 us
    all_to_all x1, waiting for transfers between devices, shards(): lax.all_to_all(outgoing.reshape(parts, slots, width), 'nodes', 0, 0, tile...  11 us
    all_to_all x2, starting transfers between devices, exchange(): lax.all_to_all(array, ('nodes', 'rep'), 0, 0, tiled=True, axis_index_grou...  8.41 us
  transfers between devices with their start and end apart: 13, of which 9 were waited for; matrix products, arithmetic and copies ran while one was open for 12% of the time, Pallas kernels for 6%

profile of v2, /device:TPU:1, one launch (start us, length us, event | category | flops | bytes accessed | tf_op | source)
XLA Modules:
  0.0 202.7 jit_solution(839110266349953259)
XLA Ops:
  0.6 3.3 %collective-permute-start = (bf16[1280,512]{1,0:T(8,128)(2,1)}, bf16[1280,512]{1,0:T(8,128)(2,1)S(1)}, u32[]{:S(2)}, u32[]{:S(2)}) collective-permute-start(bf16[1280,512]{1,0:T(8,128)(2,1)} %param.15), channel_id=1, source_target_pairs={{0,1},{1,0},{2,3},{3,2},{4,5},{5,4},{6,7},{7,6},{8,9},{9,8},{10,11... | collective-permute-start | bytes 3932168 | tf_op jit(solution)/shard_map/ppermute | solution.py:18
  8.8 13.8 %all-to-all-start = ((bf16[128,4,512]{2,1,0:T(4,128)(2,1)}), bf16[128,4,512]{2,1,0:T(4,128)(2,1)S(1)}, u32[]{:S(2)}, u32[]{:S(2)}) async-start(bf16[128,4,512]{2,1,0:T(4,128)(2,1)} %reshape.55), calls=%async_computation | async-start | bytes 1048576 | tf_op jit(solution)/shard_map/all_to_all | solution.py:337
  26.3 2.4 %convolution_add_fusion.known_ref = f32[1280,512]{1,0:T(8,128)} fusion(f32[1280,512]{1,0:T(8,128)S(1)} %fusion.11, bf16[1280,512]{1,0:T(8,128)(2,1)S(1)} %collective-permute-done.edge_ref, bf16[1536,512]{1,0:T(8,128)(2,1)S(1)} %copy-done.1), kind=kOutput, calls=%fused_computation.1 | convolution fusion | flops 671744000 | bytes 7077888 | tf_op jit(solution)/shard_map/dot_general | solution.py:22
  28.7 11.0 %all-to-all-done = bf16[128,4,512]{2,1,0:T(4,128)(2,1)S(1)} async-done(((bf16[128,4,512]{2,1,0:T(4,128)(2,1)}), bf16[128,4,512]{2,1,0:T(4,128)(2,1)S(1)}, u32[]{:S(2)}, u32[]{:S(2)}) %all-to-all-start) | async-done | bytes 524320 | tf_op jit(solution)/shard_map/all_to_all | solution.py:337
  39.9 3.1 %collective-permute-start.2 = (bf16[512,512]{1,0:T(8,128)(2,1)S(1)}, bf16[512,512]{1,0:T(8,128)(2,1)S(1)}, u32[]{:S(2)}, u32[]{:S(2)}) collective-permute-start(bf16[512,512]{1,0:T(8,128)(2,1)S(1)} %reshape.56.mine_ref), channel_id=1, source_target_pairs={{0,1},{1,0},{2,3},{3,2},{4,5},{5,4},{6,7},{7,6},{8,9},{9,8},{10,11... | collective-permute-start | bytes 1572872 | tf_op jit(solution)/shard_map/ppermute | solution.py:18
  45.5 9.8 %forward.1 = (bf16[1280,512]{1,0:T(8,128)(2,1)}, f32[1280,512]{1,0:T(8,128)}, bf16[1280,512]{1,0:T(8,128)(2,1)}, f32[1280,512]{1,0:T(8,128)}, f32[1280,128]{1,0:T(8,128)}, /*index=5*/f32[320,512]{1,0:T(8,128)}) custom-call(f32[1280,512]{1,0:T(8,128)} %convolution_add_fusion.known_ref, bf16[1280,512]{1,0:T(8,128)(2,1)} %convolution_convert_fusion.local_ref, ...), custom_call_target="tpu_custom_call" | custom-call | flops 4026531840 | bytes 8388608 | tf_op jit(solution)/shard_map/forward/pallas_call | solution.py:290
  60.4 11.0 %backward.1 = (bf16[512,512]{1,0:T(8,128)(2,1)}, f32[512,512]{1,0:T(8,128)}, bf16[1280,512]{1,0:T(8,128)(2,1)}, bf16[1280,512]{1,0:T(8,128)(2,1)}, bf16[160,512]...) custom-call(f32[320,512]{1,0:T(8,128)} %get-tuple-element.50.partial_ref, ...), custom_call_target="tpu_custom_call" | custom-call | flops 5368709120 | bytes 8388608 | tf_op jit(solution)/shard_map/backward/pallas_call | solution.py:290
  75.8 7.0 %all-to-all-start.1 = ((bf16[128,4,512]{2,1,0:T(4,128)(2,1)}), bf16[128,4,512]{2,1,0:T(4,128)(2,1)S(1)}, u32[]{:S(2)}, u32[]{:S(2)}) async-start(bf16[128,4,512]{2,1,0:T(4,128)(2,1)} %reshape.57), calls=%async_computation.1 | async-start | bytes 1048576 | tf_op jit(solution)/shard_map/all_to_all | solution.py:426
  82.8 11.7 %weights.1 = (f32[1792,512]{1,0:T(8,128)}, bf16[1792,512]{1,0:T(8,128)(2,1)}, bf16[1280,512]{1,0:T(8,128)(2,1)}, f32[320,512]{1,0:T(8,128)}, f32[320,512]{1,0:T(8,128)}, /*index=5*/f32[160,512]{1,0:T(8,128)}) custom-call(s32[1]{0:T(128)} %bitcast.core_ref, bf16[1280,512]{1,0:T(8,128)(2,1)} %copy-done.8, bf16[1280,512]{1,0:T(8,128)(2,1)} %get-tuple-element.47.send_ref, ...), custom_call_target="tpu_custom_call" | custom-call | flops 4026531840 | bytes 8388608 | tf_op jit(solution)/shard_map/weights/pallas_call | solution.py:290
  94.6 5.6 %all-to-all-done.1 = bf16[128,4,512]{2,1,0:T(4,128)(2,1)S(1)} async-done(((bf16[128,4,512]{2,1,0:T(4,128)(2,1)}), bf16[128,4,512]{2,1,0:T(4,128)(2,1)S(1)}, u32[]{:S(2)}, u32[]{:S(2)}) %all-to-all-start.1) | async-done | bytes 524320 | tf_op jit(solution)/shard_map/all_to_all | solution.py:426
  100.2 2.2 %collective-permute-start.6 = (bf16[1792,512]{1,0:T(8,128)(2,1)}, bf16[1792,512]{1,0:T(8,128)(2,1)S(1)}, u32[]{:S(2)}, u32[]{:S(2)}) collective-permute-start(bf16[1792,512]{1,0:T(8,128)(2,1)} %get-tuple-element.68), channel_id=1, source_target_pairs={{0,1},{1,0},{2,3},{3,2},{4,5},{5,4},{6,7},{7,6},{8,9},{9,8},{10,11... | collective-permute-start | bytes 5505032 | tf_op jit(solution)/shard_map/ppermute | solution.py:18
  102.4 3.6 %collective-permute-done.6 = bf16[1792,512]{1,0:T(8,128)(2,1)S(1)} collective-permute-done((bf16[1792,512]{1,0:T(8,128)(2,1)}, bf16[1792,512]{1,0:T(8,128)(2,1)S(1)}, u32[]{:S(2)}, u32[]{:S(2)}) %collective-permute-start.6) | collective-permute-done | bytes 1835040 | tf_op jit(solution)/shard_map/ppermute | solution.py:18
  106.0 3.9 %add_convert_fusion = bf16[1792,512]{1,0:T(8,128)(2,1)} fusion(f32[1792,512]{1,0:T(8,128)} %get-tuple-element.67, bf16[1792,512]{1,0:T(8,128)(2,1)S(1)} %collective-permute-done.6), kind=kLoop, calls=%fused_computation | loop fusion | flops 2752512 | bytes 7340032 | tf_op jit(solution)/shard_map/convert_element_type | solution.py:94
  109.9 3.7 %all-to-all-start.2 = ((bf16[4,448,512]{2,1,0:T(8,128)(2,1)}), bf16[4,448,512]{2,1,0:T(8,128)(2,1)S(1)}, u32[]{:S(2)}, u32[]{:S(2)}) async-start(bf16[4,448,512]{2,1,0:T(8,128)(2,1)} %bitcast.4), calls=%async_computation.2 | async-start | bytes 3670016 | tf_op jit(solution)/shard_map/all_to_all | solution.py:78
  118.4 2.4 %fusion.2 = f32[320,512]{1,0:T(8,128)} fusion(bf16[512,512]{1,0:T(8,128)(2,1)} %reshape.60, s32[512]{0:T(512)S(1)} %compare_select_fusion.2), kind=kOutput, calls=%fused_computation.18 | convolution fusion | flops 167936000 | bytes 1181696 | tf_op jit(solution)/shard_map/dot_general | solution.py:26
  120.8 7.1 %all-to-all-done.2 = bf16[4,448,512]{2,1,0:T(8,128)(2,1)S(1)} async-done(((bf16[4,448,512]{2,1,0:T(8,128)(2,1)}), bf16[4,448,512]{2,1,0:T(8,128)(2,1)S(1)}, u32[]{:S(2)}, u32[]{:S(2)}) %all-to-all-start.2) | async-done | bytes 1835040 | tf_op jit(solution)/shard_map/all_to_all | solution.py:78
  129.0 2.1 %reshape.59 = bf16[32,14,512]{2,1,0:T(8,128)(2,1)} reshape(bf16[448,512]{1,0:T(8,128)(2,1)} %reduce_sum.24) | data formatting | bytes 917504 | tf_op jit(solution)/shard_map/reshape | solution.py:83
  131.1 4.7 %all-to-all-start.3 = ((bf16[32,14,512]{2,1,0:T(8,128)(2,1)}), bf16[32,14,512]{2,1,0:T(8,128)(2,1)}, u32[]{:S(2)}, u32[]{:S(2)}) async-start(bf16[32,14,512]{2,1,0:T(8,128)(2,1)} %reshape.59), calls=%async_computation.3 | async-start | bytes 1048576 | tf_op jit(solution)/shard_map/all_to_all | solution.py:78
  140.1 12.4 %all-to-all-done.3 = bf16[32,14,512]{2,1,0:T(8,128)(2,1)} async-done(((bf16[32,14,512]{2,1,0:T(8,128)(2,1)}), bf16[32,14,512]{2,1,0:T(8,128)(2,1)}, u32[]{:S(2)}, u32[]{:S(2)}) %all-to-all-start.3) | async-done | bytes 458784 | tf_op jit(solution)/shard_map/all_to_all | solution.py:78
  153.7 20.9 %all_to_all.30 = bf16[32,14,512]{2,1,0:T(8,128)(2,1)S(1)} all-to-all(bf16[32,14,512]{2,1,0:T(8,128)(2,1)S(1)} %broadcast_in_dim.50), channel_id=1, replica_groups={{0,8,16,24,32,40,48,56,64,72,80,88,96,104,112,120,128,136,144,152,160,1..., dimensions={0} | all-to-all | bytes 917504 | tf_op jit(solution)/shard_map/all_to_all | solution.py:78
  174.9 16.7 %all_to_all.31 = bf16[4,448,512]{2,1,0:T(8,128)(2,1)S(1)} all-to-all(bf16[4,448,512]{2,1,0:T(8,128)(2,1)S(1)} %broadcast_in_dim.52), channel_id=1, replica_groups={{0,2,4,6},{8,10,12,14},{16,18,20,22},{24,26,28,30},{32,34,36,38},{40,42..., dimensions={0} | all-to-all | bytes 3670016 | tf_op jit(solution)/shard_map/all_to_all | solution.py:78
  191.6 3.3 %collective-permute-start.8 = (bf16[1792,512]{1,0:T(8,128)(2,1)S(1)}, bf16[1792,512]{1,0:T(8,128)(2,1)}, u32[]{:S(2)}, u32[]{:S(2)}) collective-permute-start(bf16[1792,512]{1,0:T(8,128)(2,1)S(1)} %bitcast.12), channel_id=1, source_target_pairs={{0,1},{1,0},{2,3},{3,2},{4,5},{5,4},{6,7},{7,6},{8,9},{9,8},{10,11... | collective-permute-start | bytes 5505032 | tf_op jit(solution)/shard_map/ppermute | solution.py:18
  195.0 3.5 %collective-permute-done.8.got_ref = bf16[1792,512]{1,0:T(8,128)(2,1)} collective-permute-done((bf16[1792,512]{1,0:T(8,128)(2,1)S(1)}, bf16[1792,512]{1,0:T(8,128)(2,1)}, u32[]{:S(2)}, u32[]{:S(2)}) %collective-permute-start.8) | collective-permute-done | bytes 1835040 | tf_op jit(solution)/shard_map/ppermute | solution.py:18
  198.5 4.0 %assemble.1 = (bf16[1536,512]{1,0:T(8,128)(2,1)}, bf16[512,512]{1,0:T(8,128)(2,1)}, bf16[1024,512]{1,0:T(8,128)(2,1)}, bf16[512,512]{1,0:T(8,128)(2,1)}) custom-call(s32[1]{0:T(128)} %bitcast.core_ref, bf16[1792,512]{1,0:T(8,128)(2,1)} %bitcast.13, bf16[1792,512]{1,0:T(8,128)(2,1)} %collective-permute-done.8.got_ref), custom_call_target="tpu_custom_call" | custom-call | tf_op jit(solution)/shard_map/assemble/pallas_call | solution.py:129
  (79 shorter events, 32.2 us)
Async XLA Ops:
  0.6 25.7 %collective-permute-start = (bf16[1280,512]{1,0:T(8,128)(2,1)}, bf16[1280,512]{1,0:T(8,128)(2,1)S(1)}, u32[]{:S(2)}, u32[]{:S(2)}) collective-permute-start(bf16[1280,512]{1,0:T(8,128)(2,1)} %param.15), channel_id=1, source_target_pairs={{0,1},{1,0},{2,3},{3,2},{4,5},{5,4},{6,7},{7,6},{8,9},{9,8},{10,11... | collective-permute-start | bytes 3932168 | tf_op jit(solution)/shard_map/ppermute | solution.py:18
  4.0 3.4 %collective-permute-start.1 = (bf16[160,512]{1,0:T(8,128)(2,1)}, bf16[160,512]{1,0:T(8,128)(2,1)S(1)}, u32[]{:S(2)}, u32[]{:S(2)}) collective-permute-start(bf16[160,512]{1,0:T(8,128)(2,1)} %param.14), channel_id=1, source_target_pairs={{0,1},{1,0},{2,3},{3,2},{4,5},{5,4},{6,7},{7,6},{8,9},{9,8},{10,11... | collective-permute-start | bytes 491528 | tf_op jit(solution)/shard_map/ppermute | solution.py:18
  7.4 16.1 %copy-start.13 = (bf16[320,512]{1,0:T(8,128)(2,1)}, bf16[320,512]{1,0:T(8,128)(2,1)S(1)}, u32[]{:S(2)}) copy-start(bf16[320,512]{1,0:T(8,128)(2,1)S(1)} %constant_dynamic-update-slice_fusion.part_ref) | copy-start | bytes 983044
  8.8 30.9 %all-to-all-start = ((bf16[128,4,512]{2,1,0:T(4,128)(2,1)}), bf16[128,4,512]{2,1,0:T(4,128)(2,1)S(1)}, u32[]{:S(2)}, u32[]{:S(2)}) async-start(bf16[128,4,512]{2,1,0:T(4,128)(2,1)} %reshape.55), calls=%async_computation | async-start | bytes 1048576 | tf_op jit(solution)/shard_map/all_to_all | solution.py:337
  23.5 2.8 %copy-start.9 = (bf16[1280,512]{1,0:T(8,128)(2,1)}, bf16[1280,512]{1,0:T(8,128)(2,1)S(1)}, u32[]{:S(2)}) copy-start(bf16[1280,512]{1,0:T(8,128)(2,1)S(1)} %convolution_convert_fusion.1.recv_ref) | copy-start | bytes 3932164
  39.9 4.9 %copy-start.10 = (bf16[512,512]{1,0:T(8,128)(2,1)}, bf16[512,512]{1,0:T(8,128)(2,1)S(1)}, u32[]{:S(2)}) copy-start(bf16[512,512]{1,0:T(8,128)(2,1)S(1)} %reshape.56.mine_ref) | copy-start | bytes 1572868
  39.9 4.8 %collective-permute-start.2 = (bf16[512,512]{1,0:T(8,128)(2,1)S(1)}, bf16[512,512]{1,0:T(8,128)(2,1)S(1)}, u32[]{:S(2)}, u32[]{:S(2)}) collective-permute-start(bf16[512,512]{1,0:T(8,128)(2,1)S(1)} %reshape.56.mine_ref), channel_id=1, source_target_pairs={{0,1},{1,0},{2,3},{3,2},{4,5},{5,4},{6,7},{7,6},{8,9},{9,8},{10,11... | collective-permute-start | bytes 1572872 | tf_op jit(solution)/shard_map/ppermute | solution.py:18
  45.5 10.0 %copy-start.12 = (bf16[160,512]{1,0:T(8,128)(2,1)S(1)}, bf16[160,512]{1,0:T(8,128)(2,1)}, u32[]{:S(2)}) copy-start(bf16[160,512]{1,0:T(8,128)(2,1)} %node_cot_ref.1) | copy-start | bytes 491524
  55.3 4.2 %collective-permute-start.3 = (f32[320,512]{1,0:T(8,128)}, f32[320,512]{1,0:T(8,128)S(1)}, u32[]{:S(2)}, u32[]{:S(2)}) collective-permute-start(f32[320,512]{1,0:T(8,128)} %get-tuple-element.50.partial_ref), channel_id=1, source_target_pairs={{0,1},{1,0},{2,3},{3,2},{4,5},{5,4},{6,7},{7,6},{8,9},{9,8},{10,11... | collective-permute-start | bytes 1966088 | tf_op jit(solution)/shard_map/ppermute | solution.py:18
  55.5 2.1 %collective-permute-start.4 = (bf16[160,512]{1,0:T(8,128)(2,1)S(1)}, bf16[160,512]{1,0:T(8,128)(2,1)S(1)}, u32[]{:S(2)}, u32[]{:S(2)}) collective-permute-start(bf16[160,512]{1,0:T(8,128)(2,1)S(1)} %copy-done.12), channel_id=1, source_target_pairs={{0,1},{1,0},{2,3},{3,2},{4,5},{5,4},{6,7},{7,6},{8,9},{9,8},{10,11... | collective-permute-start | bytes 491528 | tf_op jit(solution)/shard_map/ppermute | solution.py:18
  71.3 2.2 %collective-permute-start.5 = (bf16[512,512]{1,0:T(8,128)(2,1)}, bf16[512,512]{1,0:T(8,128)(2,1)S(1)}, u32[]{:S(2)}, u32[]{:S(2)}) collective-permute-start(bf16[512,512]{1,0:T(8,128)(2,1)} %get-tuple-element.58), channel_id=1, source_target_pairs={{0,1},{1,0},{2,3},{3,2},{4,5},{5,4},{6,7},{7,6},{8,9},{9,8},{10,11... | collective-permute-start | bytes 1572872 | tf_op jit(solution)/shard_map/ppermute | solution.py:18
  75.8 24.4 %all-to-all-start.1 = ((bf16[128,4,512]{2,1,0:T(4,128)(2,1)}), bf16[128,4,512]{2,1,0:T(4,128)(2,1)S(1)}, u32[]{:S(2)}, u32[]{:S(2)}) async-start(bf16[128,4,512]{2,1,0:T(4,128)(2,1)} %reshape.57), calls=%async_computation.1 | async-start | bytes 1048576 | tf_op jit(solution)/shard_map/all_to_all | solution.py:426
  100.2 9.7 %copy-start.7 = (bf16[128,4,512]{2,1,0:T(4,128)(2,1)}, bf16[128,4,512]{2,1,0:T(4,128)(2,1)S(1)}, u32[]{:S(2)}) copy-start(bf16[128,4,512]{2,1,0:T(4,128)(2,1)S(1)} %all-to-all-done.1) | copy-start | bytes 1572868
  100.2 5.8 %collective-permute-start.6 = (bf16[1792,512]{1,0:T(8,128)(2,1)}, bf16[1792,512]{1,0:T(8,128)(2,1)S(1)}, u32[]{:S(2)}, u32[]{:S(2)}) collective-permute-start(bf16[1792,512]{1,0:T(8,128)(2,1)} %get-tuple-element.68), channel_id=1, source_target_pairs={{0,1},{1,0},{2,3},{3,2},{4,5},{5,4},{6,7},{7,6},{8,9},{9,8},{10,11... | collective-permute-start | bytes 5505032 | tf_op jit(solution)/shard_map/ppermute | solution.py:18
  109.9 3.7 %copy-start.2 = (bf16[1536,512]{1,0:T(8,128)(2,1)S(1)}, bf16[1536,512]{1,0:T(8,128)(2,1)}, u32[]{:S(2)}) copy-start(bf16[1536,512]{1,0:T(8,128)(2,1)} %w_in_ref.3) | copy-start | bytes 4718596
  109.9 17.9 %all-to-all-start.2 = ((bf16[4,448,512]{2,1,0:T(8,128)(2,1)}), bf16[4,448,512]{2,1,0:T(8,128)(2,1)S(1)}, u32[]{:S(2)}, u32[]{:S(2)}) async-start(bf16[4,448,512]{2,1,0:T(8,128)(2,1)} %bitcast.4), calls=%async_computation.2 | async-start | bytes 3670016 | tf_op jit(solution)/shard_map/all_to_all | solution.py:78
  129.0 6.8 %copy-start.3 = (f32[320,512]{1,0:T(8,128)S(1)}, f32[320,512]{1,0:T(8,128)}, u32[]{:S(2)}) copy-start(f32[320,512]{1,0:T(8,128)} %fusion.2) | copy-start | bytes 1966084
  129.0 6.8 %copy-start.5 = (f32[320,512]{1,0:T(8,128)S(1)}, f32[320,512]{1,0:T(8,128)}, u32[]{:S(2)}) copy-start(f32[320,512]{1,0:T(8,128)} %get-tuple-element.70) | copy-start | bytes 1966084
  129.0 6.8 %copy-start.6 = (f32[320,512]{1,0:T(8,128)S(1)}, f32[320,512]{1,0:T(8,128)}, u32[]{:S(2)}) copy-start(f32[320,512]{1,0:T(8,128)} %convolution_add_fusion.3) | copy-start | bytes 1966084
  131.1 21.4 %all-to-all-start.3 = ((bf16[32,14,512]{2,1,0:T(8,128)(2,1)}), bf16[32,14,512]{2,1,0:T(8,128)(2,1)}, u32[]{:S(2)}, u32[]{:S(2)}) async-start(bf16[32,14,512]{2,1,0:T(8,128)(2,1)} %reshape.59), calls=%async_computation.3 | async-start | bytes 1048576 | tf_op jit(solution)/shard_map/all_to_all | solution.py:78
  136.2 3.1 %copy-start.11 = (f32[160,512]{1,0:T(8,128)S(1)}, f32[160,512]{1,0:T(8,128)}, u32[]{:S(2)}) copy-start(f32[160,512]{1,0:T(8,128)} %get-tuple-element.72) | copy-start | bytes 983044
  136.7 2.7 %collective-permute-start.7 = (f32[160,512]{1,0:T(8,128)S(1)}, f32[160,512]{1,0:T(8,128)S(1)}, u32[]{:S(2)}, u32[]{:S(2)}) collective-permute-start(f32[160,512]{1,0:T(8,128)S(1)} %slice.22), channel_id=1, source_target_pairs={{0,1},{1,0},{2,3},{3,2},{4,5},{5,4},{6,7},{7,6},{8,9},{9,8},{10,11... | collective-permute-start | bytes 983048 | tf_op jit(solution)/shard_map/ppermute | solution.py:18
  191.6 6.9 %copy-start = (bf16[4,448,512]{2,1,0:T(8,128)(2,1)}, bf16[4,448,512]{2,1,0:T(8,128)(2,1)S(1)}, u32[]{:S(2)}) copy-start(bf16[4,448,512]{2,1,0:T(8,128)(2,1)S(1)} %all_to_all.31) | copy-start | bytes 5505028
  191.6 6.9 %collective-permute-start.8 = (bf16[1792,512]{1,0:T(8,128)(2,1)S(1)}, bf16[1792,512]{1,0:T(8,128)(2,1)}, u32[]{:S(2)}, u32[]{:S(2)}) collective-permute-start(bf16[1792,512]{1,0:T(8,128)(2,1)S(1)} %bitcast.12), channel_id=1, source_target_pairs={{0,1},{1,0},{2,3},{3,2},{4,5},{5,4},{6,7},{7,6},{8,9},{9,8},{10,11... | collective-permute-start | bytes 5505032 | tf_op jit(solution)/shard_map/ppermute | solution.py:18
  (5 other events, 7.6 us)

commit v3 on v2

--- a/solution.py
+++ b/solution.py
@@ -64,14 +64,17 @@
     def device(y, z, x, r):
         return ((y * nz + z) * nx + x) * 2 + r
 
-    near = [[device(y, z, x, 0) for x in range(nx)] for y in range(ny) for z in range(nz)]
-    near += [[device(y, z, x, 1) for y in range(ny)] for x in range(nx) for z in range(nz)]
-    far = [[device(y, z, x, 0) for y in range(ny) for z in range(nz)] for x in range(nx)]
-    far += [[device(y, z, x, 1) for x in range(nx) for z in range(nz)] for y in range(ny)]
-    return near, far
-
-
-NEAR, FAR = groups((4, 8, 4))
+    def along_x(r):
+        return [[device(y, z, x, r) for x in range(nx)] for y in range(ny) for z in range(nz)]
+
+    def along_y(r):
+        return [[device(y, z, x, r) for y in range(ny)] for x in range(nx) for z in range(nz)]
+
+    last = [[device(y, z, x, r) for z in range(nz)] for y in range(ny) for x in range(nx) for r in range(2)]
+    return along_x(0) + along_y(1), along_y(0) + along_x(1), last
+
+
+STAGES = groups((4, 8, 4))
 
 
 def exchange(array, stage):
@@ -90,58 +93,75 @@
     return blocks.reshape(count * value.shape[0], value.shape[1])
 
 
-def reduced(kept, sent, core):
-    value = (kept + swapped(sent).astype(f32)).astype(bf16)
-    return summed(summed(value, NEAR), FAR)
+def reduced(value):
+    for stage in STAGES:
+        value = summed(value, stage)
+    return value
 
 
 def spread(value, core):
-    value = gathered(gathered(value, FAR), NEAR)
+    for stage in STAGES[::-1]:
+        value = gathered(value, stage)
     width = value.shape[1]
-    return assemble(value, swapped(value), core, [3 * width, width, 2 * width, width])
-
-
-def assemble_kernel(sizes, core_ref, mine_ref, got_ref, *refs):
-    outs, sems = refs[:-1], refs[-1]
+    sizes = [3 * width, width, 2 * width, width]
+    return place(swapped(value), 1 - core, sizes, place(value, core, sizes))
+
+
+def place_kernel(sizes, core_ref, half_ref, *refs):
+    outs, sems = refs[-1 - len(sizes) : -1], refs[-1]
     core = core_ref[0]
     copies = []
-    start = 0
-    half = mine_ref.shape[1] // 2
-    for k, rows in enumerate(sizes):
+    half = half_ref.shape[1] // 2
+    for out, rows in zip(outs, sizes):
         for block in range(rows // (2 * half)):
-            for source, place in ((mine_ref, core), (got_ref, 1 - core)):
-                row = pl.multiple_of(block * 2 * half + place * half, half)
-                copies.append(
-                    pltpu.make_async_copy(
-                        source.at[pl.ds(start, half), :],
-                        outs[k].at[pl.ds(row, half), :],
-                        sems.at[len(copies)],
-                    )
+            start = len(copies) * half
+            row = pl.multiple_of(block * 2 * half + core * half, half)
+            copies.append(
+                pltpu.make_async_copy(
+                    half_ref.at[pl.ds(start, half), :],
+                    out.at[pl.ds(row, half), :],
+                    sems.at[len(copies)],
                 )
-            start += half
+            )
     for copy in copies:
         copy.start()
     for copy in copies:
         copy.wait()
 
 
-def assemble(mine, got, core, sizes):
+def place(half, core, sizes, outs=()):
+    blocks = sum(sizes) // half.shape[1]
+    anywhere = pl.BlockSpec(memory_space=pl.ANY)
     return pl.pallas_call(
-        functools.partial(assemble_kernel, sizes),
-        out_shape=[jax.ShapeDtypeStruct((rows, mine.shape[1]), mine.dtype) for rows in sizes],
-        in_specs=[pl.BlockSpec(memory_space=pltpu.SMEM)]
-        + [pl.BlockSpec(memory_space=pltpu.VMEM)] * 2,
-        out_specs=[pl.BlockSpec(memory_space=pl.ANY)] * len(sizes),
-        scratch_shapes=[pltpu.SemaphoreType.DMA((14,))],
-        name="assemble",
-    )(core.astype(jnp.int32).reshape(1), mine, got)
-
-
-CHUNK = 1280
+        functools.partial(place_kernel, sizes),
+        out_shape=[jax.ShapeDtypeStruct((rows, half.shape[1]), half.dtype) for rows in sizes],
+        in_specs=[pl.BlockSpec(memory_space=pltpu.SMEM), pl.BlockSpec(memory_space=pltpu.VMEM)]
+        + [anywhere] * len(outs),
+        out_specs=[anywhere] * len(sizes),
+        scratch_shapes=[pltpu.SemaphoreType.DMA((blocks,))],
+        input_output_aliases={2 + k: k for k in range(len(outs))},
+        name="place",
+    )(core.astype(jnp.int32).reshape(1), half, *outs)
 
 
 def by_lane(index, count):
     return (index == lax.broadcasted_iota(jnp.int32, (index.shape[0], count), 1)).astype(bf16)
+
+
+LANES = 128
+
+
+def column(square_ref, count):
+    turned = jnp.transpose(square_ref[...])
+    return jnp.concatenate([turned[:, k : k + 1] for k in range(count // LANES)], 0)
+
+
+def line(square_ref, count):
+    return jnp.concatenate([square_ref[k : k + 1] for k in range(count // LANES)], 1)
+
+
+def in_square(index):
+    return jnp.pad(index.reshape(-1, LANES), ((0, LANES - index.shape[0] // LANES), (0, 0)))
 
 
 def by_row(index, count):
@@ -158,51 +178,36 @@
     return value * sigmoid_v, sigmoid_v * (1.0 + value * (1.0 - sigmoid_v))
 
 
-def each_chunk(count, body):
-    def step(i, carry):
-        body(pl.ds(pl.multiple_of(i * CHUNK, CHUNK), CHUNK))
-        return carry
-
-    lax.fori_loop(0, count // CHUNK, step, 0)
-
-
 def forward_kernel(
-    known_ref, local_ref, send_col_ref, recv_row_ref, mine_ref, theirs_ref, w_in_ref, w_out_ref, gain_ref,
-    offset_ref, send_ref, slope_ref, hidden_ref, normed_ref, inverse_ref, totals_ref, high_ref, low_ref,
-    table_ref,
+    known_ref, local_ref, sender_ref, receiver_ref, mine_ref, theirs_ref, w_in_ref, w_out_ref, gain_ref,
+    offset_ref, send_ref, slope_ref, hidden_ref, normed_ref, inverse_ref, totals_ref, table_ref,
 ):
-    width = known_ref.shape[1]
+    edges, width = known_ref.shape
     ghosts = mine_ref.shape[0]
     table_ref[:ghosts] = mine_ref[...]
     table_ref[ghosts:] = theirs_ref[...]
     count = totals_ref.shape[0]
-
-    def body(at):
-        index = send_col_ref[at] - count
-        rows = mat_mul(by_lane(index, 2 * ghosts), table_ref[...])
-        send_rows = (local_ref[at].astype(f32) + rows).astype(bf16)
-        send_ref[at] = send_rows
-        pre_act = known_ref[at] + mat_mul(send_rows, w_in_ref[width : 2 * width])
-        hidden, slope = silu_parts(pre_act)
-        slope_ref[at] = slope
-        hidden = hidden.astype(bf16)
-        hidden_ref[at] = hidden
-        normed, inverse = norm_forward(mat_mul(hidden, w_out_ref[...]))
-        normed_ref[at] = normed
-        inverse_ref[at] = jnp.broadcast_to(inverse, (CHUNK, inverse_ref.shape[1]))
-        high, low = in_two(normed * gain_ref[...] + offset_ref[...])
-        high_ref[at] = high
-        low_ref[at] = low
-
-    each_chunk(known_ref.shape[0], body)
-    pick = by_row(recv_row_ref[...], count)
-    totals_ref[...] = mat_mul(pick, high_ref[...]) + mat_mul(pick, low_ref[...])
+    index = column(sender_ref, edges) - count
+    rows = mat_mul(by_lane(index, 2 * ghosts), table_ref[...])
+    send_rows = (local_ref[...].astype(f32) + rows).astype(bf16)
+    send_ref[...] = send_rows
+    pre_act = known_ref[...] + mat_mul(send_rows, w_in_ref[width : 2 * width])
+    hidden, slope = silu_parts(pre_act)
+    slope_ref[...] = slope
+    hidden = hidden.astype(bf16)
+    hidden_ref[...] = hidden
+    normed, inverse = norm_forward(mat_mul(hidden, w_out_ref[...]))
+    normed_ref[...] = normed
+    inverse_ref[...] = jnp.broadcast_to(inverse, inverse_ref.shape)
+    high, low = in_two(normed * gain_ref[...] + offset_ref[...])
+    pick = by_row(line(receiver_ref, edges), count)
+    totals_ref[...] = mat_mul(pick, high) + mat_mul(pick, low)
 
 
 def backward_kernel(
     partial_ref, other_ref, part_ref, node_cot_ref, w_node_in_ref, w_node_out_ref, node_gain_ref,
     cot_ref, slope_ref, normed_ref, inverse_ref,
-    recv_col_ref, send_row_ref, w_out_ref, gain_ref,
+    receiver_ref, sender_ref, w_out_ref, gain_ref,
     theirs_ref, mine_ref, grad_act_ref, grad_out_ref,
     totals_ref, node_hidden_ref, node_act_ref, node_out_ref,
     totals_grad_ref,
@@ -230,29 +235,28 @@
     node_act_ref[...] = grad_act[:own]
     node_out_ref[...] = grad_out[:own]
 
-    def body(at):
-        message_grad = cot_ref[at].astype(f32) + mat_mul(
-            by_lane(recv_col_ref[at], rows), totals_grad_ref[...]
-        )
-        grad_out = norm_backward(
-            message_grad * gain_ref[...], normed_ref[at], inverse_ref[at][:, :1]
-        ).astype(bf16)
-        grad_out_ref[at] = grad_out
-        grad_act_ref[at] = (mat_nt(grad_out, w_out_ref[...]) * slope_ref[at]).astype(bf16)
-
-    each_chunk(cot_ref.shape[0], body)
-    index = send_row_ref[...]
+    edges = cot_ref.shape[0]
+    message_grad = cot_ref[...].astype(f32) + mat_mul(
+        by_lane(column(receiver_ref, edges), rows), totals_grad_ref[...]
+    )
+    grad_out = norm_backward(
+        message_grad * gain_ref[...], normed_ref[...], inverse_ref[:, :1]
+    ).astype(bf16)
+    grad_out_ref[...] = grad_out
+    grad_act_ref[...] = (mat_nt(grad_out, w_out_ref[...]) * slope_ref[...]).astype(bf16)
+    index = line(sender_ref, edges)
     theirs_ref[...] = mat_mul(by_row(index - rows - ghosts, ghosts), grad_act_ref[...]).astype(bf16)
     mine_ref[...] = mat_mul(by_row(index - rows, ghosts), grad_act_ref[...])
 
 
 def weights_kernel(
     core_ref, edge_ref, send_ref, recv_ref, hidden_ref, part_ref, totals_ref, node_hidden_ref,
-    grad_act_ref, grad_out_ref, node_act_ref, node_out_ref, cot_ref, w_in_ref,
-    recv_row_ref, send_row_ref, node_cot_ref, w_node_in_ref,
-    kept_ref, sent_ref, grad_edge_ref, local_ref, recv_sum_ref, direct_ref, block_ref,
-    *, edge_scale, node_scale,
+    grad_act_ref, grad_out_ref, node_act_ref, node_out_ref,
+    receiver_ref, sender_ref, node_cot_ref, w_node_in_ref,
+    kept_ref, local_ref, recv_sum_ref, direct_ref, *sent_refs_and_block,
+    edge_scale, node_scale,
 ):
+    *sent_refs, block_ref = sent_refs_and_block
     width = edge_ref.shape[1]
     half = width // 2
     core = core_ref[0]
@@ -270,19 +274,29 @@
         block_ref[...] = mat_tn(left, right) * scale
         mine = block_ref[pl.ds(pl.multiple_of(core * half, half), half), :]
         other = block_ref[pl.ds(pl.multiple_of((1 - core) * half, half), half), :]
-        kept_ref[k * half : (k + 1) * half] = mine
-        sent_ref[k * half : (k + 1) * half] = other.astype(bf16)
-
-    def body(at):
-        grad_edge_ref[at] = (
-            cot_ref[at].astype(f32) + mat_nt(grad_act_ref[at], w_in_ref[:width])
-        ).astype(bf16)
-
-    each_chunk(cot_ref.shape[0], body)
-    rows = part_ref.shape[0]
-    local_ref[...] = mat_mul(by_row(send_row_ref[...], rows), grad_act_ref[...])
-    recv_sum_ref[...] = mat_mul(by_row(recv_row_ref[...], rows), grad_act_ref[...])
+        kept_ref[k * half : (k + 1) * half] = mine.astype(bf16)
+        other = other.astype(bf16)
+        size = sent_refs[0].shape[0]
+        start = k * half
+        while start < (k + 1) * half:
+            stop = min((start // size + 1) * size, (k + 1) * half)
+            sent_refs[start // size][start % size : start % size + stop - start] = other[
+                start - k * half : stop - k * half
+            ]
+            start = stop
+
+    rows, edges = part_ref.shape[0], edge_ref.shape[0]
+    local_ref[...] = mat_mul(by_row(line(sender_ref, edges), rows), grad_act_ref[...])
+    recv_sum_ref[...] = mat_mul(by_row(line(receiver_ref, edges), rows), grad_act_ref[...])
     direct_ref[...] = mat_nt(node_act_ref[...], w_node_in_ref[:width]) + node_cot_ref[...].astype(f32)
+
+
+def pair_kernel(kept_ref, *refs):
+    *got_refs, out_ref = refs
+    rows = got_refs[0].shape[0]
+    for k, got_ref in enumerate(got_refs):
+        at = slice(k * rows, (k + 1) * rows)
+        out_ref[at] = (kept_ref[at].astype(f32) + got_ref[...].astype(f32)).astype(bf16)
 
 
 def run(kernel, name, arguments, results, scratch=(), scalars=0, flops=0):
@@ -333,8 +347,9 @@
     partition = jnp.concatenate([node_latent, swapped(node_latent)], 0)
     lists = lax.dynamic_slice_in_dim(ghost_rows[0], core * slots, slots, 1).reshape(-1)
     pick_ghost = one_hot(local_row(lists), rows)
-    outgoing = mat_mul(pick_ghost, partition).astype(bf16)
-    arrived = lax.all_to_all(outgoing.reshape(parts, slots, width), "nodes", 0, 0, tiled=True)
+    outgoing = mat_mul(pick_ghost, partition).astype(bf16).reshape(parts, slots, width)
+    outgoing, senders, receivers = lax.optimization_barrier((outgoing, senders, receivers))
+    arrived = lax.all_to_all(outgoing, "nodes", 0, 0, tiled=True)
 
     edge_latent = swapped(edge_saved)
     node_cots = jnp.concatenate([node_cot, swapped(node_cot)], 0)
@@ -347,16 +362,17 @@
         rows + side * ghosts + (slot >> 3) * slots + (slot & (slots - 1)),
         local_row(senders),
     )
-    recv_col, send_col = receiver[:, None], sender[:, None]
-    recv_row, send_row = receiver[None], sender[None]
+    sender_square, receiver_square = in_square(sender), in_square(receiver)
     square = 2 * edges * width * width
     pick_recv = one_hot(receiver, rows)
     pick_local = one_hot(jnp.where(slot >= 0, -1, sender), rows)
     recv_rows = mat_mul(pick_recv, partition).astype(bf16)
     local_rows = mat_mul(pick_local, partition).astype(bf16)
     known = mat_mul(edge_latent, w_edge_in[:width]) + mat_mul(recv_rows, w_edge_in[2 * width :])
-    arrived, known, local_rows, recv_rows, recv_col, send_col = lax.optimization_barrier(
-        (arrived, known, local_rows, recv_rows, recv_col, send_col)
+    (
+        arrived, known, local_rows, recv_rows, sender_square, receiver_square, node_cots
+    ) = lax.optimization_barrier(
+        (arrived, known, local_rows, recv_rows, sender_square, receiver_square, node_cots)
     )
     arrived = arrived.reshape(ghosts, width)
     send_rows, edge_slope, edge_hidden, edge_normed, edge_inverse, partial = run(
@@ -365,8 +381,8 @@
         [
             known,
             local_rows,
-            send_col,
-            recv_row,
+            sender_square,
+            receiver_square,
             arrived,
             swapped(arrived),
             w_edge_in,
@@ -382,7 +398,7 @@
             ((edges, 128), f32),
             ((rows, width), f32),
         ],
-        [pltpu.VMEM((edges, width), bf16)] * 2 + [pltpu.VMEM((2 * ghosts, width), bf16)],
+        [pltpu.VMEM((2 * ghosts, width), bf16)],
         flops=6 * square,
     )
     device_count = lax.axis_size("nodes") * lax.axis_size("rep")
@@ -406,8 +422,8 @@
             edge_slope,
             edge_normed,
             edge_inverse,
-            recv_col,
-            send_row,
+            receiver_square,
+            sender_square,
             w_edge_out,
             edge_gain[None],
         ],
@@ -425,7 +441,7 @@
     paired, grad_act = lax.optimization_barrier((paired, grad_act))
     returned = lax.all_to_all(paired.reshape(parts, slots, width), "nodes", 0, 0, tiled=True)
 
-    kept, sent, grad_edges, local_sum, recv_sum, direct_grad = run(
+    kept, local_sum, recv_sum, direct_grad, *sent = run(
         functools.partial(weights_kernel, edge_scale=edge_scale, node_scale=node_scale),
         "weights",
         [
@@ -441,23 +457,25 @@
             grad_out,
             node_act,
             node_out,
-            edge_cot,
-            w_edge_in,
-            recv_row,
-            send_row,
+            receiver_square,
+            sender_square,
             node_cot,
             w_node_in,
         ],
-        [((7 * width // 2, width), f32), ((7 * width // 2, width), bf16), ((edges, width), bf16)]
+        [((7 * width // 2, width), bf16)]
         + [((rows, width), f32)] * 2
-        + [((own, width), f32)],
+        + [((own, width), f32)]
+        + [((7 * width // 8, width), bf16)] * 4,
         [pltpu.VMEM((width, width), f32)],
         scalars=1,
         flops=6 * square,
     )
 
-    kept, sent, returned = lax.optimization_barrier((kept, sent, returned))
-    value = reduced(kept, sent, core)
+    got = [swapped(block) for block in sent]
+    kept, got, returned = lax.optimization_barrier((kept, got, returned))
+    value = reduced(
+        run(pair_kernel, "pair", [kept, *got], [(kept.shape, bf16)], flops=kept.size)[0]
+    )
     send_high, send_low = split_two(local_sum + mat_tn(pick_ghost, returned.reshape(ghosts, width)))
     recv_high, recv_low = split_two(recv_sum)
     a2, a3 = w_edge_in[width : 2 * width], w_edge_in[2 * width :]
@@ -467,7 +485,8 @@
     own_grad = row_grad[:own] + swapped(row_grad[own:])
     grad_nodes = (own_grad + direct_grad).astype(bf16)
 
-    value, grad_nodes = lax.optimization_barrier((value, grad_nodes))
+    grad_edges = (edge_cot.astype(f32) + mat_nt(grad_act, w_edge_in[:width])).astype(bf16)
+    value, grad_nodes, grad_edges = lax.optimization_barrier((value, grad_nodes, grad_edges))
     total = spread(value, core)
     return (grad_nodes, grad_edges, *total)
 

time: 204 us -> 196 us (0.961)
  waiting for transfers between devices: 47.7 us -> 31.8 us
  starting transfers between devices: 43.5 us -> 51.2 us
  matrix products: 12.4 us -> 18.2 us
  other arithmetic: 11.2 us -> 5.81 us
  Pallas kernels: 36.5 us -> 39.8 us
  local copies, waits for them, and re-layouts: 12.6 us -> 9.82 us
    all_to_all x2 -> x3, waiting for transfers between devices: 19.5 us -> 11 us  [exchange(): lax.all_to_all(array, ('nodes', 'rep'), 0, 0, tiled=True, axis_index_grou...]
    dot_general x4 -> x5, matrix products: 3.48 us -> 8.99 us  [mat_nt(): lax.dot_general(left, right, (((1,), (1,)), ((), ())), preferred_element_...]
    ppermute x9 -> x12, starting transfers between devices: 14.3 us -> 19.6 us  [swapped(): return lax.ppermute(array, 'rep', pairs)]
    convert_element_type x1 -> x0, other arithmetic: 3.93 us -> none  [reduced(): value = (kept + swapped(sent).astype(f32)).astype(bf16)]
    all_to_all x1, waiting for transfers between devices: 11 us -> 7.94 us  [shards(): arrived = lax.all_to_all(outgoing, 'nodes', 0, 0, tiled=True)]
    all_to_all x1, waiting for transfers between devices: 5.64 us -> 3.12 us  [shards(): lax.all_to_all(paired.reshape(parts, slots, width), 'nodes', 0, 0, tiled=...]
    all_to_all x2 -> x3, starting transfers between devices: 8.41 us -> 10.9 us  [exchange(): lax.all_to_all(array, ('nodes', 'rep'), 0, 0, tiled=True, axis_index_grou...]
    optimization_barrier x2 -> x0, local copies, waits for them, and re-layouts: 2.21 us -> none  [shards(): lax.optimization_barrier((arrived, known, local_rows, recv_rows, recv_col...]
  transfers between devices with their start and end apart: 13 -> 17, of which waited for: 9 -> 13; matrix products, arithmetic and copies ran while one was open for 12% -> 14% of each run, Pallas kernels for 6% -> 6%
where the time goes in v3:
time: 196 us; the launch traced here: 195 us
  starting transfers between devices  51.2 us (26%)
  Pallas kernels  39.8 us (20%)
  blocking collectives  37.2 us (19%)
  waiting for transfers between devices  31.8 us (16%)
  matrix products  18.2 us (9%)
  local copies, waits for them, and re-layouts  9.82 us (5%)
  other arithmetic  5.81 us (3%)
    all_to_all x3, blocking collectives, exchange(): lax.all_to_all(array, ('nodes', 'rep'), 0, 0, tiled=True, axis_index_grou...  37.2 us
    pallas_call x4, Pallas kernels, run(): pl.pallas_call(kernel, in_specs=[pl.BlockSpec(memory_space=pltpu.SMEM)] *...  34.2 us
    ppermute x12, starting transfers between devices, swapped(): return lax.ppermute(array, 'rep', pairs)  19.6 us
    all_to_all x1, starting transfers between devices, shards(): arrived = lax.all_to_all(outgoing, 'nodes', 0, 0, tiled=True)  13.9 us
    all_to_all x3, waiting for transfers between devices, exchange(): lax.all_to_all(array, ('nodes', 'rep'), 0, 0, tiled=True, axis_index_grou...  11 us
    all_to_all x3, starting transfers between devices, exchange(): lax.all_to_all(array, ('nodes', 'rep'), 0, 0, tiled=True, axis_index_grou...  10.9 us
    ppermute x12, waiting for transfers between devices, swapped(): return lax.ppermute(array, 'rep', pairs)  9.72 us
    dot_general x5, matrix products, mat_nt(): lax.dot_general(left, right, (((1,), (1,)), ((), ())), preferred_element_...  8.99 us
  transfers between devices with their start and end apart: 17, of which 13 were waited for; matrix products, arithmetic and copies ran while one was open for 14% of the time, Pallas kernels for 6%

profile of v3, /device:TPU:1, one launch (start us, length us, event | category | flops | bytes accessed | tf_op | source)
XLA Modules:
  0.0 195.0 jit_solution(1169505530063184420)
XLA Ops:
  0.6 3.3 %collective-permute-start = (bf16[1280,512]{1,0:T(8,128)(2,1)}, bf16[1280,512]{1,0:T(8,128)(2,1)S(1)}, u32[]{:S(2)}, u32[]{:S(2)}) collective-permute-start(bf16[1280,512]{1,0:T(8,128)(2,1)} %param.15), channel_id=1, source_target_pairs={{0,1},{1,0},{2,3},{3,2},{4,5},{5,4},{6,7},{7,6},{8,9},{9,8},{10,11... | collective-permute-start | bytes 3932168 | tf_op jit(solution)/shard_map/ppermute | solution.py:18
  8.6 13.9 %all-to-all-start = ((bf16[128,4,512]{2,1,0:T(4,128)(2,1)}), bf16[128,4,512]{2,1,0:T(4,128)(2,1)S(1)}, u32[]{:S(2)}, u32[]{:S(2)}) async-start(bf16[128,4,512]{2,1,0:T(4,128)(2,1)} %reshape.68), calls=%async_computation | async-start | bytes 1048576 | tf_op jit(solution)/shard_map/all_to_all | solution.py:352
  29.3 2.4 %convolution_add_fusion.1.known_ref = f32[1280,512]{1,0:T(8,128)} fusion(f32[1280,512]{1,0:T(8,128)S(1)} %fusion.13, bf16[1280,512]{1,0:T(8,128)(2,1)S(1)} %collective-permute-done.edge_ref, bf16[1536,512]{1,0:T(8,128)(2,1)S(1)} %copy-done.1), kind=kOutput, calls=%fused_computation.1 | convolution fusion | flops 671744000 | bytes 7077888 | tf_op jit(solution)/shard_map/dot_general | solution.py:22
  31.7 7.9 %all-to-all-done = bf16[128,4,512]{2,1,0:T(4,128)(2,1)S(1)} async-done(((bf16[128,4,512]{2,1,0:T(4,128)(2,1)}), bf16[128,4,512]{2,1,0:T(4,128)(2,1)S(1)}, u32[]{:S(2)}, u32[]{:S(2)}) %all-to-all-start) | async-done | bytes 524320 | tf_op jit(solution)/shard_map/all_to_all | solution.py:352
  39.8 3.3 %collective-permute-start.3 = (bf16[512,512]{1,0:T(8,128)(2,1)S(1)}, bf16[512,512]{1,0:T(8,128)(2,1)S(1)}, u32[]{:S(2)}, u32[]{:S(2)}) collective-permute-start(bf16[512,512]{1,0:T(8,128)(2,1)S(1)} %reshape.71.mine_ref), channel_id=1, source_target_pairs={{0,1},{1,0},{2,3},{3,2},{4,5},{5,4},{6,7},{7,6},{8,9},{9,8},{10,11... | collective-permute-start | bytes 1572872 | tf_op jit(solution)/shard_map/ppermute | solution.py:18
  45.4 10.0 %forward.1 = (bf16[1280,512]{1,0:T(8,128)(2,1)}, f32[1280,512]{1,0:T(8,128)}, bf16[1280,512]{1,0:T(8,128)(2,1)}, f32[1280,512]{1,0:T(8,128)}, f32[1280,128]{1,0:T(8,128)}, /*index=5*/f32[320,512]{1,0:T(8,128)}) custom-call(f32[1280,512]{1,0:T(8,128)} %convolution_add_fusion.1.known_ref, bf16[1280,512]{1,0:T(8,128)(2,1)} %convolution_convert_fusion.local_ref, ...), custom_call_target="tpu_custom_call" | custom-call | flops 4026531840 | bytes 8388608 | tf_op jit(solution)/shard_map/forward/pallas_call | solution.py:304
  58.5 10.8 %backward.1 = (bf16[512,512]{1,0:T(8,128)(2,1)}, f32[512,512]{1,0:T(8,128)}, bf16[1280,512]{1,0:T(8,128)(2,1)}, bf16[1280,512]{1,0:T(8,128)(2,1)}, bf16[160,512]...) custom-call(f32[320,512]{1,0:T(8,128)} %get-tuple-element.68.partial_ref, ...), custom_call_target="tpu_custom_call" | custom-call | flops 5368709120 | bytes 8388608 | tf_op jit(solution)/shard_map/backward/pallas_call | solution.py:304
  73.8 6.8 %all-to-all-start.1 = ((bf16[128,4,512]{2,1,0:T(4,128)(2,1)}), bf16[128,4,512]{2,1,0:T(4,128)(2,1)S(1)}, u32[]{:S(2)}, u32[]{:S(2)}) async-start(bf16[128,4,512]{2,1,0:T(4,128)(2,1)} %reshape.72), calls=%async_computation.1 | async-start | bytes 1048576 | tf_op jit(solution)/shard_map/all_to_all | solution.py:442
  80.6 9.7 %weights.1 = (bf16[1792,512]{1,0:T(8,128)(2,1)}, f32[320,512]{1,0:T(8,128)}, f32[320,512]{1,0:T(8,128)}, f32[160,512]{1,0:T(8,128)}, bf16[448,512]{1,0:T(8,128)(...) custom-call(s32[1]{0:T(128)} %bitcast.core_ref, bf16[1280,512]{1,0:T(8,128)(2,1)} %copy-done.7, ...), custom_call_target="tpu_custom_call" | custom-call | flops 4026531840 | bytes 8388608 | tf_op jit(solution)/shard_map/weights/pallas_call | solution.py:304
  94.7 3.1 %all-to-all-done.1 = bf16[128,4,512]{2,1,0:T(4,128)(2,1)S(1)} async-done(((bf16[128,4,512]{2,1,0:T(4,128)(2,1)}), bf16[128,4,512]{2,1,0:T(4,128)(2,1)S(1)}, u32[]{:S(2)}, u32[]{:S(2)}) %all-to-all-start.1) | async-done | bytes 524320 | tf_op jit(solution)/shard_map/all_to_all | solution.py:442
  97.8 3.8 %pair.1 = bf16[1792,512]{1,0:T(8,128)(2,1)} custom-call(bf16[1792,512]{1,0:T(8,128)(2,1)} %get-tuple-element.88.kept_ref, bf16[448,512]{1,0:T(8,128)(2,1)} %copy-done.10, bf16[448,512]{1,0:T(8,128)(2,1)} %copy-done.11, bf16[448,512]{1,0:T(8,128)(2,1)} %copy-done.12, bf16[448,512]{1,0:T(8,128)(2,1)} %copy-done.13), custom_call_target="tpu_custom_call" | custom-call | flops 917504 | bytes 8388608 | tf_op jit(solution)/shard_map/pair/pallas_call | solution.py:304
  101.6 3.7 %all-to-all-start.2 = ((bf16[4,448,512]{2,1,0:T(8,128)(2,1)}), bf16[4,448,512]{2,1,0:T(8,128)(2,1)S(1)}, u32[]{:S(2)}, u32[]{:S(2)}) async-start(bf16[4,448,512]{2,1,0:T(8,128)(2,1)} %bitcast.22), calls=%async_computation.2 | async-start | bytes 3670016 | tf_op jit(solution)/shard_map/all_to_all | solution.py:81
  112.6 2.3 %convolution_add_fusion.3 = f32[320,512]{1,0:T(8,128)} fusion(f32[320,512]{1,0:T(8,128)} %convolution_add_fusion.4, bf16[1536,512]{1,0:T(8,128)(2,1)S(1)} %copy-done.2, f32[320,512]{1,0:T(8,128)S(1)} %copy-done.5, f32[320,512]{1,0:T(8,128)S(1)} %fusion.3), kind=kOutput, calls=%fused_computation.9 | convolution fusion | flops 168427520 | bytes 3145728 | tf_op jit(solution)/shard_map/dot_general | solution.py:30
  114.9 4.7 %all-to-all-done.2 = bf16[4,448,512]{2,1,0:T(8,128)(2,1)S(1)} async-done(((bf16[4,448,512]{2,1,0:T(8,128)(2,1)}), bf16[4,448,512]{2,1,0:T(8,128)(2,1)S(1)}, u32[]{:S(2)}, u32[]{:S(2)}) %all-to-all-start.2) | async-done | bytes 1835040 | tf_op jit(solution)/shard_map/all_to_all | solution.py:81
  120.7 3.5 %all-to-all-start.3 = ((bf16[4,112,512]{2,1,0:T(8,128)(2,1)}), bf16[4,112,512]{2,1,0:T(8,128)(2,1)S(1)}, u32[]{:S(2)}, u32[]{:S(2)}) async-start(bf16[4,112,512]{2,1,0:T(8,128)(2,1)} %bitcast.23), calls=%async_computation.3 | async-start | bytes 917504 | tf_op jit(solution)/shard_map/all_to_all | solution.py:81
  126.3 3.9 %collective-permute-start.10 = (f32[160,512]{1,0:T(8,128)S(1)}, f32[160,512]{1,0:T(8,128)}, u32[]{:S(2)}, u32[]{:S(2)}) collective-permute-start(f32[160,512]{1,0:T(8,128)S(1)} %slice.23), channel_id=1, source_target_pairs={{0,1},{1,0},{2,3},{3,2},{4,5},{5,4},{6,7},{7,6},{8,9},{9,8},{10,11... | collective-permute-start | bytes 983048 | tf_op jit(solution)/shard_map/ppermute | solution.py:18
  132.9 3.7 %all-to-all-start.4 = ((bf16[8,14,512]{2,1,0:T(8,128)(2,1)}), bf16[8,14,512]{2,1,0:T(8,128)(2,1)S(1)}, u32[]{:S(2)}, u32[]{:S(2)}) async-start(bf16[8,14,512]{2,1,0:T(8,128)(2,1)} %reshape.75), calls=%async_computation.4 | async-start | bytes 262144 | tf_op jit(solution)/shard_map/all_to_all | solution.py:81
  138.3 6.3 %all-to-all-done.4 = bf16[8,14,512]{2,1,0:T(8,128)(2,1)S(1)} async-done(((bf16[8,14,512]{2,1,0:T(8,128)(2,1)}), bf16[8,14,512]{2,1,0:T(8,128)(2,1)S(1)}, u32[]{:S(2)}, u32[]{:S(2)}) %all-to-all-start.4) | async-done | bytes 114720 | tf_op jit(solution)/shard_map/all_to_all | solution.py:81
  144.7 10.3 %all_to_all.40 = bf16[8,14,512]{2,1,0:T(8,128)(2,1)S(1)} all-to-all(bf16[8,14,512]{2,1,0:T(8,128)(2,1)S(1)} %broadcast_in_dim.41), channel_id=1, replica_groups={{0,8,16,24,32,40,48,56},{1,9,17,25,33,41,49,57},{2,10,18,26,34,42,50,58..., dimensions={0} | all-to-all | bytes 229376 | tf_op jit(solution)/shard_map/all_to_all | solution.py:81
  155.1 9.0 %all_to_all.41 = bf16[4,112,512]{2,1,0:T(8,128)(2,1)S(1)} all-to-all(bf16[4,112,512]{2,1,0:T(8,128)(2,1)S(1)} %broadcast_in_dim.43), channel_id=1, replica_groups={{0,64,128,192},{8,72,136,200},{16,80,144,208},{24,88,152,216},{32,96,16..., dimensions={0} | all-to-all | bytes 917504 | tf_op jit(solution)/shard_map/all_to_all | solution.py:81
  164.2 18.0 %all_to_all.42 = bf16[4,448,512]{2,1,0:T(8,128)(2,1)S(1)} all-to-all(bf16[4,448,512]{2,1,0:T(8,128)(2,1)S(1)} %broadcast_in_dim.45), channel_id=1, replica_groups={{0,2,4,6},{8,10,12,14},{16,18,20,22},{24,26,28,30},{32,34,36,38},{40,42..., dimensions={0} | all-to-all | bytes 3670016 | tf_op jit(solution)/shard_map/all_to_all | solution.py:81
  182.2 6.3 %collective-permute-start.11 = (bf16[1792,512]{1,0:T(8,128)(2,1)S(1)}, bf16[1792,512]{1,0:T(8,128)(2,1)}, u32[]{:S(2)}, u32[]{:S(2)}) collective-permute-start(bf16[1792,512]{1,0:T(8,128)(2,1)S(1)} %bitcast.20), channel_id=1, source_target_pairs={{0,1},{1,0},{2,3},{3,2},{4,5},{5,4},{6,7},{7,6},{8,9},{9,8},{10,11... | collective-permute-start | bytes 5505032 | tf_op jit(solution)/shard_map/ppermute | solution.py:18
  188.5 2.8 %place.2 = (bf16[1536,512]{1,0:T(8,128)(2,1)}, bf16[512,512]{1,0:T(8,128)(2,1)}, bf16[1024,512]{1,0:T(8,128)(2,1)}, bf16[512,512]{1,0:T(8,128)(2,1)}) custom-call(s32[1]{0:T(128)} %bitcast.core_ref, bf16[1792,512]{1,0:T(8,128)(2,1)} %bitcast.21), custom_call_target="tpu_custom_call" | custom-call | tf_op jit(solution)/shard_map/place/pallas_call | solution.py:135
  192.0 2.8 %place.3 = (bf16[1536,512]{1,0:T(8,128)(2,1)}, bf16[512,512]{1,0:T(8,128)(2,1)}, bf16[1024,512]{1,0:T(8,128)(2,1)}, bf16[512,512]{1,0:T(8,128)(2,1)}) custom-call(s32[1]{0:T(128)} %bitcast.8.core_ref, bf16[1792,512]{1,0:T(8,128)(2,1)} %collective-permute-done.11.half_ref, ...), custom_call_target="tpu_custom_call", output_to_operand_aliasing={{0}: (2, {}), {1}: (3, {}), {2}: (4, {}), {3}: (5, {})} | custom-call | tf_op jit(solution)/shard_map/place/pallas_call | solution.py:135
  (105 shorter events, 41.6 us)
Async XLA Ops:
  0.6 7.9 %copy-start.18 = (s32[1280]{0:T(1024)S(1)}, s32[1280]{0:T(1024)}, u32[]{:S(2)}) copy-start(s32[1280]{0:T(1024)} %param.19) | copy-start | bytes 15364
  0.6 28.7 %collective-permute-start = (bf16[1280,512]{1,0:T(8,128)(2,1)}, bf16[1280,512]{1,0:T(8,128)(2,1)S(1)}, u32[]{:S(2)}, u32[]{:S(2)}) collective-permute-start(bf16[1280,512]{1,0:T(8,128)(2,1)} %param.15), channel_id=1, source_target_pairs={{0,1},{1,0},{2,3},{3,2},{4,5},{5,4},{6,7},{7,6},{8,9},{9,8},{10,11... | collective-permute-start | bytes 3932168 | tf_op jit(solution)/shard_map/ppermute | solution.py:18
  4.0 3.1 %collective-permute-start.1 = (bf16[160,512]{1,0:T(8,128)(2,1)}, bf16[160,512]{1,0:T(8,128)(2,1)S(1)}, u32[]{:S(2)}, u32[]{:S(2)}) collective-permute-start(bf16[160,512]{1,0:T(8,128)(2,1)} %param.14), channel_id=1, source_target_pairs={{0,1},{1,0},{2,3},{3,2},{4,5},{5,4},{6,7},{7,6},{8,9},{9,8},{10,11... | collective-permute-start | bytes 491528 | tf_op jit(solution)/shard_map/ppermute | solution.py:18
  4.1 20.4 %collective-permute-start.2 = (bf16[160,512]{1,0:T(8,128)(2,1)}, bf16[160,512]{1,0:T(8,128)(2,1)S(1)}, u32[]{:S(2)}, u32[]{:S(2)}) collective-permute-start(bf16[160,512]{1,0:T(8,128)(2,1)} %node_cot_ref.1), channel_id=1, source_target_pairs={{0,1},{1,0},{2,3},{3,2},{4,5},{5,4},{6,7},{7,6},{8,9},{9,8},{10,11... | collective-permute-start | bytes 491528 | tf_op jit(solution)/shard_map/ppermute | solution.py:18
  8.5 15.9 %copy-start.19 = (s32[1280]{0:T(1024)S(1)}, s32[1280]{0:T(1024)}, u32[]{:S(2)}) copy-start(s32[1280]{0:T(1024)} %param.18) | copy-start | bytes 15364
  8.5 15.9 %copy-start.15 = (bf16[160,512]{1,0:T(8,128)(2,1)S(1)}, bf16[160,512]{1,0:T(8,128)(2,1)}, u32[]{:S(2)}) copy-start(bf16[160,512]{1,0:T(8,128)(2,1)} %node_cot_ref.1) | copy-start | bytes 491524
  8.6 31.1 %all-to-all-start = ((bf16[128,4,512]{2,1,0:T(4,128)(2,1)}), bf16[128,4,512]{2,1,0:T(4,128)(2,1)S(1)}, u32[]{:S(2)}, u32[]{:S(2)}) async-start(bf16[128,4,512]{2,1,0:T(4,128)(2,1)} %reshape.68), calls=%async_computation | async-start | bytes 1048576 | tf_op jit(solution)/shard_map/all_to_all | solution.py:352
  39.8 4.8 %collective-permute-start.3 = (bf16[512,512]{1,0:T(8,128)(2,1)S(1)}, bf16[512,512]{1,0:T(8,128)(2,1)S(1)}, u32[]{:S(2)}, u32[]{:S(2)}) collective-permute-start(bf16[512,512]{1,0:T(8,128)(2,1)S(1)} %reshape.71.mine_ref), channel_id=1, source_target_pairs={{0,1},{1,0},{2,3},{3,2},{4,5},{5,4},{6,7},{7,6},{8,9},{9,8},{10,11... | collective-permute-start | bytes 1572872 | tf_op jit(solution)/shard_map/ppermute | solution.py:18
  55.3 2.3 %collective-permute-start.4 = (f32[320,512]{1,0:T(8,128)}, f32[320,512]{1,0:T(8,128)S(1)}, u32[]{:S(2)}, u32[]{:S(2)}) collective-permute-start(f32[320,512]{1,0:T(8,128)} %get-tuple-element.68.partial_ref), channel_id=1, source_target_pairs={{0,1},{1,0},{2,3},{3,2},{4,5},{5,4},{6,7},{7,6},{8,9},{9,8},{10,11... | collective-permute-start | bytes 1966088 | tf_op jit(solution)/shard_map/ppermute | solution.py:18
  69.3 2.2 %collective-permute-start.5 = (bf16[512,512]{1,0:T(8,128)(2,1)}, bf16[512,512]{1,0:T(8,128)(2,1)S(1)}, u32[]{:S(2)}, u32[]{:S(2)}) collective-permute-start(bf16[512,512]{1,0:T(8,128)(2,1)} %get-tuple-element.76), channel_id=1, source_target_pairs={{0,1},{1,0},{2,3},{3,2},{4,5},{5,4},{6,7},{7,6},{8,9},{9,8},{10,11... | collective-permute-start | bytes 1572872 | tf_op jit(solution)/shard_map/ppermute | solution.py:18
  73.8 24.0 %all-to-all-start.1 = ((bf16[128,4,512]{2,1,0:T(4,128)(2,1)}), bf16[128,4,512]{2,1,0:T(4,128)(2,1)S(1)}, u32[]{:S(2)}, u32[]{:S(2)}) async-start(bf16[128,4,512]{2,1,0:T(4,128)(2,1)} %reshape.72), calls=%async_computation.1 | async-start | bytes 1048576 | tf_op jit(solution)/shard_map/all_to_all | solution.py:442
  90.3 2.4 %collective-permute-start.6 = (bf16[448,512]{1,0:T(8,128)(2,1)}, bf16[448,512]{1,0:T(8,128)(2,1)S(1)}, u32[]{:S(2)}, u32[]{:S(2)}) collective-permute-start(bf16[448,512]{1,0:T(8,128)(2,1)} %get-tuple-element.83), channel_id=1, source_target_pairs={{0,1},{1,0},{2,3},{3,2},{4,5},{5,4},{6,7},{7,6},{8,9},{9,8},{10,11... | collective-permute-start | bytes 1376264 | tf_op jit(solution)/shard_map/ppermute | solution.py:18
  91.0 2.3 %collective-permute-start.7 = (bf16[448,512]{1,0:T(8,128)(2,1)}, bf16[448,512]{1,0:T(8,128)(2,1)S(1)}, u32[]{:S(2)}, u32[]{:S(2)}) collective-permute-start(bf16[448,512]{1,0:T(8,128)(2,1)} %get-tuple-element.84), channel_id=1, source_target_pairs={{0,1},{1,0},{2,3},{3,2},{4,5},{5,4},{6,7},{7,6},{8,9},{9,8},{10,11... | collective-permute-start | bytes 1376264 | tf_op jit(solution)/shard_map/ppermute | solution.py:18
  91.1 2.9 %collective-permute-start.8 = (bf16[448,512]{1,0:T(8,128)(2,1)}, bf16[448,512]{1,0:T(8,128)(2,1)S(1)}, u32[]{:S(2)}, u32[]{:S(2)}) collective-permute-start(bf16[448,512]{1,0:T(8,128)(2,1)} %get-tuple-element.85), channel_id=1, source_target_pairs={{0,1},{1,0},{2,3},{3,2},{4,5},{5,4},{6,7},{7,6},{8,9},{9,8},{10,11... | collective-permute-start | bytes 1376264 | tf_op jit(solution)/shard_map/ppermute | solution.py:18
  91.5 3.1 %collective-permute-start.9 = (bf16[448,512]{1,0:T(8,128)(2,1)}, bf16[448,512]{1,0:T(8,128)(2,1)S(1)}, u32[]{:S(2)}, u32[]{:S(2)}) collective-permute-start(bf16[448,512]{1,0:T(8,128)(2,1)} %get-tuple-element.86), channel_id=1, source_target_pairs={{0,1},{1,0},{2,3},{3,2},{4,5},{5,4},{6,7},{7,6},{8,9},{9,8},{10,11... | collective-permute-start | bytes 1376264 | tf_op jit(solution)/shard_map/ppermute | solution.py:18
  101.6 17.9 %all-to-all-start.2 = ((bf16[4,448,512]{2,1,0:T(8,128)(2,1)}), bf16[4,448,512]{2,1,0:T(8,128)(2,1)S(1)}, u32[]{:S(2)}, u32[]{:S(2)}) async-start(bf16[4,448,512]{2,1,0:T(8,128)(2,1)} %bitcast.22), calls=%async_computation.2 | async-start | bytes 3670016 | tf_op jit(solution)/shard_map/all_to_all | solution.py:81
  120.7 11.4 %all-to-all-start.3 = ((bf16[4,112,512]{2,1,0:T(8,128)(2,1)}), bf16[4,112,512]{2,1,0:T(8,128)(2,1)S(1)}, u32[]{:S(2)}, u32[]{:S(2)}) async-start(bf16[4,112,512]{2,1,0:T(8,128)(2,1)} %bitcast.23), calls=%async_computation.3 | async-start | bytes 917504 | tf_op jit(solution)/shard_map/all_to_all | solution.py:81
  124.2 6.0 %copy-start.20 = (bf16[1280,512]{1,0:T(8,128)(2,1)S(1)}, bf16[1280,512]{1,0:T(8,128)(2,1)}, u32[]{:S(2)}) copy-start(bf16[1280,512]{1,0:T(8,128)(2,1)} %cot_ref.1) | copy-start | bytes 3932164
  124.2 6.0 %copy-start.23 = (bf16[1280,512]{1,0:T(8,128)(2,1)S(1)}, bf16[1280,512]{1,0:T(8,128)(2,1)}, u32[]{:S(2)}) copy-start(bf16[1280,512]{1,0:T(8,128)(2,1)} %get-tuple-element.78.grad_act_ref) | copy-start | bytes 3932164
  126.3 10.4 %copy-start.14 = (f32[160,512]{1,0:T(8,128)S(1)}, f32[160,512]{1,0:T(8,128)}, u32[]{:S(2)}) copy-start(f32[160,512]{1,0:T(8,128)} %get-tuple-element.96) | copy-start | bytes 983044
  126.3 10.3 %collective-permute-start.10 = (f32[160,512]{1,0:T(8,128)S(1)}, f32[160,512]{1,0:T(8,128)}, u32[]{:S(2)}, u32[]{:S(2)}) collective-permute-start(f32[160,512]{1,0:T(8,128)S(1)} %slice.23), channel_id=1, source_target_pairs={{0,1},{1,0},{2,3},{3,2},{4,5},{5,4},{6,7},{7,6},{8,9},{9,8},{10,11... | collective-permute-start | bytes 983048 | tf_op jit(solution)/shard_map/ppermute | solution.py:18
  132.9 11.7 %all-to-all-start.4 = ((bf16[8,14,512]{2,1,0:T(8,128)(2,1)}), bf16[8,14,512]{2,1,0:T(8,128)(2,1)S(1)}, u32[]{:S(2)}, u32[]{:S(2)}) async-start(bf16[8,14,512]{2,1,0:T(8,128)(2,1)} %reshape.75), calls=%async_computation.4 | async-start | bytes 262144 | tf_op jit(solution)/shard_map/all_to_all | solution.py:81
  182.2 6.3 %copy-start = (bf16[4,448,512]{2,1,0:T(8,128)(2,1)}, bf16[4,448,512]{2,1,0:T(8,128)(2,1)S(1)}, u32[]{:S(2)}) copy-start(bf16[4,448,512]{2,1,0:T(8,128)(2,1)S(1)} %all_to_all.42) | copy-start | bytes 5505028
  182.2 9.9 %collective-permute-start.11 = (bf16[1792,512]{1,0:T(8,128)(2,1)S(1)}, bf16[1792,512]{1,0:T(8,128)(2,1)}, u32[]{:S(2)}, u32[]{:S(2)}) collective-permute-start(bf16[1792,512]{1,0:T(8,128)(2,1)S(1)} %bitcast.20), channel_id=1, source_target_pairs={{0,1},{1,0},{2,3},{3,2},{4,5},{5,4},{6,7},{7,6},{8,9},{9,8},{10,11... | collective-permute-start | bytes 5505032 | tf_op jit(solution)/shard_map/ppermute | solution.py:18
  (17 other events, 51.2 us)

commit v4 on v3

--- a/solution.py
+++ b/solution.py
@@ -140,6 +140,7 @@
         out_specs=[anywhere] * len(sizes),
         scratch_shapes=[pltpu.SemaphoreType.DMA((blocks,))],
         input_output_aliases={2 + k: k for k in range(len(outs))},
+        compiler_params=pltpu.CompilerParams(vmem_limit_bytes=4 * 1024 * 1024),
         name="place",
     )(core.astype(jnp.int32).reshape(1), half, *outs)
 
@@ -299,7 +300,7 @@
         out_ref[at] = (kept_ref[at].astype(f32) + got_ref[...].astype(f32)).astype(bf16)
 
 
-def run(kernel, name, arguments, results, scratch=(), scalars=0, flops=0):
+def run(kernel, name, arguments, results, scratch=(), scalars=0, flops=0, room=22):
     vmem = pl.BlockSpec(memory_space=pltpu.VMEM)
     return pl.pallas_call(
         kernel,
@@ -308,7 +309,7 @@
         out_specs=[vmem] * len(results),
         out_shape=[jax.ShapeDtypeStruct(*result) for result in results],
         scratch_shapes=list(scratch),
-        compiler_params=pltpu.CompilerParams(vmem_limit_bytes=60 * 1024 * 1024),
+        compiler_params=pltpu.CompilerParams(vmem_limit_bytes=room * 1024 * 1024),
         cost_estimate=pl.CostEstimate(
             flops=flops, transcendentals=0, bytes_accessed=8 * 1024 * 1024
         ),
@@ -474,7 +475,7 @@
     got = [swapped(block) for block in sent]
     kept, got, returned = lax.optimization_barrier((kept, got, returned))
     value = reduced(
-        run(pair_kernel, "pair", [kept, *got], [(kept.shape, bf16)], flops=kept.size)[0]
+        run(pair_kernel, "pair", [kept, *got], [(kept.shape, bf16)], flops=kept.size, room=6)[0]
     )
     send_high, send_low = split_two(local_sum + mat_tn(pick_ghost, returned.reshape(ghosts, width)))
     recv_high, recv_low = split_two(recv_sum)

time: 196 us -> 208 us (1.061)
  local copies, waits for them, and re-layouts: 9.82 us -> 38.1 us
  Pallas kernels: 39.8 us -> 21 us
  matrix products: 18.2 us -> 16 us
    unnamed x49 -> x107, local copies, waits for them, and re-layouts: 3.47 us -> 30.8 us
    pallas_call x4, Pallas kernels: 34.2 us -> 16.9 us  [run(): pl.pallas_call(kernel, in_specs=[pl.BlockSpec(memory_space=pltpu.SMEM)] *...]
    all_to_all x3, starting transfers between devices: 10.9 us -> 14.3 us  [exchange(): lax.all_to_all(array, ('nodes', 'rep'), 0, 0, tiled=True, axis_index_grou...]
    all_to_all x3, waiting for transfers between devices: 11 us -> 14.3 us  [exchange(): lax.all_to_all(array, ('nodes', 'rep'), 0, 0, tiled=True, axis_index_grou...]
    all_to_all x1, waiting for transfers between devices: 3.12 us -> 0.01 us  [shards(): lax.all_to_all(paired.reshape(parts, slots, width), 'nodes', 0, 0, tiled=...]
    ppermute x12, starting transfers between devices: 19.6 us -> 16.5 us  [swapped(): return lax.ppermute(array, 'rep', pairs)]
    dot_general x5, matrix products: 8.99 us -> 6.38 us  [mat_nt(): lax.dot_general(left, right, (((1,), (1,)), ((), ())), preferred_element_...]
  transfers between devices with their start and end apart: 17 -> 17, of which waited for: 13 -> 11; matrix products, arithmetic and copies ran while one was open for 14% -> 11% of each run, Pallas kernels for 6% -> 3%
where the time goes in v4:
time: 208 us; the launch traced here: 206 us
  starting transfers between devices  52.8 us (25%)
  local copies, waits for them, and re-layouts  38.1 us (18%)
  blocking collectives  38 us (18%)
  waiting for transfers between devices  32.7 us (16%)
  Pallas kernels  21 us (10%)
  matrix products  16 us (8%)
  other arithmetic  6.17 us (3%)
    all_to_all x3, blocking collectives, exchange(): lax.all_to_all(array, ('nodes', 'rep'), 0, 0, tiled=True, axis_index_grou...  38 us
    unnamed x107, local copies, waits for them, and re-layouts  30.8 us
    pallas_call x4, Pallas kernels, run(): pl.pallas_call(kernel, in_specs=[pl.BlockSpec(memory_space=pltpu.SMEM)] *...  16.9 us
    ppermute x12, starting transfers between devices, swapped(): return lax.ppermute(array, 'rep', pairs)  16.5 us
    all_to_all x1, starting transfers between devices, shards(): arrived = lax.all_to_all(outgoing, 'nodes', 0, 0, tiled=True)  14.4 us
    all_to_all x3, waiting for transfers between devices, exchange(): lax.all_to_all(array, ('nodes', 'rep'), 0, 0, tiled=True, axis_index_grou...  14.3 us
    all_to_all x3, starting transfers between devices, exchange(): lax.all_to_all(array, ('nodes', 'rep'), 0, 0, tiled=True, axis_index_grou...  14.3 us
    ppermute x12, waiting for transfers between devices, swapped(): return lax.ppermute(array, 'rep', pairs)  9.37 us
  transfers between devices with their start and end apart: 17, of which 11 were waited for; matrix products, arithmetic and copies ran while one was open for 11% of the time, Pallas kernels for 3%

profile of v4, /device:TPU:1, one launch (start us, length us, event | category | flops | bytes accessed | tf_op | source)
XLA Modules:
  0.0 206.0 jit_solution(6102294748134964246)
XLA Ops:
  0.6 3.3 %collective-permute-start = (bf16[1280,512]{1,0:T(8,128)(2,1)}, bf16[1280,512]{1,0:T(8,128)(2,1)S(1)}, u32[]{:S(2)}, u32[]{:S(2)}) collective-permute-start(bf16[1280,512]{1,0:T(8,128)(2,1)} %param.15), channel_id=1, source_target_pairs={{0,1},{1,0},{2,3},{3,2},{4,5},{5,4},{6,7},{7,6},{8,9},{9,8},{10,11... | collective-permute-start | bytes 3932168 | tf_op jit(solution)/shard_map/ppermute | solution.py:18
  8.6 14.4 %all-to-all-start = ((bf16[128,4,512]{2,1,0:T(4,128)(2,1)}), bf16[128,4,512]{2,1,0:T(4,128)(2,1)}, u32[]{:S(2)}, u32[]{:S(2)}) async-start(bf16[128,4,512]{2,1,0:T(4,128)(2,1)} %reshape.68), calls=%async_computation | async-start | bytes 1048576 | tf_op jit(solution)/shard_map/all_to_all | solution.py:353
  24.0 3.4 %convolution_convert_fusion.local_ref = bf16[1280,512]{1,0:T(8,128)(2,1)} fusion(bf16[320,512]{1,0:T(8,128)(2,1)} %copy-done.17, s32[1280]{0:T(1024)S(1)} %get-tuple-element.109), kind=kOutput, calls=%fused_computation.3 | convolution fusion | flops 420495360 | bytes 1643520 | tf_op jit(solution)/shard_map/dot_general | solution.py:22
  28.4 2.3 %convolution_add_fusion.1.known_ref = f32[1280,512]{1,0:T(8,128)} fusion(f32[1280,512]{1,0:T(8,128)S(1)} %fusion.13, bf16[1280,512]{1,0:T(8,128)(2,1)S(1)} %collective-permute-done.edge_ref, bf16[1536,512]{1,0:T(8,128)(2,1)S(1)} %copy-done), kind=kOutput, calls=%fused_computation.1 | convolution fusion | flops 671744000 | bytes 7077888 | tf_op jit(solution)/shard_map/dot_general | solution.py:22
  30.7 9.0 %all-to-all-done = bf16[128,4,512]{2,1,0:T(4,128)(2,1)} async-done(((bf16[128,4,512]{2,1,0:T(4,128)(2,1)}), bf16[128,4,512]{2,1,0:T(4,128)(2,1)}, u32[]{:S(2)}, u32[]{:S(2)}) %all-to-all-start) | async-done | bytes 524320 | tf_op jit(solution)/shard_map/all_to_all | solution.py:353
  40.9 3.3 %collective-permute-start.3 = (bf16[512,512]{1,0:T(8,128)(2,1)S(1)}, bf16[512,512]{1,0:T(8,128)(2,1)S(1)}, u32[]{:S(2)}, u32[]{:S(2)}) collective-permute-start(bf16[512,512]{1,0:T(8,128)(2,1)S(1)} %reshape.71.mine_ref), channel_id=1, source_target_pairs={{0,1},{1,0},{2,3},{3,2},{4,5},{5,4},{6,7},{7,6},{8,9},{9,8},{10,11... | collective-permute-start | bytes 1572872 | tf_op jit(solution)/shard_map/ppermute | solution.py:18
  49.9 5.5 %forward.1 = (bf16[1280,512]{1,0:T(8,128)(2,1)S(1)}, f32[1280,512]{1,0:T(8,128)S(1)}, bf16[1280,512]{1,0:T(8,128)(2,1)S(1)}, f32[1280,512]{1,0:T(8,128)S(1)}, f3...) custom-call(f32[1280,512]{1,0:T(8,128)S(1)} %copy-done.1, bf16[1280,512]{1,0:T(8,128)(2,1)S(1)} %copy-done.33, ...), custom_call_target="tpu_custom_call" | custom-call | flops 4026531840 | bytes 8388608 | tf_op jit(solution)/shard_map/forward/pallas_call | solution.py:305
  59.7 5.2 %backward.1 = (bf16[512,512]{1,0:T(8,128)(2,1)S(1)}, f32[512,512]{1,0:T(8,128)S(1)}, bf16[1280,512]{1,0:T(8,128)(2,1)S(1)}, bf16[1280,512]{1,0:T(8,128)(2,1)S(1)...) custom-call(f32[320,512]{1,0:T(8,128)S(1)} %get-tuple-element.68.par, ...), custom_call_target="tpu_custom_call" | custom-call | flops 5368709120 | bytes 8388608 | tf_op jit(solution)/shard_map/backward/pallas_call | solution.py:305
  69.0 2.0 reshape.72
  71.0 7.5 %all-to-all-start.1 = ((bf16[128,4,512]{2,1,0:T(4,128)(2,1)}), bf16[128,4,512]{2,1,0:T(4,128)(2,1)}, u32[]{:S(2)}, u32[]{:S(2)}) async-start(bf16[128,4,512]{2,1,0:T(4,128)(2,1)} %reshape.72), calls=%async_computation.1 | async-start | bytes 1048576 | tf_op jit(solution)/shard_map/all_to_all | solution.py:443
  91.3 4.5 %weights.1 = (bf16[1792,512]{1,0:T(8,128)(2,1)S(1)}, f32[320,512]{1,0:T(8,128)S(1)}, f32[320,512]{1,0:T(8,128)S(1)}, f32[160,512]{1,0:T(8,128)S(1)}, bf16[448,51...) custom-call(s32[1]{0:T(128)} %bitcast.core_ref, ...), custom_call_target="tpu_custom_call" | custom-call | flops 4026531840 | bytes 8388608 | tf_op jit(solution)/shard_map/weights/pallas_call | solution.py:305
  109.0 4.4 %all-to-all-start.2 = ((bf16[4,448,512]{2,1,0:T(8,128)(2,1)}), bf16[4,448,512]{2,1,0:T(8,128)(2,1)}, u32[]{:S(2)}, u32[]{:S(2)}) async-start(bf16[4,448,512]{2,1,0:T(8,128)(2,1)} %bitcast.6), calls=%async_computation.2 | async-start | bytes 3670016 | tf_op jit(solution)/shard_map/all_to_all | solution.py:81
  119.8 7.9 %all-to-all-done.2 = bf16[4,448,512]{2,1,0:T(8,128)(2,1)} async-done(((bf16[4,448,512]{2,1,0:T(8,128)(2,1)}), bf16[4,448,512]{2,1,0:T(8,128)(2,1)}, u32[]{:S(2)}, u32[]{:S(2)}) %all-to-all-start.2) | async-done | bytes 1835040 | tf_op jit(solution)/shard_map/all_to_all | solution.py:81
  127.7 2.7 %reduce_sum.36 = bf16[448,512]{1,0:T(8,128)(2,1)} reduce(bf16[4,448,512]{2,1,0:T(8,128)(2,1)} %all-to-all-done.2, bf16[]{:T(256)} %constant.36.clone.1), dimensions={0}, to_apply=%region_0.1 | reduce | flops 688128 | bytes 2293762 | tf_op jit(solution)/shard_map/reduce_sum | solution.py:87
  130.4 3.5 %all-to-all-start.3 = ((bf16[4,112,512]{2,1,0:T(8,128)(2,1)}), bf16[4,112,512]{2,1,0:T(8,128)(2,1)S(1)}, u32[]{:S(2)}, u32[]{:S(2)}) async-start(bf16[4,112,512]{2,1,0:T(8,128)(2,1)} %bitcast.7), calls=%async_computation.3 | async-start | bytes 917504 | tf_op jit(solution)/shard_map/all_to_all | solution.py:81
  136.4 2.0 collective-permute-start.10
  141.2 6.4 %all-to-all-start.4 = ((bf16[8,14,512]{2,1,0:T(8,128)(2,1)}), bf16[8,14,512]{2,1,0:T(8,128)(2,1)S(1)}, u32[]{:S(2)}, u32[]{:S(2)}) async-start(bf16[8,14,512]{2,1,0:T(8,128)(2,1)} %reshape.75), calls=%async_computation.4 | async-start | bytes 262144 | tf_op jit(solution)/shard_map/all_to_all | solution.py:81
  149.3 6.3 %all-to-all-done.4 = bf16[8,14,512]{2,1,0:T(8,128)(2,1)S(1)} async-done(((bf16[8,14,512]{2,1,0:T(8,128)(2,1)}), bf16[8,14,512]{2,1,0:T(8,128)(2,1)S(1)}, u32[]{:S(2)}, u32[]{:S(2)}) %all-to-all-start.4) | async-done | bytes 114720 | tf_op jit(solution)/shard_map/all_to_all | solution.py:81
  155.6 10.3 %all_to_all.40 = bf16[8,14,512]{2,1,0:T(8,128)(2,1)S(1)} all-to-all(bf16[8,14,512]{2,1,0:T(8,128)(2,1)S(1)} %broadcast_in_dim.41), channel_id=1, replica_groups={{0,8,16,24,32,40,48,56},{1,9,17,25,33,41,49,57},{2,10,18,26,34,42,50,58..., dimensions={0} | all-to-all | bytes 229376 | tf_op jit(solution)/shard_map/all_to_all | solution.py:81
  166.0 9.0 %all_to_all.41 = bf16[4,112,512]{2,1,0:T(8,128)(2,1)S(1)} all-to-all(bf16[4,112,512]{2,1,0:T(8,128)(2,1)S(1)} %broadcast_in_dim.43), channel_id=1, replica_groups={{0,64,128,192},{8,72,136,200},{16,80,144,208},{24,88,152,216},{32,96,16..., dimensions={0} | all-to-all | bytes 917504 | tf_op jit(solution)/shard_map/all_to_all | solution.py:81
  175.1 18.8 %all_to_all.42 = bf16[4,448,512]{2,1,0:T(8,128)(2,1)S(1)} all-to-all(bf16[4,448,512]{2,1,0:T(8,128)(2,1)S(1)} %broadcast_in_dim.45), channel_id=1, replica_groups={{0,2,4,6},{8,10,12,14},{16,18,20,22},{24,26,28,30},{32,34,36,38},{40,42..., dimensions={0} | all-to-all | bytes 3670016 | tf_op jit(solution)/shard_map/all_to_all | solution.py:81
  193.9 5.6 %collective-permute-start.11 = (bf16[1792,512]{1,0:T(8,128)(2,1)S(1)}, bf16[1792,512]{1,0:T(8,128)(2,1)}, u32[]{:S(2)}, u32[]{:S(2)}) collective-permute-start(bf16[1792,512]{1,0:T(8,128)(2,1)S(1)} %bitcast.20), channel_id=1, source_target_pairs={{0,1},{1,0},{2,3},{3,2},{4,5},{5,4},{6,7},{7,6},{8,9},{9,8},{10,11... | collective-permute-start | bytes 5505032 | tf_op jit(solution)/shard_map/ppermute | solution.py:18
  200.8 2.3 %collective-permute-done.11.half_ref = bf16[1792,512]{1,0:T(8,128)(2,1)} collective-permute-done((bf16[1792,512]{1,0:T(8,128)(2,1)S(1)}, bf16[1792,512]{1,0:T(8,128)(2,1)}, u32[]{:S(2)}, u32[]{:S(2)}) %collective-permute-start.11) | collective-permute-done | bytes 1835040 | tf_op jit(solution)/shard_map/ppermute | solution.py:18
  203.1 2.8 %place.3 = (bf16[1536,512]{1,0:T(8,128)(2,1)}, bf16[512,512]{1,0:T(8,128)(2,1)}, bf16[1024,512]{1,0:T(8,128)(2,1)}, bf16[512,512]{1,0:T(8,128)(2,1)}) custom-call(s32[1]{0:T(128)} %bitcast.8.core_ref, bf16[1792,512]{1,0:T(8,128)(2,1)} %collective-permute-done.11.half_ref, ...), custom_call_target="tpu_custom_call", output_to_operand_aliasing={{0}: (2, {}), {1}: (3, {}), {2}: (4, {}), {3}: (5, {})} | custom-call | tf_op jit(solution)/shard_map/place/pallas_call | solution.py:135
  (163 shorter events, 62.3 us)
Async XLA Ops:
  0.6 27.7 %collective-permute-start = (bf16[1280,512]{1,0:T(8,128)(2,1)}, bf16[1280,512]{1,0:T(8,128)(2,1)S(1)}, u32[]{:S(2)}, u32[]{:S(2)}) collective-permute-start(bf16[1280,512]{1,0:T(8,128)(2,1)} %param.15), channel_id=1, source_target_pairs={{0,1},{1,0},{2,3},{3,2},{4,5},{5,4},{6,7},{7,6},{8,9},{9,8},{10,11... | collective-permute-start | bytes 3932168 | tf_op jit(solution)/shard_map/ppermute | solution.py:18
  4.0 3.1 %collective-permute-start.1 = (bf16[160,512]{1,0:T(8,128)(2,1)}, bf16[160,512]{1,0:T(8,128)(2,1)S(1)}, u32[]{:S(2)}, u32[]{:S(2)}) collective-permute-start(bf16[160,512]{1,0:T(8,128)(2,1)} %param.14), channel_id=1, source_target_pairs={{0,1},{1,0},{2,3},{3,2},{4,5},{5,4},{6,7},{7,6},{8,9},{9,8},{10,11... | collective-permute-start | bytes 491528 | tf_op jit(solution)/shard_map/ppermute | solution.py:18
  4.1 19.9 %collective-permute-start.2 = (bf16[160,512]{1,0:T(8,128)(2,1)}, bf16[160,512]{1,0:T(8,128)(2,1)S(1)}, u32[]{:S(2)}, u32[]{:S(2)}) collective-permute-start(bf16[160,512]{1,0:T(8,128)(2,1)} %node_cot_ref.1), channel_id=1, source_target_pairs={{0,1},{1,0},{2,3},{3,2},{4,5},{5,4},{6,7},{7,6},{8,9},{9,8},{10,11... | collective-permute-start | bytes 491528 | tf_op jit(solution)/shard_map/ppermute | solution.py:18
  7.1 16.8 %copy-start.17 = (bf16[320,512]{1,0:T(8,128)(2,1)}, bf16[320,512]{1,0:T(8,128)(2,1)S(1)}, u32[]{:S(2)}) copy-start(bf16[320,512]{1,0:T(8,128)(2,1)S(1)} %constant_dynamic-update-slice_fusion.part_ref) | copy-start | bytes 983044
  8.5 15.4 %copy-start.52 = (s32[1280]{0:T(1024)S(1)}, s32[1280]{0:T(1024)}, u32[]{:S(2)}) copy-start(s32[1280]{0:T(1024)} %param.18) | copy-start | bytes 15364
  8.5 15.4 %copy-start.16 = (bf16[160,512]{1,0:T(8,128)(2,1)S(1)}, bf16[160,512]{1,0:T(8,128)(2,1)}, u32[]{:S(2)}) copy-start(bf16[160,512]{1,0:T(8,128)(2,1)} %node_cot_ref.1) | copy-start | bytes 491524
  8.6 31.2 %all-to-all-start = ((bf16[128,4,512]{2,1,0:T(4,128)(2,1)}), bf16[128,4,512]{2,1,0:T(4,128)(2,1)}, u32[]{:S(2)}, u32[]{:S(2)}) async-start(bf16[128,4,512]{2,1,0:T(4,128)(2,1)} %reshape.68), calls=%async_computation | async-start | bytes 1048576 | tf_op jit(solution)/shard_map/all_to_all | solution.py:353
  28.3 17.4 %copy-start.27 = (f32[512]{0:T(512)S(1)}, f32[512]{0:T(512)}, u32[]{:S(2)}) copy-start(f32[512]{0:T(512)} %param.24) | copy-start | bytes 6148
  28.3 17.4 %copy-start.28 = (f32[512]{0:T(512)S(1)}, f32[512]{0:T(512)}, u32[]{:S(2)}) copy-start(f32[512]{0:T(512)} %param.23) | copy-start | bytes 6148
  40.9 4.8 %collective-permute-start.3 = (bf16[512,512]{1,0:T(8,128)(2,1)S(1)}, bf16[512,512]{1,0:T(8,128)(2,1)S(1)}, u32[]{:S(2)}, u32[]{:S(2)}) collective-permute-start(bf16[512,512]{1,0:T(8,128)(2,1)S(1)} %reshape.71.mine_ref), channel_id=1, source_target_pairs={{0,1},{1,0},{2,3},{3,2},{4,5},{5,4},{6,7},{7,6},{8,9},{9,8},{10,11... | collective-permute-start | bytes 1572872 | tf_op jit(solution)/shard_map/ppermute | solution.py:18
  57.6 2.1 %collective-permute-start.4 = (f32[320,512]{1,0:T(8,128)S(1)}, f32[320,512]{1,0:T(8,128)S(1)}, u32[]{:S(2)}, u32[]{:S(2)}) collective-permute-start(f32[320,512]{1,0:T(8,128)S(1)} %get-tuple-element.68.partial_ref), channel_id=1, source_target_pairs={{0,1},{1,0},{2,3},{3,2},{4,5},{5,4},{6,7},{7,6},{8,9},{9,8},{10,11... | collective-permute-start | bytes 1966088 | tf_op jit(solution)/shard_map/ppermute | solution.py:18
  66.0 2.0 collective-permute-start.5
  71.0 31.7 %all-to-all-start.1 = ((bf16[128,4,512]{2,1,0:T(4,128)(2,1)}), bf16[128,4,512]{2,1,0:T(4,128)(2,1)}, u32[]{:S(2)}, u32[]{:S(2)}) async-start(bf16[128,4,512]{2,1,0:T(4,128)(2,1)} %reshape.72), calls=%async_computation.1 | async-start | bytes 1048576 | tf_op jit(solution)/shard_map/all_to_all | solution.py:443
  97.8 1.9 collective-permute-start.6
  98.3 2.1 %collective-permute-start.7 = (bf16[448,512]{1,0:T(8,128)(2,1)S(1)}, bf16[448,512]{1,0:T(8,128)(2,1)S(1)}, u32[]{:S(2)}, u32[]{:S(2)}) collective-permute-start(bf16[448,512]{1,0:T(8,128)(2,1)S(1)} %get-tuple-element.84), channel_id=1, source_target_pairs={{0,1},{1,0},{2,3},{3,2},{4,5},{5,4},{6,7},{7,6},{8,9},{9,8},{10,11... | collective-permute-start | bytes 1376264 | tf_op jit(solution)/shard_map/ppermute | solution.py:18
  98.4 2.8 %collective-permute-start.8 = (bf16[448,512]{1,0:T(8,128)(2,1)S(1)}, bf16[448,512]{1,0:T(8,128)(2,1)S(1)}, u32[]{:S(2)}, u32[]{:S(2)}) collective-permute-start(bf16[448,512]{1,0:T(8,128)(2,1)S(1)} %get-tuple-element.85), channel_id=1, source_target_pairs={{0,1},{1,0},{2,3},{3,2},{4,5},{5,4},{6,7},{7,6},{8,9},{9,8},{10,11... | collective-permute-start | bytes 1376264 | tf_op jit(solution)/shard_map/ppermute | solution.py:18
  98.8 3.1 %collective-permute-start.9 = (bf16[448,512]{1,0:T(8,128)(2,1)S(1)}, bf16[448,512]{1,0:T(8,128)(2,1)S(1)}, u32[]{:S(2)}, u32[]{:S(2)}) collective-permute-start(bf16[448,512]{1,0:T(8,128)(2,1)S(1)} %get-tuple-element.86), channel_id=1, source_target_pairs={{0,1},{1,0},{2,3},{3,2},{4,5},{5,4},{6,7},{7,6},{8,9},{9,8},{10,11... | collective-permute-start | bytes 1376264 | tf_op jit(solution)/shard_map/ppermute | solution.py:18
  109.0 18.7 %all-to-all-start.2 = ((bf16[4,448,512]{2,1,0:T(8,128)(2,1)}), bf16[4,448,512]{2,1,0:T(8,128)(2,1)}, u32[]{:S(2)}, u32[]{:S(2)}) async-start(bf16[4,448,512]{2,1,0:T(8,128)(2,1)} %bitcast.6), calls=%async_computation.2 | async-start | bytes 3670016 | tf_op jit(solution)/shard_map/all_to_all | solution.py:81
  130.4 10.0 %all-to-all-start.3 = ((bf16[4,112,512]{2,1,0:T(8,128)(2,1)}), bf16[4,112,512]{2,1,0:T(8,128)(2,1)S(1)}, u32[]{:S(2)}, u32[]{:S(2)}) async-start(bf16[4,112,512]{2,1,0:T(8,128)(2,1)} %bitcast.7), calls=%async_computation.3 | async-start | bytes 917504 | tf_op jit(solution)/shard_map/all_to_all | solution.py:81
  136.4 11.2 %copy-start.15 = (f32[160,512]{1,0:T(8,128)S(1)}, f32[160,512]{1,0:T(8,128)}, u32[]{:S(2)}) copy-start(f32[160,512]{1,0:T(8,128)} %copy-done.14) | copy-start | bytes 983044
  136.4 11.2 %copy-start.49 = (f32[320,512]{1,0:T(8,128)S(1)}, f32[320,512]{1,0:T(8,128)}, u32[]{:S(2)}) copy-start(f32[320,512]{1,0:T(8,128)} %copy-done.48) | copy-start | bytes 1966084
  136.4 11.2 %collective-permute-start.10 = (f32[160,512]{1,0:T(8,128)S(1)}, f32[160,512]{1,0:T(8,128)}, u32[]{:S(2)}, u32[]{:S(2)}) collective-permute-start(f32[160,512]{1,0:T(8,128)S(1)} %slice.23), channel_id=1, source_target_pairs={{0,1},{1,0},{2,3},{3,2},{4,5},{5,4},{6,7},{7,6},{8,9},{9,8},{10,11... | collective-permute-start | bytes 983048 | tf_op jit(solution)/shard_map/ppermute | solution.py:18
  141.2 14.4 %all-to-all-start.4 = ((bf16[8,14,512]{2,1,0:T(8,128)(2,1)}), bf16[8,14,512]{2,1,0:T(8,128)(2,1)S(1)}, u32[]{:S(2)}, u32[]{:S(2)}) async-start(bf16[8,14,512]{2,1,0:T(8,128)(2,1)} %reshape.75), calls=%async_computation.4 | async-start | bytes 262144 | tf_op jit(solution)/shard_map/all_to_all | solution.py:81
  193.9 9.1 %collective-permute-start.11 = (bf16[1792,512]{1,0:T(8,128)(2,1)S(1)}, bf16[1792,512]{1,0:T(8,128)(2,1)}, u32[]{:S(2)}, u32[]{:S(2)}) collective-permute-start(bf16[1792,512]{1,0:T(8,128)(2,1)S(1)} %bitcast.20), channel_id=1, source_target_pairs={{0,1},{1,0},{2,3},{3,2},{4,5},{5,4},{6,7},{7,6},{8,9},{9,8},{10,11... | collective-permute-start | bytes 5505032 | tf_op jit(solution)/shard_map/ppermute | solution.py:18
  (46 other events, 143.3 us)

commit v5 on v3

--- a/solution.py
+++ b/solution.py
@@ -299,7 +299,7 @@
         out_ref[at] = (kept_ref[at].astype(f32) + got_ref[...].astype(f32)).astype(bf16)
 
 
-def run(kernel, name, arguments, results, scratch=(), scalars=0, flops=0):
+def run(kernel, name, arguments, results, scratch=(), scalars=0, flops=0, room=60):
     vmem = pl.BlockSpec(memory_space=pltpu.VMEM)
     return pl.pallas_call(
         kernel,
@@ -308,7 +308,7 @@
         out_specs=[vmem] * len(results),
         out_shape=[jax.ShapeDtypeStruct(*result) for result in results],
         scratch_shapes=list(scratch),
-        compiler_params=pltpu.CompilerParams(vmem_limit_bytes=60 * 1024 * 1024),
+        compiler_params=pltpu.CompilerParams(vmem_limit_bytes=room * 1024 * 1024),
         cost_estimate=pl.CostEstimate(
             flops=flops, transcendentals=0, bytes_accessed=8 * 1024 * 1024
         ),
@@ -400,6 +400,7 @@
         ],
         [pltpu.VMEM((2 * ghosts, width), bf16)],
         flops=6 * square,
+        room=22,
     )
     device_count = lax.axis_size("nodes") * lax.axis_size("rep")
     edge_scale = 1.0 / math.sqrt(edges * device_count)
@@ -436,6 +437,7 @@
         + [((own, width), bf16)] * 4,
         [pltpu.VMEM((rows, width), bf16)],
         flops=8 * square,
+        room=22,
     )
     paired = (mine + swapped(theirs).astype(f32)).astype(bf16)
     paired, grad_act = lax.optimization_barrier((paired, grad_act))

time: 196 us -> 189 us (0.964)
  Pallas kernels: 39.8 us -> 29.9 us
  local copies, waits for them, and re-layouts: 9.82 us -> 13.2 us
    pallas_call x4, Pallas kernels: 34.2 us -> 24.3 us  [run(): pl.pallas_call(kernel, in_specs=[pl.BlockSpec(memory_space=pltpu.SMEM)] *...]
    unnamed x49 -> x73, local copies, waits for them, and re-layouts: 3.47 us -> 7.08 us
  transfers between devices with their start and end apart: 17 -> 17, of which waited for: 13 -> 12; matrix products, arithmetic and copies ran while one was open for 14% -> 14% of each run, Pallas kernels for 6% -> 7%
where the time goes in v5:
time: 189 us; the launch traced here: 188 us
  starting transfers between devices  51.1 us (27%)
  blocking collectives  37.2 us (20%)
  waiting for transfers between devices  32.9 us (17%)
  Pallas kernels  29.9 us (16%)
  matrix products  18.5 us (10%)
  local copies, waits for them, and re-layouts  13.2 us (7%)
  other arithmetic  3.87 us (2%)
    all_to_all x3, blocking collectives, exchange(): lax.all_to_all(array, ('nodes', 'rep'), 0, 0, tiled=True, axis_index_grou...  37.2 us
    pallas_call x4, Pallas kernels, run(): pl.pallas_call(kernel, in_specs=[pl.BlockSpec(memory_space=pltpu.SMEM)] *...  24.3 us
    ppermute x12, starting transfers between devices, swapped(): return lax.ppermute(array, 'rep', pairs)  18.7 us
    all_to_all x1, starting transfers between devices, shards(): arrived = lax.all_to_all(outgoing, 'nodes', 0, 0, tiled=True)  14.4 us
    all_to_all x3, waiting for transfers between devices, exchange(): lax.all_to_all(array, ('nodes', 'rep'), 0, 0, tiled=True, axis_index_grou...  11 us
    all_to_all x3, starting transfers between devices, exchange(): lax.all_to_all(array, ('nodes', 'rep'), 0, 0, tiled=True, axis_index_grou...  10.7 us
    all_to_all x1, waiting for transfers between devices, shards(): arrived = lax.all_to_all(outgoing, 'nodes', 0, 0, tiled=True)  9.6 us
    ppermute x12, waiting for transfers between devices, swapped(): return lax.ppermute(array, 'rep', pairs)  9.18 us
  transfers between devices with their start and end apart: 17, of which 12 were waited for; matrix products, arithmetic and copies ran while one was open for 14% of the time, Pallas kernels for 7%

profile of v5, /device:TPU:1, one launch (start us, length us, event | category | flops | bytes accessed | tf_op | source)
XLA Modules:
  0.0 188.1 jit_solution(18033436314639890544)
XLA Ops:
  0.6 3.3 %collective-permute-start = (bf16[1280,512]{1,0:T(8,128)(2,1)}, bf16[1280,512]{1,0:T(8,128)(2,1)}, u32[]{:S(2)}, u32[]{:S(2)}) collective-permute-start(bf16[1280,512]{1,0:T(8,128)(2,1)} %param.15), channel_id=1, source_target_pairs={{0,1},{1,0},{2,3},{3,2},{4,5},{5,4},{6,7},{7,6},{8,9},{9,8},{10,11... | collective-permute-start | bytes 3932168 | tf_op jit(solution)/shard_map/ppermute | solution.py:18
  8.4 14.4 %all-to-all-start = ((bf16[128,4,512]{2,1,0:T(4,128)(2,1)}), bf16[128,4,512]{2,1,0:T(4,128)(2,1)}, u32[]{:S(2)}, u32[]{:S(2)}) async-start(bf16[128,4,512]{2,1,0:T(4,128)(2,1)} %reshape.68), calls=%async_computation | async-start | bytes 1048576 | tf_op jit(solution)/shard_map/all_to_all | solution.py:352
  26.8 3.7 %convolution_add_fusion.1.known_ref = f32[1280,512]{1,0:T(8,128)} fusion(f32[1280,512]{1,0:T(8,128)S(1)} %fusion.13, bf16[1280,512]{1,0:T(8,128)(2,1)} %collective-permute-done.edge_ref, bf16[1536,512]{1,0:T(8,128)(2,1)S(1)} %copy-done), kind=kOutput, calls=%fused_computation.1 | convolution fusion | flops 671744000 | bytes 7077888 | tf_op jit(solution)/shard_map/dot_general | solution.py:22
  30.5 9.6 %all-to-all-done = bf16[128,4,512]{2,1,0:T(4,128)(2,1)} async-done(((bf16[128,4,512]{2,1,0:T(4,128)(2,1)}), bf16[128,4,512]{2,1,0:T(4,128)(2,1)}, u32[]{:S(2)}, u32[]{:S(2)}) %all-to-all-start) | async-done | bytes 524320 | tf_op jit(solution)/shard_map/all_to_all | solution.py:352
  41.3 2.4 %collective-permute-start.3 = (bf16[512,512]{1,0:T(8,128)(2,1)S(1)}, bf16[512,512]{1,0:T(8,128)(2,1)S(1)}, u32[]{:S(2)}, u32[]{:S(2)}) collective-permute-start(bf16[512,512]{1,0:T(8,128)(2,1)S(1)} %reshape.71.mine_ref), channel_id=1, source_target_pairs={{0,1},{1,0},{2,3},{3,2},{4,5},{5,4},{6,7},{7,6},{8,9},{9,8},{10,11... | collective-permute-start | bytes 1572872 | tf_op jit(solution)/shard_map/ppermute | solution.py:18
  48.3 5.6 %forward.1 = (bf16[1280,512]{1,0:T(8,128)(2,1)S(1)}, f32[1280,512]{1,0:T(8,128)S(1)}, bf16[1280,512]{1,0:T(8,128)(2,1)S(1)}, f32[1280,512]{1,0:T(8,128)S(1)}, f3...) custom-call(f32[1280,512]{1,0:T(8,128)S(1)} %copy-done.1, bf16[1280,512]{1,0:T(8,128)(2,1)S(1)} %copy-done.15, ...), custom_call_target="tpu_custom_call" | custom-call | flops 4026531840 | bytes 8388608 | tf_op jit(solution)/shard_map/forward/pallas_call | solution.py:304
  57.1 5.2 %backward.1 = (bf16[512,512]{1,0:T(8,128)(2,1)S(1)}, f32[512,512]{1,0:T(8,128)S(1)}, bf16[1280,512]{1,0:T(8,128)(2,1)S(1)}, bf16[1280,512]{1,0:T(8,128)(2,1)S(1)...) custom-call(f32[320,512]{1,0:T(8,128)S(1)} %get-tuple-element.68.par, ...), custom_call_target="tpu_custom_call" | custom-call | flops 5368709120 | bytes 8388608 | tf_op jit(solution)/shard_map/backward/pallas_call | solution.py:304
  66.6 7.2 %all-to-all-start.1 = ((bf16[128,4,512]{2,1,0:T(4,128)(2,1)}), bf16[128,4,512]{2,1,0:T(4,128)(2,1)S(1)}, u32[]{:S(2)}, u32[]{:S(2)}) async-start(bf16[128,4,512]{2,1,0:T(4,128)(2,1)} %reshape.72), calls=%async_computation.1 | async-start | bytes 1048576 | tf_op jit(solution)/shard_map/all_to_all | solution.py:444
  73.8 9.7 %weights.1 = (bf16[1792,512]{1,0:T(8,128)(2,1)}, f32[320,512]{1,0:T(8,128)}, f32[320,512]{1,0:T(8,128)}, f32[160,512]{1,0:T(8,128)}, bf16[448,512]{1,0:T(8,128)(...) custom-call(s32[1]{0:T(128)} %bitcast.core_ref, ...), custom_call_target="tpu_custom_call" | custom-call | flops 4026531840 | bytes 8388608 | tf_op jit(solution)/shard_map/weights/pallas_call | solution.py:304
  87.9 3.1 %all-to-all-done.1 = bf16[128,4,512]{2,1,0:T(4,128)(2,1)S(1)} async-done(((bf16[128,4,512]{2,1,0:T(4,128)(2,1)}), bf16[128,4,512]{2,1,0:T(4,128)(2,1)S(1)}, u32[]{:S(2)}, u32[]{:S(2)}) %all-to-all-start.1) | async-done | bytes 524320 | tf_op jit(solution)/shard_map/all_to_all | solution.py:444
  91.0 3.8 %pair.1 = bf16[1792,512]{1,0:T(8,128)(2,1)} custom-call(bf16[1792,512]{1,0:T(8,128)(2,1)} %get-tuple-element.88.kept_ref, bf16[448,512]{1,0:T(8,128)(2,1)} %copy-done.29, bf16[448,512]{1,0:T(8,128)(2,1)} %copy-done.30, bf16[448,512]{1,0:T(8,128)(2,1)} %copy-done.31, bf16[448,512]{1,0:T(8,128)(2,1)} %collective-permute-done.9.refs_3_), custom_call_target="tpu_custom_call" | custom-call | flops 917504 | bytes 8388608 | tf_op jit(solution)/shard_map/pair/pallas_call | solution.py:304
  94.8 3.6 %all-to-all-start.2 = ((bf16[4,448,512]{2,1,0:T(8,128)(2,1)}), bf16[4,448,512]{2,1,0:T(8,128)(2,1)S(1)}, u32[]{:S(2)}, u32[]{:S(2)}) async-start(bf16[4,448,512]{2,1,0:T(8,128)(2,1)} %bitcast.26), calls=%async_computation.2 | async-start | bytes 3670016 | tf_op jit(solution)/shard_map/all_to_all | solution.py:81
  105.6 2.3 %convolution_add_fusion.3 = f32[320,512]{1,0:T(8,128)} fusion(f32[320,512]{1,0:T(8,128)} %convolution_add_fusion.4, bf16[1536,512]{1,0:T(8,128)(2,1)S(1)} %copy-done, f32[320,512]{1,0:T(8,128)S(1)} %copy-done.26, f32[320,512]{1,0:T(8,128)S(1)} %fusion.3), kind=kOutput, calls=%fused_computation.9 | convolution fusion | flops 168427520 | bytes 3145728 | tf_op jit(solution)/shard_map/dot_general | solution.py:30
  107.9 4.7 %all-to-all-done.2 = bf16[4,448,512]{2,1,0:T(8,128)(2,1)S(1)} async-done(((bf16[4,448,512]{2,1,0:T(8,128)(2,1)}), bf16[4,448,512]{2,1,0:T(8,128)(2,1)S(1)}, u32[]{:S(2)}, u32[]{:S(2)}) %all-to-all-start.2) | async-done | bytes 1835040 | tf_op jit(solution)/shard_map/all_to_all | solution.py:81
  113.8 3.5 %all-to-all-start.3 = ((bf16[4,112,512]{2,1,0:T(8,128)(2,1)}), bf16[4,112,512]{2,1,0:T(8,128)(2,1)S(1)}, u32[]{:S(2)}, u32[]{:S(2)}) async-start(bf16[4,112,512]{2,1,0:T(8,128)(2,1)} %bitcast.27), calls=%async_computation.3 | async-start | bytes 917504 | tf_op jit(solution)/shard_map/all_to_all | solution.py:81
  119.3 3.9 %collective-permute-start.10 = (f32[160,512]{1,0:T(8,128)S(1)}, f32[160,512]{1,0:T(8,128)}, u32[]{:S(2)}, u32[]{:S(2)}) collective-permute-start(f32[160,512]{1,0:T(8,128)S(1)} %slice.23), channel_id=1, source_target_pairs={{0,1},{1,0},{2,3},{3,2},{4,5},{5,4},{6,7},{7,6},{8,9},{9,8},{10,11... | collective-permute-start | bytes 983048 | tf_op jit(solution)/shard_map/ppermute | solution.py:18
  126.0 3.7 %all-to-all-start.4 = ((bf16[8,14,512]{2,1,0:T(8,128)(2,1)}), bf16[8,14,512]{2,1,0:T(8,128)(2,1)S(1)}, u32[]{:S(2)}, u32[]{:S(2)}) async-start(bf16[8,14,512]{2,1,0:T(8,128)(2,1)} %reshape.75), calls=%async_computation.4 | async-start | bytes 262144 | tf_op jit(solution)/shard_map/all_to_all | solution.py:81
  131.4 6.3 %all-to-all-done.4 = bf16[8,14,512]{2,1,0:T(8,128)(2,1)S(1)} async-done(((bf16[8,14,512]{2,1,0:T(8,128)(2,1)}), bf16[8,14,512]{2,1,0:T(8,128)(2,1)S(1)}, u32[]{:S(2)}, u32[]{:S(2)}) %all-to-all-start.4) | async-done | bytes 114720 | tf_op jit(solution)/shard_map/all_to_all | solution.py:81
  137.8 10.3 %all_to_all.40 = bf16[8,14,512]{2,1,0:T(8,128)(2,1)S(1)} all-to-all(bf16[8,14,512]{2,1,0:T(8,128)(2,1)S(1)} %broadcast_in_dim.41), channel_id=1, replica_groups={{0,8,16,24,32,40,48,56},{1,9,17,25,33,41,49,57},{2,10,18,26,34,42,50,58..., dimensions={0} | all-to-all | bytes 229376 | tf_op jit(solution)/shard_map/all_to_all | solution.py:81
  148.2 9.0 %all_to_all.41 = bf16[4,112,512]{2,1,0:T(8,128)(2,1)S(1)} all-to-all(bf16[4,112,512]{2,1,0:T(8,128)(2,1)S(1)} %broadcast_in_dim.43), channel_id=1, replica_groups={{0,64,128,192},{8,72,136,200},{16,80,144,208},{24,88,152,216},{32,96,16..., dimensions={0} | all-to-all | bytes 917504 | tf_op jit(solution)/shard_map/all_to_all | solution.py:81
  157.3 18.0 %all_to_all.42 = bf16[4,448,512]{2,1,0:T(8,128)(2,1)S(1)} all-to-all(bf16[4,448,512]{2,1,0:T(8,128)(2,1)S(1)} %broadcast_in_dim.45), channel_id=1, replica_groups={{0,2,4,6},{8,10,12,14},{16,18,20,22},{24,26,28,30},{32,34,36,38},{40,42..., dimensions={0} | all-to-all | bytes 3670016 | tf_op jit(solution)/shard_map/all_to_all | solution.py:81
  175.2 6.3 %collective-permute-start.11 = (bf16[1792,512]{1,0:T(8,128)(2,1)S(1)}, bf16[1792,512]{1,0:T(8,128)(2,1)}, u32[]{:S(2)}, u32[]{:S(2)}) collective-permute-start(bf16[1792,512]{1,0:T(8,128)(2,1)S(1)} %bitcast.24), channel_id=1, source_target_pairs={{0,1},{1,0},{2,3},{3,2},{4,5},{5,4},{6,7},{7,6},{8,9},{9,8},{10,11... | collective-permute-start | bytes 5505032 | tf_op jit(solution)/shard_map/ppermute | solution.py:18
  181.6 2.8 %place.2 = (bf16[1536,512]{1,0:T(8,128)(2,1)}, bf16[512,512]{1,0:T(8,128)(2,1)}, bf16[1024,512]{1,0:T(8,128)(2,1)}, bf16[512,512]{1,0:T(8,128)(2,1)}) custom-call(s32[1]{0:T(128)} %bitcast.core_ref, bf16[1792,512]{1,0:T(8,128)(2,1)} %bitcast.25), custom_call_target="tpu_custom_call" | custom-call | tf_op jit(solution)/shard_map/place/pallas_call | solution.py:135
  185.1 2.8 %place.3 = (bf16[1536,512]{1,0:T(8,128)(2,1)}, bf16[512,512]{1,0:T(8,128)(2,1)}, bf16[1024,512]{1,0:T(8,128)(2,1)}, bf16[512,512]{1,0:T(8,128)(2,1)}) custom-call(s32[1]{0:T(128)} %bitcast.8.core_ref, bf16[1792,512]{1,0:T(8,128)(2,1)} %collective-permute-done.11.half_ref, ...), custom_call_target="tpu_custom_call", output_to_operand_aliasing={{0}: (2, {}), {1}: (3, {}), {2}: (4, {}), {3}: (5, {})} | custom-call | tf_op jit(solution)/shard_map/place/pallas_call | solution.py:135
  (129 shorter events, 41.4 us)
Async XLA Ops:
  0.6 26.1 %collective-permute-start = (bf16[1280,512]{1,0:T(8,128)(2,1)}, bf16[1280,512]{1,0:T(8,128)(2,1)}, u32[]{:S(2)}, u32[]{:S(2)}) collective-permute-start(bf16[1280,512]{1,0:T(8,128)(2,1)} %param.15), channel_id=1, source_target_pairs={{0,1},{1,0},{2,3},{3,2},{4,5},{5,4},{6,7},{7,6},{8,9},{9,8},{10,11... | collective-permute-start | bytes 3932168 | tf_op jit(solution)/shard_map/ppermute | solution.py:18
  4.0 3.0 %collective-permute-start.1 = (bf16[160,512]{1,0:T(8,128)(2,1)}, bf16[160,512]{1,0:T(8,128)(2,1)S(1)}, u32[]{:S(2)}, u32[]{:S(2)}) collective-permute-start(bf16[160,512]{1,0:T(8,128)(2,1)} %param.14), channel_id=1, source_target_pairs={{0,1},{1,0},{2,3},{3,2},{4,5},{5,4},{6,7},{7,6},{8,9},{9,8},{10,11... | collective-permute-start | bytes 491528 | tf_op jit(solution)/shard_map/ppermute | solution.py:18
  4.1 19.8 %collective-permute-start.2 = (bf16[160,512]{1,0:T(8,128)(2,1)}, bf16[160,512]{1,0:T(8,128)(2,1)S(1)}, u32[]{:S(2)}, u32[]{:S(2)}) collective-permute-start(bf16[160,512]{1,0:T(8,128)(2,1)} %node_cot_ref.1), channel_id=1, source_target_pairs={{0,1},{1,0},{2,3},{3,2},{4,5},{5,4},{6,7},{7,6},{8,9},{9,8},{10,11... | collective-permute-start | bytes 491528 | tf_op jit(solution)/shard_map/ppermute | solution.py:18
  7.0 50.1 %copy-start.2 = (bf16[320,512]{1,0:T(8,128)(2,1)}, bf16[320,512]{1,0:T(8,128)(2,1)S(1)}, u32[]{:S(2)}) copy-start(bf16[320,512]{1,0:T(8,128)(2,1)S(1)} %constant_dynamic-update-slice_fusion.part_ref) | copy-start | bytes 983044
  8.4 15.4 %copy-start.33 = (bf16[160,512]{1,0:T(8,128)(2,1)S(1)}, bf16[160,512]{1,0:T(8,128)(2,1)}, u32[]{:S(2)}) copy-start(bf16[160,512]{1,0:T(8,128)(2,1)} %node_cot_ref.1) | copy-start | bytes 491524
  8.4 31.7 %all-to-all-start = ((bf16[128,4,512]{2,1,0:T(4,128)(2,1)}), bf16[128,4,512]{2,1,0:T(4,128)(2,1)}, u32[]{:S(2)}, u32[]{:S(2)}) async-start(bf16[128,4,512]{2,1,0:T(4,128)(2,1)} %reshape.68), calls=%async_computation | async-start | bytes 1048576 | tf_op jit(solution)/shard_map/all_to_all | solution.py:352
  23.9 33.2 %copy-start.3 = (s32[128,128]{1,0:T(8,128)}, s32[128,128]{1,0:T(8,128)S(1)}, u32[]{:S(2)}) copy-start(s32[128,128]{1,0:T(8,128)S(1)} %pad.7.sender_ref) | copy-start | bytes 196612
  23.9 33.2 %copy-start.4 = (s32[128,128]{1,0:T(8,128)}, s32[128,128]{1,0:T(8,128)S(1)}, u32[]{:S(2)}) copy-start(s32[128,128]{1,0:T(8,128)S(1)} %pad.8.receiver_ref) | copy-start | bytes 196612
  26.7 18.5 %copy-start.8 = (bf16[512,512]{1,0:T(8,128)(2,1)S(1)}, bf16[512,512]{1,0:T(8,128)(2,1)}, u32[]{:S(2)}) copy-start(bf16[512,512]{1,0:T(8,128)(2,1)} %w_out_ref.3) | copy-start | bytes 1572868
  26.7 18.5 %copy-start.10 = (f32[512]{0:T(512)S(1)}, f32[512]{0:T(512)}, u32[]{:S(2)}) copy-start(f32[512]{0:T(512)} %param.24) | copy-start | bytes 6148
  26.7 18.5 %copy-start.11 = (f32[512]{0:T(512)S(1)}, f32[512]{0:T(512)}, u32[]{:S(2)}) copy-start(f32[512]{0:T(512)} %param.23) | copy-start | bytes 6148
  41.3 3.9 %collective-permute-start.3 = (bf16[512,512]{1,0:T(8,128)(2,1)S(1)}, bf16[512,512]{1,0:T(8,128)(2,1)S(1)}, u32[]{:S(2)}, u32[]{:S(2)}) collective-permute-start(bf16[512,512]{1,0:T(8,128)(2,1)S(1)} %reshape.71.mine_ref), channel_id=1, source_target_pairs={{0,1},{1,0},{2,3},{3,2},{4,5},{5,4},{6,7},{7,6},{8,9},{9,8},{10,11... | collective-permute-start | bytes 1572872 | tf_op jit(solution)/shard_map/ppermute | solution.py:18
  55.0 2.1 %collective-permute-start.4 = (f32[320,512]{1,0:T(8,128)S(1)}, f32[320,512]{1,0:T(8,128)S(1)}, u32[]{:S(2)}, u32[]{:S(2)}) collective-permute-start(f32[320,512]{1,0:T(8,128)S(1)} %get-tuple-element.68.partial_ref), channel_id=1, source_target_pairs={{0,1},{1,0},{2,3},{3,2},{4,5},{5,4},{6,7},{7,6},{8,9},{9,8},{10,11... | collective-permute-start | bytes 1966088 | tf_op jit(solution)/shard_map/ppermute | solution.py:18
  63.5 2.0 %collective-permute-start.5 = (bf16[512,512]{1,0:T(8,128)(2,1)S(1)}, bf16[512,512]{1,0:T(8,128)(2,1)S(1)}, u32[]{:S(2)}, u32[]{:S(2)}) collective-permute-start(bf16[512,512]{1,0:T(8,128)(2,1)S(1)} %get-tuple-element.76), channel_id=1, source_target_pairs={{0,1},{1,0},{2,3},{3,2},{4,5},{5,4},{6,7},{7,6},{8,9},{9,8},{10,11... | collective-permute-start | bytes 1572872 | tf_op jit(solution)/shard_map/ppermute | solution.py:18
  66.6 24.4 %all-to-all-start.1 = ((bf16[128,4,512]{2,1,0:T(4,128)(2,1)}), bf16[128,4,512]{2,1,0:T(4,128)(2,1)S(1)}, u32[]{:S(2)}, u32[]{:S(2)}) async-start(bf16[128,4,512]{2,1,0:T(4,128)(2,1)} %reshape.72), calls=%async_computation.1 | async-start | bytes 1048576 | tf_op jit(solution)/shard_map/all_to_all | solution.py:444
  83.5 2.4 %collective-permute-start.6 = (bf16[448,512]{1,0:T(8,128)(2,1)}, bf16[448,512]{1,0:T(8,128)(2,1)S(1)}, u32[]{:S(2)}, u32[]{:S(2)}) collective-permute-start(bf16[448,512]{1,0:T(8,128)(2,1)} %get-tuple-element.83), channel_id=1, source_target_pairs={{0,1},{1,0},{2,3},{3,2},{4,5},{5,4},{6,7},{7,6},{8,9},{9,8},{10,11... | collective-permute-start | bytes 1376264 | tf_op jit(solution)/shard_map/ppermute | solution.py:18
  84.2 3.0 %collective-permute-start.7 = (bf16[448,512]{1,0:T(8,128)(2,1)}, bf16[448,512]{1,0:T(8,128)(2,1)S(1)}, u32[]{:S(2)}, u32[]{:S(2)}) collective-permute-start(bf16[448,512]{1,0:T(8,128)(2,1)} %get-tuple-element.84), channel_id=1, source_target_pairs={{0,1},{1,0},{2,3},{3,2},{4,5},{5,4},{6,7},{7,6},{8,9},{9,8},{10,11... | collective-permute-start | bytes 1376264 | tf_op jit(solution)/shard_map/ppermute | solution.py:18
  84.3 3.5 %collective-permute-start.8 = (bf16[448,512]{1,0:T(8,128)(2,1)}, bf16[448,512]{1,0:T(8,128)(2,1)S(1)}, u32[]{:S(2)}, u32[]{:S(2)}) collective-permute-start(bf16[448,512]{1,0:T(8,128)(2,1)} %get-tuple-element.85), channel_id=1, source_target_pairs={{0,1},{1,0},{2,3},{3,2},{4,5},{5,4},{6,7},{7,6},{8,9},{9,8},{10,11... | collective-permute-start | bytes 1376264 | tf_op jit(solution)/shard_map/ppermute | solution.py:18
  84.7 3.1 %collective-permute-start.9 = (bf16[448,512]{1,0:T(8,128)(2,1)}, bf16[448,512]{1,0:T(8,128)(2,1)}, u32[]{:S(2)}, u32[]{:S(2)}) collective-permute-start(bf16[448,512]{1,0:T(8,128)(2,1)} %get-tuple-element.86), channel_id=1, source_target_pairs={{0,1},{1,0},{2,3},{3,2},{4,5},{5,4},{6,7},{7,6},{8,9},{9,8},{10,11... | collective-permute-start | bytes 1376264 | tf_op jit(solution)/shard_map/ppermute | solution.py:18
  94.8 17.8 %all-to-all-start.2 = ((bf16[4,448,512]{2,1,0:T(8,128)(2,1)}), bf16[4,448,512]{2,1,0:T(8,128)(2,1)S(1)}, u32[]{:S(2)}, u32[]{:S(2)}) async-start(bf16[4,448,512]{2,1,0:T(8,128)(2,1)} %bitcast.26), calls=%async_computation.2 | async-start | bytes 3670016 | tf_op jit(solution)/shard_map/all_to_all | solution.py:81
  113.8 11.4 %all-to-all-start.3 = ((bf16[4,112,512]{2,1,0:T(8,128)(2,1)}), bf16[4,112,512]{2,1,0:T(8,128)(2,1)S(1)}, u32[]{:S(2)}, u32[]{:S(2)}) async-start(bf16[4,112,512]{2,1,0:T(8,128)(2,1)} %bitcast.27), calls=%async_computation.3 | async-start | bytes 917504 | tf_op jit(solution)/shard_map/all_to_all | solution.py:81
  119.3 10.4 %collective-permute-start.10 = (f32[160,512]{1,0:T(8,128)S(1)}, f32[160,512]{1,0:T(8,128)}, u32[]{:S(2)}, u32[]{:S(2)}) collective-permute-start(f32[160,512]{1,0:T(8,128)S(1)} %slice.23), channel_id=1, source_target_pairs={{0,1},{1,0},{2,3},{3,2},{4,5},{5,4},{6,7},{7,6},{8,9},{9,8},{10,11... | collective-permute-start | bytes 983048 | tf_op jit(solution)/shard_map/ppermute | solution.py:18
  126.0 11.7 %all-to-all-start.4 = ((bf16[8,14,512]{2,1,0:T(8,128)(2,1)}), bf16[8,14,512]{2,1,0:T(8,128)(2,1)S(1)}, u32[]{:S(2)}, u32[]{:S(2)}) async-start(bf16[8,14,512]{2,1,0:T(8,128)(2,1)} %reshape.75), calls=%async_computation.4 | async-start | bytes 262144 | tf_op jit(solution)/shard_map/all_to_all | solution.py:81
  175.2 9.9 %collective-permute-start.11 = (bf16[1792,512]{1,0:T(8,128)(2,1)S(1)}, bf16[1792,512]{1,0:T(8,128)(2,1)}, u32[]{:S(2)}, u32[]{:S(2)}) collective-permute-start(bf16[1792,512]{1,0:T(8,128)(2,1)S(1)} %bitcast.24), channel_id=1, source_target_pairs={{0,1},{1,0},{2,3},{3,2},{4,5},{5,4},{6,7},{7,6},{8,9},{9,8},{10,11... | collective-permute-start | bytes 5505032 | tf_op jit(solution)/shard_map/ppermute | solution.py:18
  (29 other events, 135.7 us)
